TPU v7x, 768 devices: a whole 4x8x12 slice. The times are simulated.
768 devices in a mesh: fact: 96 (over z, y), key: 8 (over x, core).
Axes of the slice: x: 4, y: 8, z: 12, core: 2. Of those that a mesh axis runs over, the one named last changes fastest.
Arguments:
- fact_features: bfloat16 [786432, 256], P(('fact', 'key')), may hold values from -6 to 6
- targets: bfloat16 [786432, 128], P(('fact', 'key')), may hold values from -6 to 6
- fact_keys: int32 [786432], P(('fact', 'key')), may hold values from 0 to 6143, as said below
- fill_counts: int32 [768, 8], P(('fact', 'key')), may hold values from 32 to 128, as said below
- dim_features: bfloat16 [6144, 1024], P(('fact', 'key')), may hold values from -6 to 6
- fact_weight: bfloat16 [256, 128], replicated, may hold values from -0.375 to 0.375
- dim_weight: bfloat16 [1024, 128], replicated, may hold values from -0.1875 to 0.1875
Outputs:
- grad_fact: float32 [256, 128], replicated
- grad_dim: float32 [1024, 128], replicated
Inputs may be any that keep to these rules, and one draw needn't show every extreme that they name: `fact_keys`: the slot at position s lies in bucket b = (s // 128) % 8, and its key g satisfies (g // 8) % 8 = b. `fill_counts`: each device has some bucket with all 128 slots live.
All inputs are finite; a program needn't handle non-finite values.
Results may differ from a plain program's by a relative error of at most 0.0013.
Values may be sent and summed in bfloat16 or wider, within the bound.
No kernel may reach another device: no remote copies, remote signals or barrier semaphores. Data moves between devices by JAX's collectives and lax.ppermute only.
A program may use at most 32 MiB of HBM per device.

v0:
```python
import jax
import jax.numpy as jnp
from jax import lax
from jax.sharding import PartitionSpec as P

ridge_weight = 4.0


def key_block_sums(residual, slot_ids, block_keys, block_count):

    def one_block(block):
        columns = block * block_keys + jnp.arange(block_keys, dtype=jnp.int32)
        one_hot = (slot_ids[:, None] == columns[None, :]).astype(jnp.bfloat16)
        return lax.dot_general(
            one_hot, residual, (((0,), (0,)), ((), ())), preferred_element_type=jnp.float32
        )

    blocks = lax.map(one_block, jnp.arange(block_count, dtype=jnp.int32))
    return blocks.reshape(block_count * block_keys, residual.shape[1])


def on_device(
    fact_features, targets, fact_keys, fill_counts, dim_features, fact_weight, dim_weight
):
    key_devices = lax.axis_size("key")
    fact_devices = lax.axis_size("fact")
    slot_count = fact_keys.shape[0]
    bucket_rows = slot_count // key_devices
    own_keys = dim_features.shape[0]
    out_width = fact_weight.shape[1]
    own_values = jnp.dot(dim_features, dim_weight, preferred_element_type=jnp.float32).astype(
        jnp.bfloat16
    )
    partial_value = jnp.dot(
        fact_features, fact_weight, preferred_element_type=jnp.float32
    ) - targets.astype(jnp.float32)
    slot_index = jnp.arange(slot_count, dtype=jnp.int32)
    limits = jnp.repeat(fill_counts[0], bucket_rows, total_repeat_length=slot_count)
    live_slots = slot_index % bucket_rows < limits
    key_table = lax.all_gather(own_values, "fact", axis=0, tiled=True)
    local_ids = fact_keys // (own_keys * key_devices) * own_keys + fact_keys % own_keys
    blocks = local_ids.reshape(key_devices, bucket_rows // 128, 128)
    received = lax.all_to_all(blocks, "key", split_axis=0, concat_axis=0, tiled=True)
    picked = jnp.take(key_table, received, axis=0)
    returned = lax.all_to_all(picked, "key", split_axis=0, concat_axis=0, tiled=True)
    found_values = returned
    arrived_ids = received
    found_values = found_values.reshape(slot_count, out_width)
    arrived_ids = arrived_ids.reshape(slot_count)
    residual = jnp.where(
        live_slots[:, None], partial_value + found_values.astype(jnp.float32), jnp.float32(0.0)
    ).astype(jnp.bfloat16)
    fact_term = lax.dot_general(
        fact_features, residual, (((0,), (0,)), ((), ())), preferred_element_type=jnp.float32
    )
    arrived = lax.all_to_all(
        residual.reshape(key_devices, bucket_rows, out_width),
        "key",
        split_axis=0,
        concat_axis=0,
        tiled=True,
    )
    key_totals = key_block_sums(
        arrived.reshape(slot_count, out_width), arrived_ids, key_table.shape[0], 1
    )
    own_sums = lax.psum_scatter(key_totals, "fact", scatter_dimension=0, tiled=True)
    dim_term = lax.dot_general(
        dim_features.astype(jnp.float32),
        own_sums,
        (((0,), (0,)), ((), ())),
        precision=lax.Precision.HIGHEST,
    )
    fact_total, dim_total = lax.psum((fact_term, dim_term), ("fact", "key"))
    total_rows = slot_count * fact_devices * key_devices
    row_scale = float(total_rows) ** (-0.5)
    grad_fact = fact_total * row_scale + ridge_weight * fact_weight.astype(jnp.float32)
    grad_dim = dim_total * row_scale + ridge_weight * dim_weight.astype(jnp.float32)
    return (grad_fact, grad_dim)


def solution(mesh):
    placed = (
        P(("fact", "key"), None),
        P(("fact", "key"), None),
        P(("fact", "key")),
        P(("fact", "key"), None),
        P(("fact", "key"), None),
        P(),
        P(),
    )
    return jax.shard_map(
        on_device, mesh=mesh, in_specs=placed, out_specs=(P(), P()), check_vma=False
    )
```

profile of v0, /device:TPU:1, one launch (start us, length us, event | category | flops | bytes accessed | tf_op | source)
XLA Modules:
  0.0 838.9 jit_solution(734869344375833675)
XLA Ops:
  7.2 1.3 fusion.8
  8.5 13.7 %all-to-all-start = ((s32[8,1,128]{2,1,0:T(1,128)}), s32[8,1,128]{2,1,0:T(1,128)S(1)}, u32[]{:S(2)}, u32[]{:S(2)}) async-start(s32[8,1,128]{2,1,0:T(1,128)} %bitcast.13), calls=%async_computation | async-start | bytes 8192 | tf_op jit(solution)/shard_map/all_to_all | solution.py:43
  22.3 1.6 fusion.18
  23.9 1.1 convolution_convert_fusion
  25.0 4.4 compare_select_fusion.1
  29.4 58.7 %all_gather.3 = bf16[768,128]{1,0:T(8,128)(2,1)S(1)} all-gather(bf16[8,128]{1,0:T(8,128)(2,1)S(1)} %convolution_convert_fusion), channel_id=1, replica_groups=mesh['fact'=96,'key'=8] {'fact'}, dimensions={0}, use_global_device_ids=true | all-gather | bytes 198656 | tf_op jit(solution)/shard_map/all_gather | solution.py:40
  88.1 3.2 gather_fusion
  91.3 0.9 broadcast_select_fusion
  92.2 23.6 %all-to-all-start.1 = ((bf16[8,1,128,128]{3,2,1,0:T(8,128)(2,1)}), bf16[8,1,128,128]{3,2,1,0:T(8,128)(2,1)S(1)}, u32[]{:S(2)}, u32[]{:S(2)}) async-start(bf16[8,1,128,128]{3,2,1,0:T(8,128)(2,1)} %broadcast_select_fusion), calls=%async_computation.1 | async-start | bytes 524288 | tf_op jit(solution)/shard_map/all_to_all | solution.py:45
  115.9 0.6 fusion.5
  116.5 5.8 all-to-all-done.1
  122.3 0.3 fusion.4
  122.7 9.9 %all_to_all.15 = bf16[8,128,128]{2,1,0:T(8,128)(2,1)S(1)} all-to-all(bf16[8,128,128]{2,1,0:T(8,128)(2,1)S(1)} %bitcast.48), channel_id=1, replica_groups=mesh['fact'=96,'key'=8] {'key'}, dimensions={0} | all-to-all | bytes 524288 | tf_op jit(solution)/shard_map/all_to_all | solution.py:56
  132.6 1.9 fusion
  134.6 1.3 dynamic-slice.6
  136.5 0.9 convolution_bitcast_fusion.1
  137.5 209.6 %all-reduce.5.cloned.1.call-done = f32[768,128]{1,0:T(8,128)} async-done(((f32[768,128]{1,0:T(8,128)}), f32[768,128]{1,0:T(8,128)}) %all-reduce.5.cloned.1.call-update) | async-done | bytes 393232
  347.0 1.9 convolution_bitcast_fusion
  349.1 0.8 copy-done.1
  349.9 0.1 copy.23
  350.0 479.2 %all-reduce.7.cloned.1.call-done = (f32[256,128]{0,1:T(8,128)}, f32[1024,128]{0,1:T(8,128)}) async-done(((f32[256,128]{0,1:T(8,128)}, f32[1024,128]{0,1:T(8,128)}), (f32[256,128]{0,1:T(8,128)}, f32[1024,128]{0,1:T(8,128)})) %all-reduce.7.cloned.1.call-update) | async-done | bytes 655376 | tf_op jit(solution)/shard_map/psum | solution.py:73
  829.3 1.0 multiply_add_fusion.1
  830.3 0.8 copy.24
  831.1 1.0 copy.25
  (23 shorter events, 0.3 us)
Async XLA Ops:
  7.2 115.2 %copy-start = (bf16[1024,256]{1,0:T(8,128)(2,1)S(1)}, bf16[1024,256]{1,0:T(8,128)(2,1)}, u32[]{:S(2)}) copy-start(bf16[1024,256]{1,0:T(8,128)(2,1)} %param.9) | copy-start | bytes 1572868
  8.5 79.5 %all-to-all-start = ((s32[8,1,128]{2,1,0:T(1,128)}), s32[8,1,128]{2,1,0:T(1,128)S(1)}, u32[]{:S(2)}, u32[]{:S(2)}) async-start(s32[8,1,128]{2,1,0:T(1,128)} %bitcast.13), calls=%async_computation | async-start | bytes 8192 | tf_op jit(solution)/shard_map/all_to_all | solution.py:43
  91.3 31.1 %copy-start.3 = (bf16[256,128]{1,0:T(8,128)(2,1)S(1)}, bf16[256,128]{1,0:T(8,128)(2,1)}, u32[]{:S(2)}) copy-start(bf16[256,128]{1,0:T(8,128)(2,1)} %param.14) | copy-start | bytes 196612
  91.3 31.1 %copy-start.4 = (bf16[1024,128]{1,0:T(8,128)(2,1)S(1)}, bf16[1024,128]{1,0:T(8,128)(2,1)}, u32[]{:S(2)}) copy-start(bf16[1024,128]{1,0:T(8,128)(2,1)} %param.10) | copy-start | bytes 786436
  92.2 30.1 %all-to-all-start.1 = ((bf16[8,1,128,128]{3,2,1,0:T(8,128)(2,1)}), bf16[8,1,128,128]{3,2,1,0:T(8,128)(2,1)S(1)}, u32[]{:S(2)}, u32[]{:S(2)}) async-start(bf16[8,1,128,128]{3,2,1,0:T(8,128)(2,1)} %broadcast_select_fusion), calls=%async_computation.1 | async-start | bytes 524288 | tf_op jit(solution)/shard_map/all_to_all | solution.py:45
  115.8 231.2 %all-reduce.5.cloned.1.call-start = ((), (), s32[]{:S(2)}) async-start(), calls=%async_computation.3 | async-start | bytes 786432
  134.5 212.5 %copy-start.5 = (bf16[8,1024]{1,0:T(8,128)(2,1)S(1)}, bf16[8,1024]{1,0:T(8,128)(2,1)}, u32[]{:S(2)}) copy-start(bf16[8,1024]{1,0:T(8,128)(2,1)} %param.13) | copy-start | bytes 49156
  134.5 694.7 %all-reduce.7.cloned.1.call-start = ((), (), s32[]{:S(2)}) async-start(), calls=%async_computation.4 | async-start | bytes 1310720 | tf_op jit(solution)/shard_map/psum | solution.py:73
  348.9 0.9 copy-start.1
  829.3 1.7 copy-start.2
Sparse Core Ops, SparseCore 0:
  134.7 212.3 all-reduce.4
  353.4 475.8 all-reduce.6
where the time goes:
time: 840 us; the launch traced here: 839 us
  waiting for transfers between devices  695 us (83%)
  blocking collectives  68.6 us (8%)
  starting transfers between devices  37.4 us (4%)
  between operations  14.8 us (2%)
  local copies, waits for them, and re-layouts  8.94 us (1%)
    psum x1, waiting for transfers between devices, on_device(): fact_total, dim_total = lax.psum((fact_term, dim_term), ('fact', 'key'))  479 us
    unnamed x3, waiting for transfers between devices  210 us
    all_gather x1, blocking collectives, on_device(): key_table = lax.all_gather(own_values, 'fact', axis=0, tiled=True)  58.7 us
    all_to_all x1, starting transfers between devices, on_device(): lax.all_to_all(picked, 'key', split_axis=0, concat_axis=0, tiled=True)  23.6 us
  transfers between devices with their start and end apart: 4, of which 3 were waited for; matrix products, arithmetic and copies ran while one was open for 1% of the time, Pallas kernels for 0%

commit v1 on v0

v1 whole, which is shorter than its diff:
```python
import jax
import jax.numpy as jnp
from jax import lax
from jax.sharding import PartitionSpec as P

ridge_weight = 4.0
ring_size = 8


def fact_groups(fact_devices):
    rings = fact_devices // ring_size
    inner = [[ring * ring_size + i for i in range(ring_size)] for ring in range(rings)]
    outer = [[ring * ring_size + i for ring in range(rings)] for i in range(ring_size)]
    return inner, outer


def spread(array, axis, groups=None):
    return lax.all_to_all(
        array, axis, split_axis=0, concat_axis=0, tiled=True, axis_index_groups=groups
    )


def collect(array, axis, copies, groups):
    return spread(jnp.broadcast_to(array[None], (copies, *array.shape)), axis, groups)


def total_over_devices(terms, inner, outer):
    width = terms.shape[1]
    key_devices = lax.axis_size("key")
    part = spread(terms.reshape(key_devices, -1, width), "key").sum(axis=0)
    part = spread(part.reshape(ring_size, -1, width), "fact", inner).sum(axis=0)
    part = collect(part, "fact", len(inner), outer).sum(axis=0)
    part = collect(part, "fact", ring_size, inner).reshape(-1, width)
    return lax.all_gather(part, "key", axis=0, tiled=True)


def on_device(
    fact_features, targets, fact_keys, fill_counts, dim_features, fact_weight, dim_weight
):
    key_devices = lax.axis_size("key")
    fact_devices = lax.axis_size("fact")
    inner, outer = fact_groups(fact_devices)
    slot_count = fact_keys.shape[0]
    bucket_rows = slot_count // key_devices
    own_keys = dim_features.shape[0]
    fact_width = fact_features.shape[1]
    out_width = fact_weight.shape[1]
    bucket_keys = fact_devices * own_keys
    f32, bf16 = jnp.float32, jnp.bfloat16

    rings = len(inner)
    ring_keys = rings * own_keys

    slot = lax.broadcasted_iota(jnp.int32, (key_devices, bucket_rows), 1)
    owner = fact_keys // (own_keys * key_devices)
    places = (owner % ring_size) * ring_keys + (owner // ring_size) * own_keys + fact_keys % own_keys
    codes = jnp.where(slot < fill_counts[0][:, None], places.reshape(key_devices, bucket_rows), -1)
    codes = spread(codes, "key").reshape(slot_count)
    features = spread(fact_features.reshape(key_devices, bucket_rows, fact_width), "key")
    features = features.reshape(slot_count, fact_width)
    goals = spread(targets.reshape(key_devices, bucket_rows, out_width), "key")
    goals = goals.reshape(slot_count, out_width)

    rows = collect(dim_features, "fact", rings, outer).reshape(ring_keys, -1)
    values = jnp.dot(rows, dim_weight, preferred_element_type=f32).astype(bf16)
    values = collect(values, "fact", ring_size, inner).reshape(bucket_keys, out_width)

    one_hot = (codes[:, None] == jnp.arange(bucket_keys, dtype=jnp.int32)[None, :]).astype(bf16)
    found = jnp.dot(one_hot, values, preferred_element_type=f32)
    partial_value = jnp.dot(features, fact_weight, preferred_element_type=f32) - goals.astype(f32)
    residual = jnp.where(codes[:, None] >= 0, partial_value + found, f32(0.0)).astype(bf16)

    contract = (((0,), (0,)), ((), ()))
    fact_term = lax.dot_general(features, residual, contract, preferred_element_type=f32)
    key_sums = lax.dot_general(one_hot, residual, contract, preferred_element_type=f32)
    key_sums = spread(key_sums.reshape(ring_size, ring_keys, out_width), "fact", inner).sum(axis=0)
    high = key_sums.astype(bf16)
    low = (key_sums - high.astype(f32)).astype(bf16)
    dim_term = lax.dot_general(rows, high, contract, preferred_element_type=f32)
    dim_term = dim_term + lax.dot_general(rows, low, contract, preferred_element_type=f32)

    totals = total_over_devices(jnp.concatenate([fact_term, dim_term], axis=0), inner, outer)
    total_rows = slot_count * fact_devices * key_devices
    row_scale = float(total_rows) ** (-0.5)
    grad_fact = totals[:fact_width] * row_scale + ridge_weight * fact_weight.astype(f32)
    grad_dim = totals[fact_width:] * row_scale + ridge_weight * dim_weight.astype(f32)
    return (grad_fact, grad_dim)


def solution(mesh):
    placed = (
        P(("fact", "key"), None),
        P(("fact", "key"), None),
        P(("fact", "key")),
        P(("fact", "key"), None),
        P(("fact", "key"), None),
        P(),
        P(),
    )
    return jax.shard_map(
        on_device, mesh=mesh, in_specs=placed, out_specs=(P(), P()), check_vma=False
    )
```

time: 840 us -> 172 us (0.20)
  waiting for transfers between devices: 695 us -> 28.7 us
  blocking collectives: 68.6 us -> 116 us
  starting transfers between devices: 37.4 us -> 16.6 us
  between operations: 14.8 us -> 0.76 us
    psum x1 -> x0, waiting for transfers between devices: 479 us -> none  [on_device(): fact_total, dim_total = lax.psum((fact_term, dim_term), ('fact', 'key'))]
    unnamed x3 -> x0, waiting for transfers between devices: 210 us -> none
    all_to_all x1 -> x7, blocking collectives: 9.95 us -> 98.4 us  [spread(): lax.all_to_all(array, axis, split_axis=0, concat_axis=0, tiled=True, axis...]
    all_gather x1, blocking collectives: 58.7 us -> 17.8 us  [total_over_devices(): return lax.all_gather(part, 'key', axis=0, tiled=True)]
    all_to_all x2 -> x3, waiting for transfers between devices: 5.83 us -> 28.7 us  [spread(): lax.all_to_all(array, axis, split_axis=0, concat_axis=0, tiled=True, axis...]
    all_to_all x2 -> x3, starting transfers between devices: 37.4 us -> 16.6 us  [spread(): lax.all_to_all(array, axis, split_axis=0, concat_axis=0, tiled=True, axis...]
  transfers between devices with their start and end apart: 4 -> 3, of which waited for: 3 -> 3; matrix products, arithmetic and copies ran while one was open for 1% -> 0% of each run, Pallas kernels for 0% -> 0%
where the time goes in v1:
time: 172 us; the launch traced here: 171 us
  blocking collectives  116 us (67%)
  waiting for transfers between devices  28.7 us (17%)
  starting transfers between devices  16.6 us (10%)
  matrix products  4.48 us (3%)
  other arithmetic  3.13 us (2%)
    all_to_all x7, blocking collectives, spread(): lax.all_to_all(array, axis, split_axis=0, concat_axis=0, tiled=True, axis...  98.4 us
    all_to_all x3, waiting for transfers between devices, spread(): lax.all_to_all(array, axis, split_axis=0, concat_axis=0, tiled=True, axis...  28.7 us
    all_gather x1, blocking collectives, total_over_devices(): return lax.all_gather(part, 'key', axis=0, tiled=True)  17.8 us
    all_to_all x3, starting transfers between devices, spread(): lax.all_to_all(array, axis, split_axis=0, concat_axis=0, tiled=True, axis...  16.6 us
  transfers between devices with their start and end apart: 3, of which 3 were waited for; matrix products, arithmetic and copies ran while one was open for 0% of the time, Pallas kernels for 0%

profile of v1, /device:TPU:1, one launch (start us, length us, event | category | flops | bytes accessed | tf_op | source)
XLA Modules:
  0.0 171.5 jit_solution(12474913900459502331)
XLA Ops:
  0.6 0.7 fusion.19
  1.3 0.7 compare_select_fusion
  2.1 17.4 %all_to_all.51 = s32[8,1,128]{2,1,0:T(1,128)S(1)} all-to-all(s32[8,1,128]{2,1,0:T(1,128)S(1)} %compare_select_fusion), channel_id=1, replica_groups=mesh['fact'=96,'key'=8] {'key'}, dimensions={0} | all-to-all | bytes 8192 | tf_op jit(solution)/shard_map/all_to_all | solution.py:18
  19.5 10.5 %all_to_all.52 = bf16[8,128,128]{2,1,0:T(8,128)(2,1)S(1)} all-to-all(bf16[8,128,128]{2,1,0:T(8,128)(2,1)} %bitcast.33), channel_id=1, replica_groups=mesh['fact'=96,'key'=8] {'key'}, dimensions={0} | all-to-all | bytes 524288 | tf_op jit(solution)/shard_map/all_to_all | solution.py:18
  30.0 0.7 broadcast_in_dim.26
  30.8 19.6 %all_to_all.53 = bf16[12,8,1024]{2,1,0:T(8,128)(2,1)S(1)} all-to-all(bf16[12,8,1024]{2,1,0:T(8,128)(2,1)S(1)} %broadcast_in_dim.26), channel_id=1, replica_groups={{0,64,128,192,256,320,384,448,512,576,640,704},{8,72,136,200,264,328,39..., dimensions={0} | all-to-all | bytes 393216 | tf_op jit(solution)/shard_map/all_to_all | solution.py:18
  50.3 6.3 %all-to-all-start.1 = ((bf16[8,128,256]{2,1,0:T(8,128)(2,1)}), bf16[8,128,256]{2,1,0:T(8,128)(2,1)S(1)}, u32[]{:S(2)}, u32[]{:S(2)}) async-start(bf16[8,128,256]{2,1,0:T(8,128)(2,1)} %bitcast.3), calls=%async_computation.1 | async-start | bytes 1048576 | tf_op jit(solution)/shard_map/all_to_all | solution.py:18
  56.8 9.3 %all-to-all-done.1 = bf16[8,128,256]{2,1,0:T(8,128)(2,1)S(1)} async-done(((bf16[8,128,256]{2,1,0:T(8,128)(2,1)}), bf16[8,128,256]{2,1,0:T(8,128)(2,1)S(1)}, u32[]{:S(2)}, u32[]{:S(2)}) %all-to-all-start.1) | async-done | bytes 524320 | tf_op jit(solution)/shard_map/all_to_all | solution.py:18
  66.1 0.7 broadcast_in_dim.44
  66.8 6.8 %all-to-all-start.4 = ((bf16[8,96,128]{2,1,0:T(8,128)(2,1)}), bf16[8,96,128]{2,1,0:T(8,128)(2,1)S(1)}, u32[]{:S(2)}, u32[]{:S(2)}) async-start(bf16[8,96,128]{2,1,0:T(8,128)(2,1)} %broadcast_in_dim.44), calls=%async_computation.4 | async-start | bytes 393216 | tf_op jit(solution)/shard_map/all_to_all | solution.py:18
  73.6 0.3 convolution_subtract_fusion
  73.9 8.3 %all-to-all-done.4 = bf16[8,96,128]{2,1,0:T(8,128)(2,1)S(1)} async-done(((bf16[8,96,128]{2,1,0:T(8,128)(2,1)}), bf16[8,96,128]{2,1,0:T(8,128)(2,1)S(1)}, u32[]{:S(2)}, u32[]{:S(2)}) %all-to-all-start.4) | async-done | bytes 196640 | tf_op jit(solution)/shard_map/all_to_all | solution.py:18
  82.2 1.3 fusion.7
  83.6 1.9 %fusion = f32[768,128]{1,0:T(8,128)} fusion(bf16[1024,128]{1,0:T(8,128)(2,1)S(1)} %fusion.7, s32[1024]{0:T(1024)S(1)} %bitcast.37), kind=kOutput, calls=%fused_computation.1 | convolution fusion | flops 202113024 | bytes 659456 | tf_op jit(solution)/shard_map/dot_general | solution.py:75
  85.5 3.5 %all-to-all-start.5 = ((f32[8,96,128]{2,1,0:T(8,128)}), f32[8,96,128]{2,1,0:T(8,128)S(1)}, u32[]{:S(2)}, u32[]{:S(2)}) async-start(f32[8,96,128]{2,1,0:T(8,128)} %bitcast.10), calls=%async_computation.5 | async-start | bytes 786432 | tf_op jit(solution)/shard_map/all_to_all | solution.py:18
  89.0 0.3 convolution_bitcast_fusion
  89.2 11.1 %all-to-all-done.5 = f32[8,96,128]{2,1,0:T(8,128)S(1)} async-done(((f32[8,96,128]{2,1,0:T(8,128)}), f32[8,96,128]{2,1,0:T(8,128)S(1)}, u32[]{:S(2)}, u32[]{:S(2)}) %all-to-all-start.5) | async-done | bytes 393248 | tf_op jit(solution)/shard_map/all_to_all | solution.py:18
  101.2 17.5 %all_to_all.54 = f32[8,160,128]{2,1,0:T(8,128)S(1)} all-to-all(f32[8,160,128]{2,1,0:T(8,128)S(1)} %bitcast.31), channel_id=1, replica_groups=mesh['fact'=96,'key'=8] {'key'}, dimensions={0} | all-to-all | bytes 1310720 | tf_op jit(solution)/shard_map/all_to_all | solution.py:18
  118.7 9.8 %all_to_all.55 = f32[8,20,128]{2,1,0:T(8,128)S(1)} all-to-all(f32[8,20,128]{2,1,0:T(8,128)S(1)} %reshape.107), channel_id=1, replica_groups={{0,8,16,24,32,40,48,56},{64,72,80,88,96,104,112,120},{128,136,144,152,1..., dimensions={0} | all-to-all | bytes 163840 | tf_op jit(solution)/shard_map/all_to_all | solution.py:18
  128.6 13.6 %all_to_all.56 = f32[12,20,128]{2,1,0:T(8,128)S(1)} all-to-all(f32[12,20,128]{2,1,0:T(8,128)S(1)} %broadcast_in_dim.46), channel_id=1, replica_groups={{0,64,128,192,256,320,384,448,512,576,640,704},{8,72,136,200,264,328,39..., dimensions={0} | all-to-all | bytes 245760 | tf_op jit(solution)/shard_map/all_to_all | solution.py:18
  142.2 10.0 %all_to_all.57 = f32[8,20,128]{2,1,0:T(8,128)S(1)} all-to-all(f32[8,20,128]{2,1,0:T(8,128)S(1)} %broadcast_in_dim.47), channel_id=1, replica_groups={{0,8,16,24,32,40,48,56},{64,72,80,88,96,104,112,120},{128,136,144,152,1..., dimensions={0} | all-to-all | bytes 163840 | tf_op jit(solution)/shard_map/all_to_all | solution.py:18
  152.2 17.8 %all_gather.3 = f32[1280,128]{1,0:T(8,128)S(1)} all-gather(f32[160,128]{1,0:T(8,128)S(1)} %reshape.108), channel_id=1, replica_groups=mesh['fact'=96,'key'=8] {'key'}, dimensions={0}, use_global_device_ids=true | all-gather | bytes 737280 | tf_op jit(solution)/shard_map/all_gather | solution.py:34
  169.9 0.7 fusion.13
  170.6 0.9 fusion.8
  (18 shorter events, 1.1 us)
Async XLA Ops:
  30.7 25.9 %copy-start = (bf16[1024,128]{1,0:T(8,128)(2,1)S(1)}, bf16[1024,128]{1,0:T(8,128)(2,1)}, u32[]{:S(2)}) copy-start(bf16[1024,128]{1,0:T(8,128)(2,1)} %param.13) | copy-start | bytes 786436
  50.3 15.8 %all-to-all-start.1 = ((bf16[8,128,256]{2,1,0:T(8,128)(2,1)}), bf16[8,128,256]{2,1,0:T(8,128)(2,1)S(1)}, u32[]{:S(2)}, u32[]{:S(2)}) async-start(bf16[8,128,256]{2,1,0:T(8,128)(2,1)} %bitcast.3), calls=%async_computation.1 | async-start | bytes 1048576 | tf_op jit(solution)/shard_map/all_to_all | solution.py:18
  56.6 17.0 %copy-start.1 = (bf16[256,128]{1,0:T(8,128)(2,1)S(1)}, bf16[256,128]{1,0:T(8,128)(2,1)}, u32[]{:S(2)}) copy-start(bf16[256,128]{1,0:T(8,128)(2,1)} %param.12) | copy-start | bytes 196612
  66.8 15.4 %all-to-all-start.4 = ((bf16[8,96,128]{2,1,0:T(8,128)(2,1)}), bf16[8,96,128]{2,1,0:T(8,128)(2,1)S(1)}, u32[]{:S(2)}, u32[]{:S(2)}) async-start(bf16[8,96,128]{2,1,0:T(8,128)(2,1)} %broadcast_in_dim.44), calls=%async_computation.4 | async-start | bytes 393216 | tf_op jit(solution)/shard_map/all_to_all | solution.py:18
  85.5 14.8 %all-to-all-start.5 = ((f32[8,96,128]{2,1,0:T(8,128)}), f32[8,96,128]{2,1,0:T(8,128)S(1)}, u32[]{:S(2)}, u32[]{:S(2)}) async-start(f32[8,96,128]{2,1,0:T(8,128)} %bitcast.10), calls=%async_computation.5 | async-start | bytes 786432 | tf_op jit(solution)/shard_map/all_to_all | solution.py:18

commit v2 on v1

--- a/solution.py
+++ b/solution.py
@@ -5,6 +5,8 @@
 
 ridge_weight = 4.0
 ring_size = 8
+digit = 64
+code_rows = 8
 
 
 def fact_groups(fact_devices):
@@ -54,14 +56,19 @@
     slot = lax.broadcasted_iota(jnp.int32, (key_devices, bucket_rows), 1)
     owner = fact_keys // (own_keys * key_devices)
     places = (owner % ring_size) * ring_keys + (owner // ring_size) * own_keys + fact_keys % own_keys
-    codes = jnp.where(slot < fill_counts[0][:, None], places.reshape(key_devices, bucket_rows), -1)
-    codes = spread(codes, "key").reshape(slot_count)
-    features = spread(fact_features.reshape(key_devices, bucket_rows, fact_width), "key")
-    features = features.reshape(slot_count, fact_width)
-    goals = spread(targets.reshape(key_devices, bucket_rows, out_width), "key")
-    goals = goals.reshape(slot_count, out_width)
+    codes = jnp.where(slot < fill_counts[0][:, None], places.reshape(key_devices, bucket_rows), -digit)
+    digits = jnp.concatenate([codes // digit, codes % digit, jnp.zeros_like(codes)], axis=1)
+    digits = jnp.pad(digits.astype(bf16)[:, None, :], ((0, 0), (0, code_rows - 1), (0, 0)))
+    packed = jnp.concatenate([fact_features, targets], axis=1)
+    packed = packed.reshape(key_devices, bucket_rows, fact_width + out_width)
+    packed = spread(jnp.concatenate([packed, digits], axis=1), "key")
+    slots = packed[:, :bucket_rows].reshape(slot_count, fact_width + out_width)
+    features, goals = slots[:, :fact_width], slots[:, fact_width:]
+    digits = packed[:, bucket_rows].astype(jnp.int32)
+    codes = digits[:, :bucket_rows] * digit + digits[:, bucket_rows : 2 * bucket_rows]
+    codes = codes.reshape(slot_count)
 
-    rows = collect(dim_features, "fact", rings, outer).reshape(ring_keys, -1)
+    rows = lax.all_gather(dim_features, "fact", axis=0, tiled=True, axis_index_groups=outer)
     values = jnp.dot(rows, dim_weight, preferred_element_type=f32).astype(bf16)
     values = collect(values, "fact", ring_size, inner).reshape(bucket_keys, out_width)
 

time: 172 us -> 149 us (0.87)
  blocking collectives: 116 us -> 94.1 us
  waiting for transfers between devices: 28.7 us -> 18 us
  starting transfers between devices: 16.6 us -> 24.4 us
    all_to_all x7 -> x4, blocking collectives: 98.4 us -> 56 us  [spread(): lax.all_to_all(array, axis, split_axis=0, concat_axis=0, tiled=True, axis...]
    all_gather x0 -> x1, blocking collectives: none -> 20.4 us  [on_device(): lax.all_gather(dim_features, 'fact', axis=0, tiled=True, axis_index_group...]
    all_to_all x3, waiting for transfers between devices: 28.7 us -> 18 us  [spread(): lax.all_to_all(array, axis, split_axis=0, concat_axis=0, tiled=True, axis...]
    all_to_all x3, starting transfers between devices: 16.6 us -> 24.4 us  [spread(): lax.all_to_all(array, axis, split_axis=0, concat_axis=0, tiled=True, axis...]
    concatenate x0 -> x4, other arithmetic: none -> 2.98 us  [the longest x1 1.21 us: on_device(): packed = jnp.concatenate([fact_features, targets], axis=1)]
  transfers between devices with their start and end apart: 3 -> 3, of which waited for: 3 -> 2; matrix products, arithmetic and copies ran while one was open for 0% -> 1% of each run, Pallas kernels for 0% -> 0%
where the time goes in v2:
time: 149 us; the launch traced here: 148 us
  blocking collectives  94.1 us (63%)
  starting transfers between devices  24.4 us (16%)
  waiting for transfers between devices  18 us (12%)
  other arithmetic  4.69 us (3%)
  matrix products  4.5 us (3%)
  local copies, waits for them, and re-layouts  1.78 us (1%)
    all_to_all x4, blocking collectives, spread(): lax.all_to_all(array, axis, split_axis=0, concat_axis=0, tiled=True, axis...  56 us
    all_to_all x3, starting transfers between devices, spread(): lax.all_to_all(array, axis, split_axis=0, concat_axis=0, tiled=True, axis...  24.4 us
    all_gather x1, blocking collectives, on_device(): lax.all_gather(dim_features, 'fact', axis=0, tiled=True, axis_index_group...  20.4 us
    all_to_all x3, waiting for transfers between devices, spread(): lax.all_to_all(array, axis, split_axis=0, concat_axis=0, tiled=True, axis...  18 us
    all_gather x1, blocking collectives, total_over_devices(): return lax.all_gather(part, 'key', axis=0, tiled=True)  17.8 us
  transfers between devices with their start and end apart: 3, of which 2 were waited for; matrix products, arithmetic and copies ran while one was open for 1% of the time, Pallas kernels for 0%

profile of v2, /device:TPU:1, one launch (start us, length us, event | category | flops | bytes accessed | tf_op | source)
XLA Modules:
  0.0 148.2 jit_solution(206946360254944916)
XLA Ops:
  0.6 0.8 fusion.37
  1.5 1.2 pad_maximum_fusion
  2.7 1.0 fusion.9
  3.7 14.1 %all-to-all-start = ((bf16[8,136,384]{2,1,0:T(8,128)(2,1)}), bf16[8,136,384]{2,1,0:T(8,128)(2,1)S(1)}, u32[]{:S(2)}, u32[]{:S(2)}) async-start(bf16[8,136,384]{2,1,0:T(8,128)(2,1)} %fusion.9), calls=%async_computation | async-start | bytes 1671168 | tf_op jit(solution)/shard_map/all_to_all | solution.py:20
  17.8 20.4 %all_gather.6 = bf16[96,1024]{1,0:T(8,128)(2,1)S(1)} all-gather(bf16[8,1024]{1,0:T(8,128)(2,1)S(1)} %copy-done.2), channel_id=1, replica_groups={{0,64,128,192,256,320,384,448,512,576,640,704},{8,72,136,200,264,328,39..., dimensions={0}, use_global_device_ids=true | all-gather | bytes 212992 | tf_op jit(solution)/shard_map/all_gather | solution.py:71
  38.4 0.7 broadcast_in_dim.24
  39.1 6.8 %all-to-all-start.1 = ((bf16[8,96,128]{2,1,0:T(8,128)(2,1)}), bf16[8,96,128]{2,1,0:T(8,128)(2,1)S(1)}, u32[]{:S(2)}, u32[]{:S(2)}) async-start(bf16[8,96,128]{2,1,0:T(8,128)(2,1)} %broadcast_in_dim.24), calls=%async_computation.1 | async-start | bytes 393216 | tf_op jit(solution)/shard_map/all_to_all | solution.py:20
  46.0 0.7 copy-done.1
  46.7 0.3 convolution_subtract_fusion
  47.0 7.5 %all-to-all-done.1 = bf16[8,96,128]{2,1,0:T(8,128)(2,1)S(1)} async-done(((bf16[8,96,128]{2,1,0:T(8,128)(2,1)}), bf16[8,96,128]{2,1,0:T(8,128)(2,1)S(1)}, u32[]{:S(2)}, u32[]{:S(2)}) %all-to-all-start.1) | async-done | bytes 196640 | tf_op jit(solution)/shard_map/all_to_all | solution.py:20
  54.5 1.3 fusion.8
  55.9 1.9 %fusion = f32[768,128]{1,0:T(8,128)} fusion(bf16[1024,128]{1,0:T(8,128)(2,1)S(1)} %fusion.8, s32[1024]{0:T(1024)S(1)} %get-tuple-element.3), kind=kOutput, calls=%fused_computation.1 | convolution fusion | flops 202113024 | bytes 659456 | tf_op jit(solution)/shard_map/dot_general | solution.py:82
  57.8 3.5 %all-to-all-start.2 = ((f32[8,96,128]{2,1,0:T(8,128)}), f32[8,96,128]{2,1,0:T(8,128)S(1)}, u32[]{:S(2)}, u32[]{:S(2)}) async-start(f32[8,96,128]{2,1,0:T(8,128)} %bitcast.8), calls=%async_computation.2 | async-start | bytes 786432 | tf_op jit(solution)/shard_map/all_to_all | solution.py:20
  61.2 0.3 fusion.11
  61.5 10.5 %all-to-all-done.2 = f32[8,96,128]{2,1,0:T(8,128)S(1)} async-done(((f32[8,96,128]{2,1,0:T(8,128)}), f32[8,96,128]{2,1,0:T(8,128)S(1)}, u32[]{:S(2)}, u32[]{:S(2)}) %all-to-all-start.2) | async-done | bytes 393248 | tf_op jit(solution)/shard_map/all_to_all | solution.py:20
  72.0 0.2 fusion.16
  72.3 0.2 fusion.7
  72.8 22.8 %all_to_all.35 = f32[8,160,128]{2,1,0:T(8,128)S(1)} all-to-all(f32[8,160,128]{2,1,0:T(8,128)S(1)} %bitcast.39), channel_id=1, replica_groups=mesh['fact'=96,'key'=8] {'key'}, dimensions={0} | all-to-all | bytes 1310720 | tf_op jit(solution)/shard_map/all_to_all | solution.py:20
  95.6 9.8 %all_to_all.36 = f32[8,20,128]{2,1,0:T(8,128)S(1)} all-to-all(f32[8,20,128]{2,1,0:T(8,128)S(1)} %reshape.128), channel_id=1, replica_groups={{0,8,16,24,32,40,48,56},{64,72,80,88,96,104,112,120},{128,136,144,152,1..., dimensions={0} | all-to-all | bytes 163840 | tf_op jit(solution)/shard_map/all_to_all | solution.py:20
  105.5 13.4 %all_to_all.37 = f32[12,20,128]{2,1,0:T(8,128)S(1)} all-to-all(f32[12,20,128]{2,1,0:T(8,128)S(1)} %broadcast_in_dim.41), channel_id=1, replica_groups={{0,64,128,192,256,320,384,448,512,576,640,704},{8,72,136,200,264,328,39..., dimensions={0} | all-to-all | bytes 245760 | tf_op jit(solution)/shard_map/all_to_all | solution.py:20
  118.9 10.0 %all_to_all.38 = f32[8,20,128]{2,1,0:T(8,128)S(1)} all-to-all(f32[8,20,128]{2,1,0:T(8,128)S(1)} %broadcast_in_dim.42), channel_id=1, replica_groups={{0,8,16,24,32,40,48,56},{64,72,80,88,96,104,112,120},{128,136,144,152,1..., dimensions={0} | all-to-all | bytes 163840 | tf_op jit(solution)/shard_map/all_to_all | solution.py:20
  128.9 17.8 %all_gather.7 = f32[1280,128]{1,0:T(8,128)S(1)} all-gather(f32[160,128]{1,0:T(8,128)S(1)} %reshape.129), channel_id=1, replica_groups=mesh['fact'=96,'key'=8] {'key'}, dimensions={0}, use_global_device_ids=true | all-gather | bytes 737280 | tf_op jit(solution)/shard_map/all_gather | solution.py:36
  146.7 0.9 fusion.10
  147.6 0.7 fusion.14
  (25 shorter events, 0.8 us)
Async XLA Ops:
  3.7 14.1 %copy-start.2 = (bf16[8,1024]{1,0:T(8,128)(2,1)S(1)}, bf16[8,1024]{1,0:T(8,128)(2,1)}, u32[]{:S(2)}) copy-start(bf16[8,1024]{1,0:T(8,128)(2,1)} %param.11) | copy-start | bytes 49156
  3.7 34.5 %copy-start = (bf16[1024,128]{1,0:T(8,128)(2,1)S(1)}, bf16[1024,128]{1,0:T(8,128)(2,1)}, u32[]{:S(2)}) copy-start(bf16[1024,128]{1,0:T(8,128)(2,1)} %param.13) | copy-start | bytes 786436
  3.7 34.7 %all-to-all-start = ((bf16[8,136,384]{2,1,0:T(8,128)(2,1)}), bf16[8,136,384]{2,1,0:T(8,128)(2,1)S(1)}, u32[]{:S(2)}, u32[]{:S(2)}) async-start(bf16[8,136,384]{2,1,0:T(8,128)(2,1)} %fusion.9), calls=%async_computation | async-start | bytes 1671168 | tf_op jit(solution)/shard_map/all_to_all | solution.py:20
  39.1 15.5 %all-to-all-start.1 = ((bf16[8,96,128]{2,1,0:T(8,128)(2,1)}), bf16[8,96,128]{2,1,0:T(8,128)(2,1)S(1)}, u32[]{:S(2)}, u32[]{:S(2)}) async-start(bf16[8,96,128]{2,1,0:T(8,128)(2,1)} %broadcast_in_dim.24), calls=%async_computation.1 | async-start | bytes 393216 | tf_op jit(solution)/shard_map/all_to_all | solution.py:20
  45.9 0.8 copy-start.1
  57.8 14.2 %all-to-all-start.2 = ((f32[8,96,128]{2,1,0:T(8,128)}), f32[8,96,128]{2,1,0:T(8,128)S(1)}, u32[]{:S(2)}, u32[]{:S(2)}) async-start(f32[8,96,128]{2,1,0:T(8,128)} %bitcast.8), calls=%async_computation.2 | async-start | bytes 786432 | tf_op jit(solution)/shard_map/all_to_all | solution.py:20

commit v3 on v1

v3 whole, which is shorter than its diff:
```python
import functools

import jax
import jax.numpy as jnp
from jax import lax
from jax.experimental import pallas as pl
from jax.experimental.pallas import tpu as pltpu
from jax.sharding import PartitionSpec as P

ridge_weight = 4.0
ring_size = 8
digit = 64
extra_rows = 8
f32, bf16, i32 = jnp.float32, jnp.bfloat16, jnp.int32


def fact_groups(fact_devices):
    rings = fact_devices // ring_size
    inner = [[ring * ring_size + i for i in range(ring_size)] for ring in range(rings)]
    outer = [[ring * ring_size + i for ring in range(rings)] for i in range(ring_size)]
    return inner, outer


def spread(array, axis, groups=None):
    return lax.all_to_all(
        array, axis, split_axis=0, concat_axis=0, tiled=True, axis_index_groups=groups
    )


def collect(array, axis, copies, groups):
    return spread(jnp.broadcast_to(array[None], (copies, *array.shape)), axis, groups)


def total_over_devices(terms, inner, outer):
    width = terms.shape[1]
    key_devices = lax.axis_size("key")
    part = spread(terms.reshape(key_devices, -1, width), "key").sum(axis=0)
    part = spread(part.reshape(ring_size, -1, width), "fact", inner).sum(axis=0)
    part = collect(part, "fact", len(inner), outer).sum(axis=0)
    part = collect(part, "fact", ring_size, inner).reshape(-1, width)
    return lax.all_gather(part, "key", axis=0, tiled=True)


def pack_slots(own_keys, ring_keys, keys_ref, fill_ref, features_ref, targets_ref, out_ref):
    buckets, bucket_rows = keys_ref.shape
    width, out_width = features_ref.shape[1], targets_ref.shape[1]
    keys = keys_ref[...]
    owner = keys // (own_keys * buckets)
    places = (owner % ring_size) * ring_keys + (owner // ring_size) * own_keys + keys % own_keys
    slot = lax.broadcasted_iota(i32, (1, bucket_rows), 1)
    for b in range(buckets):
        codes = jnp.where(slot < fill_ref[0, b], places[b : b + 1], -digit)
        high = codes // digit
        low = codes - high * digit
        rows = pl.ds(b * bucket_rows, bucket_rows)
        out_ref[b, pl.ds(0, bucket_rows), pl.ds(0, width)] = features_ref[rows, :]
        out_ref[b, pl.ds(0, bucket_rows), pl.ds(width, out_width)] = targets_ref[rows, :]
        digits = jnp.concatenate([high, low, jnp.zeros_like(high)], axis=1).astype(f32)
        digits = jnp.broadcast_to(digits, (extra_rows, width + out_width))
        out_ref[b, pl.ds(bucket_rows, extra_rows), :] = digits.astype(bf16)


def codes_of(packed_ref, b):
    bucket_rows = packed_ref.shape[1] - extra_rows
    digits = packed_ref[b, pl.ds(bucket_rows, extra_rows), :].astype(f32)
    codes = digits[:, :bucket_rows] * digit + digits[:, bucket_rows : 2 * bucket_rows]
    return codes.astype(i32)[:1]


def partial_of(packed_ref, weight_ref, b):
    bucket_rows = packed_ref.shape[1] - extra_rows
    width = weight_ref.shape[0]
    slots = packed_ref[b, pl.ds(0, bucket_rows), :]
    features = slots[:, :width]
    value = jnp.dot(features, weight_ref[...], preferred_element_type=f32)
    return features, value - slots[:, width:].astype(f32)


def sum_by_key(packed_ref, weight_ref, rows_ref, dim_weight_ref, out_ref):
    members, _, two_widths = out_ref.shape
    out_width = two_widths // 2
    ring_keys = rows_ref.shape[0]
    buckets = packed_ref.shape[0]
    bucket_rows = packed_ref.shape[1] - extra_rows
    places = lax.broadcasted_iota(i32, (members * ring_keys, bucket_rows), 0)
    ones = jnp.ones((extra_rows, bucket_rows), bf16)
    sums = jnp.zeros((members * ring_keys, out_width), f32)
    counts = jnp.zeros((extra_rows, members * ring_keys), f32)
    for b in range(buckets):
        one_hot = jnp.where(places == codes_of(packed_ref, b), f32(1.0), f32(0.0)).astype(bf16)
        _, value = partial_of(packed_ref, weight_ref, b)
        sums += jnp.dot(one_hot, value.astype(bf16), preferred_element_type=f32)
        counts += lax.dot_general(
            ones, one_hot, (((1,), (1,)), ((), ())), preferred_element_type=f32
        )
    values = jnp.dot(rows_ref[...], dim_weight_ref[...], preferred_element_type=f32).astype(bf16)
    high = jnp.floor(counts * (1.0 / digit))
    low = counts - high * digit
    rest = jnp.zeros((extra_rows, out_width - ring_keys), f32)
    for m in range(members):
        own = pl.ds(0, ring_keys)
        part = slice(m * ring_keys, (m + 1) * ring_keys)
        out_ref[m, own, pl.ds(0, out_width)] = sums[part].astype(bf16)
        out_ref[m, own, pl.ds(out_width, out_width)] = values
        digits = jnp.concatenate([high[:, part], rest, low[:, part], rest], axis=1)
        out_ref[m, pl.ds(ring_keys, extra_rows), :] = digits.astype(bf16)


def both_terms(packed_ref, weight_ref, rows_ref, met_ref, out_ref):
    members, _, two_widths = met_ref.shape
    out_width = two_widths // 2
    ring_keys = rows_ref.shape[0]
    buckets = packed_ref.shape[0]
    bucket_rows = packed_ref.shape[1] - extra_rows
    width = weight_ref.shape[0]
    contract = (((0,), (0,)), ((), ()))

    own = pl.ds(0, ring_keys)
    values = jnp.concatenate(
        [met_ref[m, own, pl.ds(out_width, out_width)] for m in range(members)], axis=0
    )
    codes = jnp.concatenate([codes_of(packed_ref, b) for b in range(buckets)], axis=0)
    codes = jnp.transpose(codes.astype(f32)).astype(i32)
    places = lax.broadcasted_iota(i32, (bucket_rows, members * ring_keys), 1)
    fact_term = jnp.zeros((width, out_width), f32)
    for b in range(buckets):
        code = codes[:, b : b + 1]
        one_hot = jnp.where(places == code, f32(1.0), f32(0.0)).astype(bf16)
        features, value = partial_of(packed_ref, weight_ref, b)
        found = jnp.dot(one_hot, values, preferred_element_type=f32)
        residual = jnp.where(code >= 0, value + found, f32(0.0)).astype(bf16)
        fact_term += lax.dot_general(features, residual, contract, preferred_element_type=f32)
    out_ref[pl.ds(0, width), :] = fact_term

    me = lax.rem(lax.axis_index("fact"), ring_size)
    sums = jnp.zeros((ring_keys, out_width), f32)
    digits = jnp.zeros((extra_rows, two_widths), f32)
    for m in range(members):
        sums += met_ref[m, own, pl.ds(0, out_width)].astype(f32)
        digits += met_ref[m, pl.ds(ring_keys, extra_rows), :].astype(f32)
    counts = digits[:1, :out_width] * digit + digits[:1, out_width:]
    diagonal = lax.broadcasted_iota(i32, (ring_keys, out_width), 0) == lax.broadcasted_iota(
        i32, (ring_keys, out_width), 1
    )
    counts = jnp.sum(jnp.where(diagonal, counts, f32(0.0)), axis=1, keepdims=True)
    sums += counts * met_ref[me, own, pl.ds(out_width, out_width)].astype(f32)
    high = sums.astype(bf16)
    low = (sums - high.astype(f32)).astype(bf16)
    dim_term = lax.dot_general(
        rows_ref[...], jnp.concatenate([high, low], axis=1), contract, preferred_element_type=f32
    )
    out_ref[pl.ds(width, rows_ref.shape[1]), :] = dim_term[:, :out_width] + dim_term[:, out_width:]


def kernel_call(body, out_shape, dtype, *operands, smem=()):
    spaces = [pltpu.SMEM if i in smem else pltpu.VMEM for i in range(len(operands))]
    return pl.pallas_call(
        body,
        out_shape=jax.ShapeDtypeStruct(out_shape, dtype),
        in_specs=[pl.BlockSpec(memory_space=space) for space in spaces],
        out_specs=pl.BlockSpec(memory_space=pltpu.VMEM),
        compiler_params=pltpu.CompilerParams(vmem_limit_bytes=32 << 20),
    )(*operands)


def on_device(
    fact_features, targets, fact_keys, fill_counts, dim_features, fact_weight, dim_weight
):
    key_devices = lax.axis_size("key")
    fact_devices = lax.axis_size("fact")
    inner, outer = fact_groups(fact_devices)
    slot_count = fact_keys.shape[0]
    bucket_rows = slot_count // key_devices
    own_keys, dim_width = dim_features.shape
    fact_width, out_width = fact_weight.shape
    ring_keys = len(inner) * own_keys

    packed = kernel_call(
        functools.partial(pack_slots, own_keys, ring_keys),
        (key_devices, bucket_rows + extra_rows, fact_width + out_width),
        bf16,
        fact_keys.reshape(key_devices, bucket_rows),
        fill_counts,
        fact_features,
        targets,
        smem=(1,),
    )
    packed = spread(packed, "key")
    rows = lax.all_gather(dim_features, "fact", axis=0, tiled=True, axis_index_groups=outer)

    met = kernel_call(
        sum_by_key,
        (ring_size, ring_keys + extra_rows, 2 * out_width),
        bf16,
        packed,
        fact_weight,
        rows,
        dim_weight,
    )
    met = spread(met, "fact", inner)
    terms = kernel_call(
        both_terms, (fact_width + dim_width, out_width), f32, packed, fact_weight, rows, met
    )

    totals = total_over_devices(terms, inner, outer)
    total_rows = slot_count * fact_devices * key_devices
    row_scale = float(total_rows) ** (-0.5)
    grad_fact = totals[:fact_width] * row_scale + ridge_weight * fact_weight.astype(f32)
    grad_dim = totals[fact_width:] * row_scale + ridge_weight * dim_weight.astype(f32)
    return (grad_fact, grad_dim)


def solution(mesh):
    placed = (
        P(("fact", "key"), None),
        P(("fact", "key"), None),
        P(("fact", "key")),
        P(("fact", "key"), None),
        P(("fact", "key"), None),
        P(),
        P(),
    )
    return jax.shard_map(
        on_device, mesh=mesh, in_specs=placed, out_specs=(P(), P()), check_vma=False
    )
```

time: 172 us -> 136 us (0.79)
  waiting for transfers between devices: 28.7 us -> 0.01 us
  blocking collectives: 116 us -> 111 us
  Pallas kernels: 0 us -> 4.98 us
  matrix products: 4.48 us -> 0 us
  starting transfers between devices: 16.6 us -> 14.1 us
    all_to_all x3 -> x1, waiting for transfers between devices: 28.7 us -> 0.01 us  [spread(): lax.all_to_all(array, axis, split_axis=0, concat_axis=0, tiled=True, axis...]
    all_to_all x7 -> x5, blocking collectives: 98.4 us -> 72.5 us  [spread(): lax.all_to_all(array, axis, split_axis=0, concat_axis=0, tiled=True, axis...]
    all_gather x0 -> x1, blocking collectives: none -> 20.6 us  [on_device(): lax.all_gather(dim_features, 'fact', axis=0, tiled=True, axis_index_group...]
    pallas_call x0 -> x3, Pallas kernels: none -> 4.98 us  [kernel_call(): pl.pallas_call(body, out_shape=jax.ShapeDtypeStruct(out_shape, dtype), in...]
    dot_general x7 -> x0, matrix products: 4.48 us -> none  [the longest x1 1.9 us: on_device(): lax.dot_general(one_hot, residual, contract, preferred_element_type=f32)]
    unnamed x4 -> x14, local copies, waits for them, and re-layouts: 0.01 us -> 3.34 us
    all_to_all x3 -> x1, starting transfers between devices: 16.6 us -> 14.1 us  [spread(): lax.all_to_all(array, axis, split_axis=0, concat_axis=0, tiled=True, axis...]
  transfers between devices with their start and end apart: 3 -> 1, of which waited for: 3 -> 0; matrix products, arithmetic and copies ran while one was open for 0% -> 0% of each run, Pallas kernels for 0% -> 0%
where the time goes in v3:
time: 136 us
  blocking collectives  111 us (82%)
  starting transfers between devices  14.1 us (10%)
  Pallas kernels  4.98 us (4%)
  local copies, waits for them, and re-layouts  3.37 us (2%)
  other arithmetic  1.62 us (1%)
    all_to_all x5, blocking collectives, spread(): lax.all_to_all(array, axis, split_axis=0, concat_axis=0, tiled=True, axis...  72.5 us
    all_gather x1, blocking collectives, on_device(): lax.all_gather(dim_features, 'fact', axis=0, tiled=True, axis_index_group...  20.6 us
    all_gather x1, blocking collectives, total_over_devices(): return lax.all_gather(part, 'key', axis=0, tiled=True)  17.8 us
    all_to_all x1, starting transfers between devices, spread(): lax.all_to_all(array, axis, split_axis=0, concat_axis=0, tiled=True, axis...  14.1 us
    pallas_call x3, Pallas kernels, kernel_call(): pl.pallas_call(body, out_shape=jax.ShapeDtypeStruct(out_shape, dtype), in...  4.98 us
    unnamed x14, local copies, waits for them, and re-layouts  3.34 us
  transfers between devices with their start and end apart: 1, of which 0 were waited for; matrix products, arithmetic and copies ran while one was open for 0% of the time, Pallas kernels for 0%

profile of v3, /device:TPU:1, one launch (start us, length us, event | category | flops | bytes accessed | tf_op | source)
XLA Modules:
  0.0 135.7 jit_solution(18014036961145589559)
XLA Ops:
  0.6 0.0 copy-start.5
  0.6 0.6 copy-done.5
  1.3 0.0 copy-start.2
  1.3 1.0 copy-done.2
  2.3 0.0 copy-start.3
  2.3 0.9 copy-done.3
  3.3 0.7 copy-done.4
  4.0 1.5 %shard_map.86 = bf16[8,136,384]{2,1,0:T(8,128)(2,1)} custom-call(s32[8,128]{1,0:T(8,128)S(1)} %bitcast.3, s32[1,8]{1,0:T(1,128)S(1)} %copy-done.5, bf16[1024,256]{1,0:T(8,128)(2,1)S(1)} %copy-done.2, bf16[1024,128]{1,0:T(8,128)(2,1)S(1)} %copy-done.3), custom_call_target="tpu_custom_call" | custom-call | tf_op jit(solution)/shard_map/pallas_call | solution.py:157
  5.5 14.1 %all-to-all-start = ((bf16[8,136,384]{2,1,0:T(8,128)(2,1)}), bf16[8,136,384]{2,1,0:T(8,128)(2,1)S(1)}, u32[]{:S(2)}, u32[]{:S(2)}) async-start(bf16[8,136,384]{2,1,0:T(8,128)(2,1)} %shard_map.86), calls=%async_computation | async-start | bytes 1671168 | tf_op jit(solution)/shard_map/all_to_all | solution.py:25
  19.6 0.0 copy-done.6
  19.6 20.6 %all_gather.6.rows_ref = bf16[96,1024]{1,0:T(8,128)(2,1)S(1)} all-gather(bf16[8,1024]{1,0:T(8,128)(2,1)S(1)} %copy-done.6), channel_id=1, replica_groups={{0,64,128,192,256,320,384,448,512,576,640,704},{8,72,136,200,264,328,39..., dimensions={0}, use_global_device_ids=true | all-gather | bytes 212992 | tf_op jit(solution)/shard_map/all_gather | solution.py:189
  40.2 0.0 all-to-all-done.packed_ref
  40.2 0.0 copy-done
  40.2 0.0 copy-done.1
  40.2 1.5 %shard_map.87 = bf16[8,104,256]{2,1,0:T(8,128)(2,1)S(1)} custom-call(bf16[8,136,384]{2,1,0:T(8,128)(2,1)S(1)} %all-to-all-done.packed_ref, bf16[256,128]{1,0:T(8,128)(2,1)S(1)} %copy-done.1, bf16[96,1024]{1,0:T(8,128)(2,1)S(1)} %all_gather.6.rows_ref, bf16[1024,128]{1,0:T(8,128)(2,1)S(1)} %copy-done), custom_call_target="tpu_custom_call" | custom-call | tf_op jit(solution)/shard_map/pallas_call | solution.py:157
  41.7 17.8 %all_to_all.30.met_ref = bf16[8,104,256]{2,1,0:T(8,128)(2,1)S(1)} all-to-all(bf16[8,104,256]{2,1,0:T(8,128)(2,1)S(1)} %shard_map.87), channel_id=1, replica_groups={{0,8,16,24,32,40,48,56},{64,72,80,88,96,104,112,120},{128,136,144,152,1..., dimensions={0} | all-to-all | bytes 851968 | tf_op jit(solution)/shard_map/all_to_all | solution.py:25
  59.6 2.0 %shard_map.88 = f32[1280,128]{1,0:T(8,128)S(1)} custom-call(bf16[8,136,384]{2,1,0:T(8,128)(2,1)S(1)} %all-to-all-done.packed_ref, bf16[256,128]{1,0:T(8,128)(2,1)S(1)} %copy-done.1, bf16[96,1024]{1,0:T(8,128)(2,1)S(1)} %all_gather.6.rows_ref, bf16[8,104,256]{2,1,0:T(8,128)(2,1)S(1)} %all_to_all.30.met_ref), custom_call_target="tpu_custom_call" | custom-call | tf_op jit(solution)/shard_map/pallas_call | solution.py:157
  61.5 21.5 %all_to_all.31 = f32[8,160,128]{2,1,0:T(8,128)S(1)} all-to-all(f32[8,160,128]{2,1,0:T(8,128)S(1)} %bitcast.2), channel_id=1, replica_groups=mesh['fact'=96,'key'=8] {'key'}, dimensions={0} | all-to-all | bytes 1310720 | tf_op jit(solution)/shard_map/all_to_all | solution.py:25
  83.1 9.8 %all_to_all.32 = f32[8,20,128]{2,1,0:T(8,128)S(1)} all-to-all(f32[8,20,128]{2,1,0:T(8,128)S(1)} %reshape.20), channel_id=1, replica_groups={{0,8,16,24,32,40,48,56},{64,72,80,88,96,104,112,120},{128,136,144,152,1..., dimensions={0} | all-to-all | bytes 163840 | tf_op jit(solution)/shard_map/all_to_all | solution.py:25
  93.0 13.4 %all_to_all.33 = f32[12,20,128]{2,1,0:T(8,128)S(1)} all-to-all(f32[12,20,128]{2,1,0:T(8,128)S(1)} %broadcast_in_dim.4), channel_id=1, replica_groups={{0,64,128,192,256,320,384,448,512,576,640,704},{8,72,136,200,264,328,39..., dimensions={0} | all-to-all | bytes 245760 | tf_op jit(solution)/shard_map/all_to_all | solution.py:25
  106.4 10.0 %all_to_all.34 = f32[8,20,128]{2,1,0:T(8,128)S(1)} all-to-all(f32[8,20,128]{2,1,0:T(8,128)S(1)} %broadcast_in_dim.5), channel_id=1, replica_groups={{0,8,16,24,32,40,48,56},{64,72,80,88,96,104,112,120},{128,136,144,152,1..., dimensions={0} | all-to-all | bytes 163840 | tf_op jit(solution)/shard_map/all_to_all | solution.py:25
  116.4 17.8 %all_gather.7 = f32[1280,128]{1,0:T(8,128)S(1)} all-gather(f32[160,128]{1,0:T(8,128)S(1)} %reshape.21), channel_id=1, replica_groups=mesh['fact'=96,'key'=8] {'key'}, dimensions={0}, use_global_device_ids=true | all-gather | bytes 737280 | tf_op jit(solution)/shard_map/all_gather | solution.py:41
  134.1 0.7 fusion.1
  134.8 0.9 fusion
  (11 shorter events, 0.1 us)
Async XLA Ops:
  0.6 0.7 copy-start.5
  1.3 1.0 copy-start.2
  2.3 0.9 copy-start.3
  3.3 0.7 copy-start.4
  5.5 14.1 %copy-start.6 = (bf16[8,1024]{1,0:T(8,128)(2,1)S(1)}, bf16[8,1024]{1,0:T(8,128)(2,1)}, u32[]{:S(2)}) copy-start(bf16[8,1024]{1,0:T(8,128)(2,1)} %param.11) | copy-start | bytes 49156
  5.5 34.7 %copy-start = (bf16[1024,128]{1,0:T(8,128)(2,1)S(1)}, bf16[1024,128]{1,0:T(8,128)(2,1)}, u32[]{:S(2)}) copy-start(bf16[1024,128]{1,0:T(8,128)(2,1)} %dim_weight_ref.1) | copy-start | bytes 786436
  5.5 34.7 %all-to-all-start = ((bf16[8,136,384]{2,1,0:T(8,128)(2,1)}), bf16[8,136,384]{2,1,0:T(8,128)(2,1)S(1)}, u32[]{:S(2)}, u32[]{:S(2)}) async-start(bf16[8,136,384]{2,1,0:T(8,128)(2,1)} %shard_map.86), calls=%async_computation | async-start | bytes 1671168 | tf_op jit(solution)/shard_map/all_to_all | solution.py:25
  19.6 20.6 %copy-start.1 = (bf16[256,128]{1,0:T(8,128)(2,1)S(1)}, bf16[256,128]{1,0:T(8,128)(2,1)}, u32[]{:S(2)}) copy-start(bf16[256,128]{1,0:T(8,128)(2,1)} %weight_ref.3) | copy-start | bytes 196612

commit v4 on v3

--- a/solution.py
+++ b/solution.py
@@ -14,11 +14,18 @@
 f32, bf16, i32 = jnp.float32, jnp.bfloat16, jnp.int32
 
 
-def fact_groups(fact_devices):
-    rings = fact_devices // ring_size
-    inner = [[ring * ring_size + i for i in range(ring_size)] for ring in range(rings)]
-    outer = [[ring * ring_size + i for ring in range(rings)] for i in range(ring_size)]
-    return inner, outer
+def groups_of(fact_devices, key_devices):
+    levels = range(fact_devices // ring_size)
+    chips, cores = range(key_devices // 2), range(2)
+    one_z = [[z * ring_size + y for y in range(ring_size)] for z in levels]
+    one_y = [[z * ring_size + y for z in levels] for y in range(ring_size)]
+    chip = [[2 * x + core for core in cores] for x in chips]
+    plane = [
+        [(z * ring_size + y) * key_devices + 2 * x + core for y in range(ring_size) for x in chips]
+        for z in levels
+        for core in cores
+    ]
+    return one_z, one_y, chip, plane
 
 
 def spread(array, axis, groups=None):
@@ -31,19 +38,34 @@
     return spread(jnp.broadcast_to(array[None], (copies, *array.shape)), axis, groups)
 
 
-def total_over_devices(terms, inner, outer):
+def total_over_devices(terms, one_y, chip, plane):
     width = terms.shape[1]
-    key_devices = lax.axis_size("key")
-    part = spread(terms.reshape(key_devices, -1, width), "key").sum(axis=0)
-    part = spread(part.reshape(ring_size, -1, width), "fact", inner).sum(axis=0)
-    part = collect(part, "fact", len(inner), outer).sum(axis=0)
-    part = collect(part, "fact", ring_size, inner).reshape(-1, width)
-    return lax.all_gather(part, "key", axis=0, tiled=True)
-
-
-def pack_slots(own_keys, ring_keys, keys_ref, fill_ref, features_ref, targets_ref, out_ref):
-    buckets, bucket_rows = keys_ref.shape
-    width, out_width = features_ref.shape[1], targets_ref.shape[1]
+    both = ("fact", "key")
+    members = len(plane[0])
+    part = spread(terms.reshape(2, -1, width), "key", chip).sum(axis=0)
+    part = spread(part.reshape(members, -1, width), both, plane).sum(axis=0)
+    part = collect(part, "fact", len(one_y[0]), one_y).sum(axis=0)
+    part = collect(part, both, members, plane).reshape(-1, width)
+    return lax.all_gather(part, "key", axis=0, tiled=True, axis_index_groups=chip)
+
+
+def pack_slots(
+    own_keys, ring_keys, keys_hbm, fill_hbm, features_hbm, targets_hbm, out_hbm, keys_ref, fill_ref, rows_ref, done
+):
+    buckets, bucket_rows, width = features_hbm.shape
+    out_width = targets_hbm.shape[2]
+    slots = pl.ds(0, bucket_rows)
+    copies = [
+        pltpu.make_async_copy(keys_hbm, keys_ref, done.at[0]),
+        pltpu.make_async_copy(fill_hbm, fill_ref, done.at[1]),
+        pltpu.make_async_copy(features_hbm, out_hbm.at[:, slots, pl.ds(0, width)], done.at[2]),
+        pltpu.make_async_copy(targets_hbm, out_hbm.at[:, slots, pl.ds(width, out_width)], done.at[3]),
+        pltpu.make_async_copy(rows_ref, out_hbm.at[:, pl.ds(bucket_rows, extra_rows), :], done.at[4]),
+    ]
+    for copy in copies[:4]:
+        copy.start()
+    copies[0].wait()
+    copies[1].wait()
     keys = keys_ref[...]
     owner = keys // (own_keys * buckets)
     places = (owner % ring_size) * ring_keys + (owner // ring_size) * own_keys + keys % own_keys
@@ -52,12 +74,11 @@
         codes = jnp.where(slot < fill_ref[0, b], places[b : b + 1], -digit)
         high = codes // digit
         low = codes - high * digit
-        rows = pl.ds(b * bucket_rows, bucket_rows)
-        out_ref[b, pl.ds(0, bucket_rows), pl.ds(0, width)] = features_ref[rows, :]
-        out_ref[b, pl.ds(0, bucket_rows), pl.ds(width, out_width)] = targets_ref[rows, :]
         digits = jnp.concatenate([high, low, jnp.zeros_like(high)], axis=1).astype(f32)
-        digits = jnp.broadcast_to(digits, (extra_rows, width + out_width))
-        out_ref[b, pl.ds(bucket_rows, extra_rows), :] = digits.astype(bf16)
+        rows_ref[b] = jnp.broadcast_to(digits, (extra_rows, width + out_width)).astype(bf16)
+    copies[4].start()
+    for copy in copies[2:]:
+        copy.wait()
 
 
 def codes_of(packed_ref, b):
@@ -152,12 +173,11 @@
     out_ref[pl.ds(width, rows_ref.shape[1]), :] = dim_term[:, :out_width] + dim_term[:, out_width:]
 
 
-def kernel_call(body, out_shape, dtype, *operands, smem=()):
-    spaces = [pltpu.SMEM if i in smem else pltpu.VMEM for i in range(len(operands))]
+def kernel_call(body, out_shape, dtype, *operands):
     return pl.pallas_call(
         body,
         out_shape=jax.ShapeDtypeStruct(out_shape, dtype),
-        in_specs=[pl.BlockSpec(memory_space=space) for space in spaces],
+        in_specs=[pl.BlockSpec(memory_space=pltpu.VMEM)] * len(operands),
         out_specs=pl.BlockSpec(memory_space=pltpu.VMEM),
         compiler_params=pltpu.CompilerParams(vmem_limit_bytes=32 << 20),
     )(*operands)
@@ -168,25 +188,34 @@
 ):
     key_devices = lax.axis_size("key")
     fact_devices = lax.axis_size("fact")
-    inner, outer = fact_groups(fact_devices)
+    one_z, one_y, chip, plane = groups_of(fact_devices, key_devices)
     slot_count = fact_keys.shape[0]
     bucket_rows = slot_count // key_devices
     own_keys, dim_width = dim_features.shape
     fact_width, out_width = fact_weight.shape
-    ring_keys = len(inner) * own_keys
-
-    packed = kernel_call(
+    ring_keys = len(one_z) * own_keys
+
+    packed = pl.pallas_call(
         functools.partial(pack_slots, own_keys, ring_keys),
-        (key_devices, bucket_rows + extra_rows, fact_width + out_width),
-        bf16,
+        out_shape=jax.ShapeDtypeStruct(
+            (key_devices, bucket_rows + extra_rows, fact_width + out_width), bf16
+        ),
+        in_specs=[pl.BlockSpec(memory_space=pl.ANY)] * 4,
+        out_specs=pl.BlockSpec(memory_space=pl.ANY),
+        scratch_shapes=[
+            pltpu.VMEM((key_devices, bucket_rows), i32),
+            pltpu.SMEM((1, key_devices), i32),
+            pltpu.VMEM((key_devices, extra_rows, fact_width + out_width), bf16),
+            pltpu.SemaphoreType.DMA((5,)),
+        ],
+    )(
         fact_keys.reshape(key_devices, bucket_rows),
         fill_counts,
-        fact_features,
-        targets,
-        smem=(1,),
+        fact_features.reshape(key_devices, bucket_rows, fact_width),
+        targets.reshape(key_devices, bucket_rows, out_width),
     )
     packed = spread(packed, "key")
-    rows = lax.all_gather(dim_features, "fact", axis=0, tiled=True, axis_index_groups=outer)
+    rows = lax.all_gather(dim_features, "fact", axis=0, tiled=True, axis_index_groups=one_y)
 
     met = kernel_call(
         sum_by_key,
@@ -197,12 +226,12 @@
         rows,
         dim_weight,
     )
-    met = spread(met, "fact", inner)
+    met = spread(met, "fact", one_z)
     terms = kernel_call(
         both_terms, (fact_width + dim_width, out_width), f32, packed, fact_weight, rows, met
     )
 
-    totals = total_over_devices(terms, inner, outer)
+    totals = total_over_devices(terms, one_y, chip, plane)
     total_rows = slot_count * fact_devices * key_devices
     row_scale = float(total_rows) ** (-0.5)
     grad_fact = totals[:fact_width] * row_scale + ridge_weight * fact_weight.astype(f32)

time: 136 us -> 149 us (1.096)
  Pallas kernels: 4.98 us -> 28.4 us
  blocking collectives: 111 us -> 104 us
  local copies, waits for them, and re-layouts: 3.37 us -> 0.11 us
    pallas_call x0 -> x1, Pallas kernels: none -> 25 us  [on_device(): pl.pallas_call(functools.partial(pack_slots, own_keys, ring_keys), out_sh...]
    all_gather x1, blocking collectives: 17.8 us -> 7.2 us  [total_over_devices(): lax.all_gather(part, 'key', axis=0, tiled=True, axis_index_groups=chip)]
    all_to_all x5, blocking collectives: 72.5 us -> 76 us  [spread(): lax.all_to_all(array, axis, split_axis=0, concat_axis=0, tiled=True, axis...]
    unnamed x14 -> x6, local copies, waits for them, and re-layouts: 3.34 us -> 0.02 us
    pallas_call x3 -> x2, Pallas kernels: 4.98 us -> 3.45 us  [kernel_call(): pl.pallas_call(body, out_shape=jax.ShapeDtypeStruct(out_shape, dtype), in...]
where the time goes in v4:
time: 149 us
  blocking collectives  104 us (70%)
  Pallas kernels  28.4 us (19%)
  starting transfers between devices  14.1 us (9%)
  other arithmetic  1.64 us (1%)
    all_to_all x5, blocking collectives, spread(): lax.all_to_all(array, axis, split_axis=0, concat_axis=0, tiled=True, axis...  76 us
    pallas_call x1, Pallas kernels, on_device(): pl.pallas_call(functools.partial(pack_slots, own_keys, ring_keys), out_sh...  25 us
    all_gather x1, blocking collectives, on_device(): lax.all_gather(dim_features, 'fact', axis=0, tiled=True, axis_index_group...  20.6 us
    all_to_all x1, starting transfers between devices, spread(): lax.all_to_all(array, axis, split_axis=0, concat_axis=0, tiled=True, axis...  14.1 us
    all_gather x1, blocking collectives, total_over_devices(): lax.all_gather(part, 'key', axis=0, tiled=True, axis_index_groups=chip)  7.2 us
    pallas_call x2, Pallas kernels, kernel_call(): pl.pallas_call(body, out_shape=jax.ShapeDtypeStruct(out_shape, dtype), in...  3.45 us
  transfers between devices with their start and end apart: 1, of which 0 were waited for; matrix products, arithmetic and copies ran while one was open for 0% of the time, Pallas kernels for 0%

profile of v4, /device:TPU:1, one launch (start us, length us, event | category | flops | bytes accessed | tf_op | source)
XLA Modules:
  0.0 148.8 jit_solution(5299305922614060859)
XLA Ops:
  0.6 25.0 %shard_map.86 = bf16[8,136,384]{2,1,0:T(8,128)(2,1)} custom-call(s32[8,128]{1,0:T(8,128)} %bitcast.7, s32[1,8]{1,0:T(1,128)} %fill_hbm.1, bf16[8,128,256]{2,1,0:T(8,128)(2,1)} %bitcast.5, bf16[8,128,128]{2,1,0:T(8,128)(2,1)} %bitcast.6), custom_call_target="tpu_custom_call" | custom-call | tf_op jit(solution)/shard_map/pallas_call | solution.py:198
  25.6 0.0 copy-start.2
  25.6 0.0 copy-start
  25.6 14.1 %all-to-all-start = ((bf16[8,136,384]{2,1,0:T(8,128)(2,1)}), bf16[8,136,384]{2,1,0:T(8,128)(2,1)S(1)}, u32[]{:S(2)}, u32[]{:S(2)}) async-start(bf16[8,136,384]{2,1,0:T(8,128)(2,1)} %shard_map.86), calls=%async_computation | async-start | bytes 1671168 | tf_op jit(solution)/shard_map/all_to_all | solution.py:32
  39.7 0.0 copy-done.2
  39.8 0.0 copy-start.1
  39.8 20.6 %all_gather.6.rows_ref = bf16[96,1024]{1,0:T(8,128)(2,1)S(1)} all-gather(bf16[8,1024]{1,0:T(8,128)(2,1)S(1)} %copy-done.2), channel_id=1, replica_groups={{0,64,128,192,256,320,384,448,512,576,640,704},{8,72,136,200,264,328,39..., dimensions={0}, use_global_device_ids=true | all-gather | bytes 212992 | tf_op jit(solution)/shard_map/all_gather | solution.py:218
  60.4 0.0 all-to-all-done.packed_ref
  60.4 0.0 copy-done
  60.4 0.0 copy-done.1
  60.4 1.5 shard_map.87
  61.9 17.8 %all_to_all.30.met_ref = bf16[8,104,256]{2,1,0:T(8,128)(2,1)S(1)} all-to-all(bf16[8,104,256]{2,1,0:T(8,128)(2,1)S(1)} %shard_map.87), channel_id=1, replica_groups={{0,8,16,24,32,40,48,56},{64,72,80,88,96,104,112,120},{128,136,144,152,1..., dimensions={0} | all-to-all | bytes 851968 | tf_op jit(solution)/shard_map/all_to_all | solution.py:32
  79.7 2.0 %shard_map.88 = f32[1280,128]{1,0:T(8,128)S(1)} custom-call(bf16[8,136,384]{2,1,0:T(8,128)(2,1)S(1)} %all-to-all-done.packed_ref, bf16[256,128]{1,0:T(8,128)(2,1)S(1)} %copy-done.1, bf16[96,1024]{1,0:T(8,128)(2,1)S(1)} %all_gather.6.rows_ref, bf16[8,104,256]{2,1,0:T(8,128)(2,1)S(1)} %all_to_all.30.met_ref), custom_call_target="tpu_custom_call" | custom-call | tf_op jit(solution)/shard_map/pallas_call | solution.py:177
  81.7 9.9 %all_to_all.31 = f32[2,640,128]{2,1,0:T(8,128)S(1)} all-to-all(f32[2,640,128]{2,1,0:T(8,128)S(1)} %bitcast.4), channel_id=1, replica_groups={{0,1},{2,3},{4,5},{6,7},{8,9},{10,11},{12,13},{14,15},{16,17},{18,19},{..., dimensions={0} | all-to-all | bytes 1310720 | tf_op jit(solution)/shard_map/all_to_all | solution.py:32
  91.6 18.6 %all_to_all.32 = f32[32,20,128]{2,1,0:T(8,128)S(1)} all-to-all(f32[32,20,128]{2,1,0:T(8,128)S(1)} %reshape.28), channel_id=1, replica_groups={{0,2,4,6,8,10,12,14,16,18,20,22,24,26,28,30,32,34,36,38,40,42,44,46,48,..., dimensions={0} | all-to-all | bytes 655360 | tf_op jit(solution)/shard_map/all_to_all | solution.py:32
  110.3 13.4 %all_to_all.33 = f32[12,20,128]{2,1,0:T(8,128)S(1)} all-to-all(f32[12,20,128]{2,1,0:T(8,128)S(1)} %broadcast_in_dim.4), channel_id=1, replica_groups={{0,64,128,192,256,320,384,448,512,576,640,704},{8,72,136,200,264,328,39..., dimensions={0} | all-to-all | bytes 245760 | tf_op jit(solution)/shard_map/all_to_all | solution.py:32
  123.7 16.3 %all_to_all.34 = f32[32,20,128]{2,1,0:T(8,128)S(1)} all-to-all(f32[32,20,128]{2,1,0:T(8,128)S(1)} %broadcast_in_dim.5), channel_id=1, replica_groups={{0,2,4,6,8,10,12,14,16,18,20,22,24,26,28,30,32,34,36,38,40,42,44,46,48,..., dimensions={0} | all-to-all | bytes 655360 | tf_op jit(solution)/shard_map/all_to_all | solution.py:32
  140.1 7.2 %all_gather.7 = f32[1280,128]{1,0:T(8,128)S(1)} all-gather(f32[640,128]{1,0:T(8,128)S(1)} %reshape.29), channel_id=1, replica_groups={{0,1},{2,3},{4,5},{6,7},{8,9},{10,11},{12,13},{14,15},{16,17},{18,19},{..., dimensions={0}, use_global_device_ids=true | all-gather | bytes 983040 | tf_op jit(solution)/shard_map/all_gather | solution.py:49
  147.3 0.7 fusion.1
  147.9 0.9 fusion
  (7 shorter events, 0.2 us)
Async XLA Ops:
  25.6 14.1 %copy-start.2 = (bf16[8,1024]{1,0:T(8,128)(2,1)S(1)}, bf16[8,1024]{1,0:T(8,128)(2,1)}, u32[]{:S(2)}) copy-start(bf16[8,1024]{1,0:T(8,128)(2,1)} %param.11) | copy-start | bytes 49156
  25.6 34.7 %copy-start = (bf16[1024,128]{1,0:T(8,128)(2,1)S(1)}, bf16[1024,128]{1,0:T(8,128)(2,1)}, u32[]{:S(2)}) copy-start(bf16[1024,128]{1,0:T(8,128)(2,1)} %dim_weight_ref.1) | copy-start | bytes 786436
  25.6 34.7 %all-to-all-start = ((bf16[8,136,384]{2,1,0:T(8,128)(2,1)}), bf16[8,136,384]{2,1,0:T(8,128)(2,1)S(1)}, u32[]{:S(2)}, u32[]{:S(2)}) async-start(bf16[8,136,384]{2,1,0:T(8,128)(2,1)} %shard_map.86), calls=%async_computation | async-start | bytes 1671168 | tf_op jit(solution)/shard_map/all_to_all | solution.py:32
  39.8 20.6 %copy-start.1 = (bf16[256,128]{1,0:T(8,128)(2,1)S(1)}, bf16[256,128]{1,0:T(8,128)(2,1)}, u32[]{:S(2)}) copy-start(bf16[256,128]{1,0:T(8,128)(2,1)} %weight_ref.3) | copy-start | bytes 196612

commit v5 on v4

--- a/solution.py
+++ b/solution.py
@@ -50,7 +50,7 @@
 
 
 def pack_slots(
-    own_keys, ring_keys, keys_hbm, fill_hbm, features_hbm, targets_hbm, out_hbm, keys_ref, fill_ref, rows_ref, done
+    own_keys, ring_keys, keys_hbm, fill_hbm, features_hbm, targets_hbm, out_ref, keys_ref, fill_ref, done
 ):
     buckets, bucket_rows, width = features_hbm.shape
     out_width = targets_hbm.shape[2]
@@ -58,11 +58,10 @@
     copies = [
         pltpu.make_async_copy(keys_hbm, keys_ref, done.at[0]),
         pltpu.make_async_copy(fill_hbm, fill_ref, done.at[1]),
-        pltpu.make_async_copy(features_hbm, out_hbm.at[:, slots, pl.ds(0, width)], done.at[2]),
-        pltpu.make_async_copy(targets_hbm, out_hbm.at[:, slots, pl.ds(width, out_width)], done.at[3]),
-        pltpu.make_async_copy(rows_ref, out_hbm.at[:, pl.ds(bucket_rows, extra_rows), :], done.at[4]),
+        pltpu.make_async_copy(features_hbm, out_ref.at[:, slots, pl.ds(0, width)], done.at[2]),
+        pltpu.make_async_copy(targets_hbm, out_ref.at[:, slots, pl.ds(width, out_width)], done.at[3]),
     ]
-    for copy in copies[:4]:
+    for copy in copies:
         copy.start()
     copies[0].wait()
     copies[1].wait()
@@ -75,8 +74,8 @@
         high = codes // digit
         low = codes - high * digit
         digits = jnp.concatenate([high, low, jnp.zeros_like(high)], axis=1).astype(f32)
-        rows_ref[b] = jnp.broadcast_to(digits, (extra_rows, width + out_width)).astype(bf16)
-    copies[4].start()
+        digits = jnp.broadcast_to(digits, (extra_rows, width + out_width))
+        out_ref[b, pl.ds(bucket_rows, extra_rows), :] = digits.astype(bf16)
     for copy in copies[2:]:
         copy.wait()
 
@@ -201,12 +200,11 @@
             (key_devices, bucket_rows + extra_rows, fact_width + out_width), bf16
         ),
         in_specs=[pl.BlockSpec(memory_space=pl.ANY)] * 4,
-        out_specs=pl.BlockSpec(memory_space=pl.ANY),
+        out_specs=pl.BlockSpec(memory_space=pltpu.VMEM),
         scratch_shapes=[
             pltpu.VMEM((key_devices, bucket_rows), i32),
             pltpu.SMEM((1, key_devices), i32),
-            pltpu.VMEM((key_devices, extra_rows, fact_width + out_width), bf16),
-            pltpu.SemaphoreType.DMA((5,)),
+            pltpu.SemaphoreType.DMA((4,)),
         ],
     )(
         fact_keys.reshape(key_devices, bucket_rows),

time: 149 us -> 126 us (0.85)
  Pallas kernels: 28.4 us -> 5.51 us
    pallas_call x1, Pallas kernels: 25 us -> 2.07 us  [on_device(): pl.pallas_call(functools.partial(pack_slots, own_keys, ring_keys), out_sh...]
where the time goes in v5:
time: 126 us
  blocking collectives  104 us (83%)
  starting transfers between devices  14.1 us (11%)
  Pallas kernels  5.51 us (4%)
  other arithmetic  1.64 us (1%)
    all_to_all x5, blocking collectives, spread(): lax.all_to_all(array, axis, split_axis=0, concat_axis=0, tiled=True, axis...  76 us
    all_gather x1, blocking collectives, on_device(): lax.all_gather(dim_features, 'fact', axis=0, tiled=True, axis_index_group...  20.6 us
    all_to_all x1, starting transfers between devices, spread(): lax.all_to_all(array, axis, split_axis=0, concat_axis=0, tiled=True, axis...  14.1 us
    all_gather x1, blocking collectives, total_over_devices(): lax.all_gather(part, 'key', axis=0, tiled=True, axis_index_groups=chip)  7.2 us
    pallas_call x2, Pallas kernels, kernel_call(): pl.pallas_call(body, out_shape=jax.ShapeDtypeStruct(out_shape, dtype), in...  3.45 us
  transfers between devices with their start and end apart: 1, of which 0 were waited for; matrix products, arithmetic and copies ran while one was open for 0% of the time, Pallas kernels for 0%

profile of v5, /device:TPU:1, one launch (start us, length us, event | category | flops | bytes accessed | tf_op | source)
XLA Modules:
  0.0 125.9 jit_solution(17818704465203507204)
XLA Ops:
  0.6 2.1 %shard_map.86 = bf16[8,136,384]{2,1,0:T(8,128)(2,1)} custom-call(s32[8,128]{1,0:T(8,128)} %bitcast.7, s32[1,8]{1,0:T(1,128)} %fill_hbm.1, bf16[8,128,256]{2,1,0:T(8,128)(2,1)} %bitcast.5, bf16[8,128,128]{2,1,0:T(8,128)(2,1)} %bitcast.6), custom_call_target="tpu_custom_call" | custom-call | tf_op jit(solution)/shard_map/pallas_call | solution.py:197
  2.7 0.0 copy-start.2
  2.7 0.0 copy-start
  2.7 14.1 %all-to-all-start = ((bf16[8,136,384]{2,1,0:T(8,128)(2,1)}), bf16[8,136,384]{2,1,0:T(8,128)(2,1)S(1)}, u32[]{:S(2)}, u32[]{:S(2)}) async-start(bf16[8,136,384]{2,1,0:T(8,128)(2,1)} %shard_map.86), calls=%async_computation | async-start | bytes 1671168 | tf_op jit(solution)/shard_map/all_to_all | solution.py:32
  16.8 0.0 copy-done.2
  16.8 0.0 copy-start.1
  16.8 20.6 %all_gather.6.rows_ref = bf16[96,1024]{1,0:T(8,128)(2,1)S(1)} all-gather(bf16[8,1024]{1,0:T(8,128)(2,1)S(1)} %copy-done.2), channel_id=1, replica_groups={{0,64,128,192,256,320,384,448,512,576,640,704},{8,72,136,200,264,328,39..., dimensions={0}, use_global_device_ids=true | all-gather | bytes 212992 | tf_op jit(solution)/shard_map/all_gather | solution.py:216
  37.5 0.0 all-to-all-done.packed_ref
  37.5 0.0 copy-done
  37.5 0.0 copy-done.1
  37.5 1.5 %shard_map.87 = bf16[8,104,256]{2,1,0:T(8,128)(2,1)S(1)} custom-call(bf16[8,136,384]{2,1,0:T(8,128)(2,1)S(1)} %all-to-all-done.packed_ref, bf16[256,128]{1,0:T(8,128)(2,1)S(1)} %copy-done.1, bf16[96,1024]{1,0:T(8,128)(2,1)S(1)} %all_gather.6.rows_ref, bf16[1024,128]{1,0:T(8,128)(2,1)S(1)} %copy-done), custom_call_target="tpu_custom_call" | custom-call | tf_op jit(solution)/shard_map/pallas_call | solution.py:176
  39.0 17.8 %all_to_all.30.met_ref = bf16[8,104,256]{2,1,0:T(8,128)(2,1)S(1)} all-to-all(bf16[8,104,256]{2,1,0:T(8,128)(2,1)S(1)} %shard_map.87), channel_id=1, replica_groups={{0,8,16,24,32,40,48,56},{64,72,80,88,96,104,112,120},{128,136,144,152,1..., dimensions={0} | all-to-all | bytes 851968 | tf_op jit(solution)/shard_map/all_to_all | solution.py:32
  56.8 2.0 %shard_map.88 = f32[1280,128]{1,0:T(8,128)S(1)} custom-call(bf16[8,136,384]{2,1,0:T(8,128)(2,1)S(1)} %all-to-all-done.packed_ref, bf16[256,128]{1,0:T(8,128)(2,1)S(1)} %copy-done.1, bf16[96,1024]{1,0:T(8,128)(2,1)S(1)} %all_gather.6.rows_ref, bf16[8,104,256]{2,1,0:T(8,128)(2,1)S(1)} %all_to_all.30.met_ref), custom_call_target="tpu_custom_call" | custom-call | tf_op jit(solution)/shard_map/pallas_call | solution.py:176
  58.8 9.9 %all_to_all.31 = f32[2,640,128]{2,1,0:T(8,128)S(1)} all-to-all(f32[2,640,128]{2,1,0:T(8,128)S(1)} %bitcast.4), channel_id=1, replica_groups={{0,1},{2,3},{4,5},{6,7},{8,9},{10,11},{12,13},{14,15},{16,17},{18,19},{..., dimensions={0} | all-to-all | bytes 1310720 | tf_op jit(solution)/shard_map/all_to_all | solution.py:32
  68.7 18.6 %all_to_all.32 = f32[32,20,128]{2,1,0:T(8,128)S(1)} all-to-all(f32[32,20,128]{2,1,0:T(8,128)S(1)} %reshape.28), channel_id=1, replica_groups={{0,2,4,6,8,10,12,14,16,18,20,22,24,26,28,30,32,34,36,38,40,42,44,46,48,..., dimensions={0} | all-to-all | bytes 655360 | tf_op jit(solution)/shard_map/all_to_all | solution.py:32
  87.3 13.4 %all_to_all.33 = f32[12,20,128]{2,1,0:T(8,128)S(1)} all-to-all(f32[12,20,128]{2,1,0:T(8,128)S(1)} %broadcast_in_dim.4), channel_id=1, replica_groups={{0,64,128,192,256,320,384,448,512,576,640,704},{8,72,136,200,264,328,39..., dimensions={0} | all-to-all | bytes 245760 | tf_op jit(solution)/shard_map/all_to_all | solution.py:32
  100.8 16.3 %all_to_all.34 = f32[32,20,128]{2,1,0:T(8,128)S(1)} all-to-all(f32[32,20,128]{2,1,0:T(8,128)S(1)} %broadcast_in_dim.5), channel_id=1, replica_groups={{0,2,4,6,8,10,12,14,16,18,20,22,24,26,28,30,32,34,36,38,40,42,44,46,48,..., dimensions={0} | all-to-all | bytes 655360 | tf_op jit(solution)/shard_map/all_to_all | solution.py:32
  117.1 7.2 %all_gather.7 = f32[1280,128]{1,0:T(8,128)S(1)} all-gather(f32[640,128]{1,0:T(8,128)S(1)} %reshape.29), channel_id=1, replica_groups={{0,1},{2,3},{4,5},{6,7},{8,9},{10,11},{12,13},{14,15},{16,17},{18,19},{..., dimensions={0}, use_global_device_ids=true | all-gather | bytes 983040 | tf_op jit(solution)/shard_map/all_gather | solution.py:49
  124.3 0.7 fusion.1
  125.0 0.9 fusion
  (7 shorter events, 0.2 us)
Async XLA Ops:
  2.7 14.1 %copy-start.2 = (bf16[8,1024]{1,0:T(8,128)(2,1)S(1)}, bf16[8,1024]{1,0:T(8,128)(2,1)}, u32[]{:S(2)}) copy-start(bf16[8,1024]{1,0:T(8,128)(2,1)} %param.11) | copy-start | bytes 49156
  2.7 34.7 %copy-start = (bf16[1024,128]{1,0:T(8,128)(2,1)S(1)}, bf16[1024,128]{1,0:T(8,128)(2,1)}, u32[]{:S(2)}) copy-start(bf16[1024,128]{1,0:T(8,128)(2,1)} %dim_weight_ref.1) | copy-start | bytes 786436
  2.7 34.7 %all-to-all-start = ((bf16[8,136,384]{2,1,0:T(8,128)(2,1)}), bf16[8,136,384]{2,1,0:T(8,128)(2,1)S(1)}, u32[]{:S(2)}, u32[]{:S(2)}) async-start(bf16[8,136,384]{2,1,0:T(8,128)(2,1)} %shard_map.86), calls=%async_computation | async-start | bytes 1671168 | tf_op jit(solution)/shard_map/all_to_all | solution.py:32
  16.8 20.6 %copy-start.1 = (bf16[256,128]{1,0:T(8,128)(2,1)S(1)}, bf16[256,128]{1,0:T(8,128)(2,1)}, u32[]{:S(2)}) copy-start(bf16[256,128]{1,0:T(8,128)(2,1)} %weight_ref.3) | copy-start | bytes 196612

commit v6 on v5

--- a/solution.py
+++ b/solution.py
@@ -39,14 +39,15 @@
 
 
 def total_over_devices(terms, one_y, chip, plane):
-    width = terms.shape[1]
+    rows, width = terms.shape
     both = ("fact", "key")
     members = len(plane[0])
-    part = spread(terms.reshape(2, -1, width), "key", chip).sum(axis=0)
-    part = spread(part.reshape(members, -1, width), both, plane).sum(axis=0)
+    part = spread(terms.reshape(2, -1, 4, width), "key", chip).sum(axis=0)
+    part = spread(part.reshape(members, -1, 4, width), both, plane).sum(axis=0)
     part = collect(part, "fact", len(one_y[0]), one_y).sum(axis=0)
-    part = collect(part, both, members, plane).reshape(-1, width)
-    return lax.all_gather(part, "key", axis=0, tiled=True, axis_index_groups=chip)
+    part = collect(part, both, members, plane).reshape(-1, 4, width)
+    part = lax.all_gather(part, "key", axis=0, tiled=True, axis_index_groups=chip)
+    return part.reshape(rows, width)
 
 
 def pack_slots(
@@ -87,42 +88,50 @@
     return codes.astype(i32)[:1]
 
 
-def partial_of(packed_ref, weight_ref, b):
-    bucket_rows = packed_ref.shape[1] - extra_rows
+def partial_of(packed_ref, weight_ref, pair):
+    slots = pl.ds(0, packed_ref.shape[1] - extra_rows)
     width = weight_ref.shape[0]
-    slots = packed_ref[b, pl.ds(0, bucket_rows), :]
-    features = slots[:, :width]
+    rows = jnp.concatenate([packed_ref[b, slots, :] for b in pair], axis=0)
+    features = rows[:, :width]
     value = jnp.dot(features, weight_ref[...], preferred_element_type=f32)
-    return features, value - slots[:, width:].astype(f32)
+    return features, value - rows[:, width:].astype(f32)
+
+
+def pairs_of(packed_ref):
+    return [(b, b + 1) for b in range(0, packed_ref.shape[0], 2)]
+
+
+def diagonal_of(rows, columns):
+    return lax.broadcasted_iota(i32, (rows, columns), 0) == lax.broadcasted_iota(
+        i32, (rows, columns), 1
+    )
 
 
 def sum_by_key(packed_ref, weight_ref, rows_ref, dim_weight_ref, out_ref):
     members, _, two_widths = out_ref.shape
     out_width = two_widths // 2
     ring_keys = rows_ref.shape[0]
-    buckets = packed_ref.shape[0]
-    bucket_rows = packed_ref.shape[1] - extra_rows
-    places = lax.broadcasted_iota(i32, (members * ring_keys, bucket_rows), 0)
-    ones = jnp.ones((extra_rows, bucket_rows), bf16)
-    sums = jnp.zeros((members * ring_keys, out_width), f32)
-    counts = jnp.zeros((extra_rows, members * ring_keys), f32)
-    for b in range(buckets):
-        one_hot = jnp.where(places == codes_of(packed_ref, b), f32(1.0), f32(0.0)).astype(bf16)
-        _, value = partial_of(packed_ref, weight_ref, b)
-        sums += jnp.dot(one_hot, value.astype(bf16), preferred_element_type=f32)
-        counts += lax.dot_general(
-            ones, one_hot, (((1,), (1,)), ((), ())), preferred_element_type=f32
-        )
+    two_rows = 2 * (packed_ref.shape[1] - extra_rows)
+    places = lax.broadcasted_iota(i32, (members * ring_keys, two_rows), 0)
+    ones = jnp.ones((two_rows, out_width), bf16)
+    sums = jnp.zeros((members * ring_keys, two_widths), f32)
+    for pair in pairs_of(packed_ref):
+        codes = jnp.concatenate([codes_of(packed_ref, b) for b in pair], axis=1)
+        one_hot = jnp.where(places == codes, f32(1.0), f32(0.0)).astype(bf16)
+        _, value = partial_of(packed_ref, weight_ref, pair)
+        value = jnp.concatenate([value.astype(bf16), ones], axis=1)
+        sums += jnp.dot(one_hot, value, preferred_element_type=f32)
     values = jnp.dot(rows_ref[...], dim_weight_ref[...], preferred_element_type=f32).astype(bf16)
-    high = jnp.floor(counts * (1.0 / digit))
-    low = counts - high * digit
-    rest = jnp.zeros((extra_rows, out_width - ring_keys), f32)
+    diagonal = diagonal_of(ring_keys, out_width)
+    own = pl.ds(0, ring_keys)
     for m in range(members):
-        own = pl.ds(0, ring_keys)
-        part = slice(m * ring_keys, (m + 1) * ring_keys)
-        out_ref[m, own, pl.ds(0, out_width)] = sums[part].astype(bf16)
+        part = sums[m * ring_keys : (m + 1) * ring_keys]
+        out_ref[m, own, pl.ds(0, out_width)] = part[:, :out_width].astype(bf16)
         out_ref[m, own, pl.ds(out_width, out_width)] = values
-        digits = jnp.concatenate([high[:, part], rest, low[:, part], rest], axis=1)
+        counts = jnp.where(diagonal, part[:, out_width:], f32(0.0)).sum(axis=0, keepdims=True)
+        high = jnp.floor(counts * (1.0 / digit))
+        digits = jnp.concatenate([high, counts - high * digit], axis=1)
+        digits = jnp.broadcast_to(digits, (extra_rows, two_widths))
         out_ref[m, pl.ds(ring_keys, extra_rows), :] = digits.astype(bf16)
 
 
@@ -143,12 +152,14 @@
     codes = jnp.transpose(codes.astype(f32)).astype(i32)
     places = lax.broadcasted_iota(i32, (bucket_rows, members * ring_keys), 1)
     fact_term = jnp.zeros((width, out_width), f32)
-    for b in range(buckets):
-        code = codes[:, b : b + 1]
-        one_hot = jnp.where(places == code, f32(1.0), f32(0.0)).astype(bf16)
-        features, value = partial_of(packed_ref, weight_ref, b)
-        found = jnp.dot(one_hot, values, preferred_element_type=f32)
-        residual = jnp.where(code >= 0, value + found, f32(0.0)).astype(bf16)
+    for pair in pairs_of(packed_ref):
+        one_hot = [
+            jnp.where(places == codes[:, b : b + 1], f32(1.0), f32(0.0)).astype(bf16) for b in pair
+        ]
+        features, value = partial_of(packed_ref, weight_ref, pair)
+        found = jnp.dot(jnp.concatenate(one_hot, axis=0), values, preferred_element_type=f32)
+        live = jnp.concatenate([codes[:, b : b + 1] for b in pair], axis=0) >= 0
+        residual = jnp.where(live, value + found, f32(0.0)).astype(bf16)
         fact_term += lax.dot_general(features, residual, contract, preferred_element_type=f32)
     out_ref[pl.ds(0, width), :] = fact_term
 
@@ -159,9 +170,7 @@
         sums += met_ref[m, own, pl.ds(0, out_width)].astype(f32)
         digits += met_ref[m, pl.ds(ring_keys, extra_rows), :].astype(f32)
     counts = digits[:1, :out_width] * digit + digits[:1, out_width:]
-    diagonal = lax.broadcasted_iota(i32, (ring_keys, out_width), 0) == lax.broadcasted_iota(
-        i32, (ring_keys, out_width), 1
-    )
+    diagonal = diagonal_of(ring_keys, out_width)
     counts = jnp.sum(jnp.where(diagonal, counts, f32(0.0)), axis=1, keepdims=True)
     sums += counts * met_ref[me, own, pl.ds(out_width, out_width)].astype(f32)
     high = sums.astype(bf16)
@@ -170,6 +179,16 @@
         rows_ref[...], jnp.concatenate([high, low], axis=1), contract, preferred_element_type=f32
     )
     out_ref[pl.ds(width, rows_ref.shape[1]), :] = dim_term[:, :out_width] + dim_term[:, out_width:]
+
+
+def finish(row_scale, totals_ref, fact_weight_ref, dim_weight_ref, fact_ref, dim_ref):
+    width = fact_ref.shape[0]
+    fact_ref[...] = totals_ref[pl.ds(0, width), :] * row_scale + ridge_weight * fact_weight_ref[
+        ...
+    ].astype(f32)
+    dim_ref[...] = totals_ref[
+        pl.ds(width, dim_ref.shape[0]), :
+    ] * row_scale + ridge_weight * dim_weight_ref[...].astype(f32)
 
 
 def kernel_call(body, out_shape, dtype, *operands):
@@ -232,9 +251,19 @@
     totals = total_over_devices(terms, one_y, chip, plane)
     total_rows = slot_count * fact_devices * key_devices
     row_scale = float(total_rows) ** (-0.5)
-    grad_fact = totals[:fact_width] * row_scale + ridge_weight * fact_weight.astype(f32)
-    grad_dim = totals[fact_width:] * row_scale + ridge_weight * dim_weight.astype(f32)
-    return (grad_fact, grad_dim)
+    vmem = pl.BlockSpec(memory_space=pltpu.VMEM)
+    return tuple(
+        pl.pallas_call(
+            functools.partial(finish, row_scale),
+            out_shape=(
+                jax.ShapeDtypeStruct((fact_width, out_width), f32),
+                jax.ShapeDtypeStruct((dim_width, out_width), f32),
+            ),
+            in_specs=[vmem] * 3,
+            out_specs=(vmem, vmem),
+            compiler_params=pltpu.CompilerParams(vmem_limit_bytes=16 << 20),
+        )(totals, fact_weight, dim_weight)
+    )
 
 
 def solution(mesh):

time: 126 us -> 122 us (0.968)
  blocking collectives: 104 us -> 101 us
  other arithmetic: 1.64 us -> 0.35 us
    all_to_all x5, blocking collectives: 76 us -> 73.5 us  [spread(): lax.all_to_all(array, axis, split_axis=0, concat_axis=0, tiled=True, axis...]
    add x2 -> x0, other arithmetic: 1.55 us -> none  [the longest x1 0.87 us: on_device(): totals[fact_width:] * row_scale + ridge_weight * dim_weight.astype(f32)]
where the time goes in v6:
time: 122 us
  blocking collectives  101 us (83%)
  starting transfers between devices  14.1 us (12%)
  Pallas kernels  5.78 us (5%)
    all_to_all x5, blocking collectives, spread(): lax.all_to_all(array, axis, split_axis=0, concat_axis=0, tiled=True, axis...  73.5 us
    all_gather x1, blocking collectives, on_device(): lax.all_gather(dim_features, 'fact', axis=0, tiled=True, axis_index_group...  20.6 us
    all_to_all x1, starting transfers between devices, spread(): lax.all_to_all(array, axis, split_axis=0, concat_axis=0, tiled=True, axis...  14.1 us
    all_gather x1, blocking collectives, total_over_devices(): lax.all_gather(part, 'key', axis=0, tiled=True, axis_index_groups=chip)  6.49 us
    pallas_call x2, Pallas kernels, kernel_call(): pl.pallas_call(body, out_shape=jax.ShapeDtypeStruct(out_shape, dtype), in...  2.83 us
  transfers between devices with their start and end apart: 1, of which 0 were waited for; matrix products, arithmetic and copies ran while one was open for 0% of the time, Pallas kernels for 0%

profile of v6, /device:TPU:1, one launch (start us, length us, event | category | flops | bytes accessed | tf_op | source)
XLA Modules:
  0.0 121.7 jit_solution(4960321123083617187)
XLA Ops:
  0.6 2.1 %shard_map.86 = bf16[8,136,384]{2,1,0:T(8,128)(2,1)} custom-call(s32[8,128]{1,0:T(8,128)} %bitcast.13, s32[1,8]{1,0:T(1,128)} %fill_hbm.1, bf16[8,128,256]{2,1,0:T(8,128)(2,1)} %bitcast.11, bf16[8,128,128]{2,1,0:T(8,128)(2,1)} %bitcast.12), custom_call_target="tpu_custom_call" | custom-call | tf_op jit(solution)/shard_map/pallas_call | solution.py:216
  2.7 0.0 copy-start.2
  2.7 0.0 copy-start
  2.7 14.1 %all-to-all-start = ((bf16[8,136,384]{2,1,0:T(8,128)(2,1)}), bf16[8,136,384]{2,1,0:T(8,128)(2,1)S(1)}, u32[]{:S(2)}, u32[]{:S(2)}) async-start(bf16[8,136,384]{2,1,0:T(8,128)(2,1)} %shard_map.86), calls=%async_computation | async-start | bytes 1671168 | tf_op jit(solution)/shard_map/all_to_all | solution.py:32
  16.8 0.0 copy-done.2
  16.8 0.0 copy-start.1
  16.8 20.6 %all_gather.6.rows_ref = bf16[96,1024]{1,0:T(8,128)(2,1)S(1)} all-gather(bf16[8,1024]{1,0:T(8,128)(2,1)S(1)} %copy-done.2), channel_id=1, replica_groups={{0,64,128,192,256,320,384,448,512,576,640,704},{8,72,136,200,264,328,39..., dimensions={0}, use_global_device_ids=true | all-gather | bytes 212992 | tf_op jit(solution)/shard_map/all_gather | solution.py:235
  37.5 0.0 all-to-all-done.packed_ref
  37.5 0.0 copy-done
  37.5 0.0 copy-done.1
  37.5 1.2 %shard_map.87 = bf16[8,104,256]{2,1,0:T(8,128)(2,1)S(1)} custom-call(bf16[8,136,384]{2,1,0:T(8,128)(2,1)S(1)} %all-to-all-done.packed_ref, bf16[256,128]{1,0:T(8,128)(2,1)S(1)} %copy-done.1, bf16[96,1024]{1,0:T(8,128)(2,1)S(1)} %all_gather.6.rows_ref, bf16[1024,128]{1,0:T(8,128)(2,1)S(1)} %copy-done), custom_call_target="tpu_custom_call" | custom-call | tf_op jit(solution)/shard_map/pallas_call | solution.py:195
  38.7 17.8 %all_to_all.30.met_ref = bf16[8,104,256]{2,1,0:T(8,128)(2,1)S(1)} all-to-all(bf16[8,104,256]{2,1,0:T(8,128)(2,1)S(1)} %shard_map.87), channel_id=1, replica_groups={{0,8,16,24,32,40,48,56},{64,72,80,88,96,104,112,120},{128,136,144,152,1..., dimensions={0} | all-to-all | bytes 851968 | tf_op jit(solution)/shard_map/all_to_all | solution.py:32
  56.5 1.6 %shard_map.88 = f32[1280,128]{1,0:T(8,128)S(1)} custom-call(bf16[8,136,384]{2,1,0:T(8,128)(2,1)S(1)} %all-to-all-done.packed_ref, bf16[256,128]{1,0:T(8,128)(2,1)S(1)} %copy-done.1, bf16[96,1024]{1,0:T(8,128)(2,1)S(1)} %all_gather.6.rows_ref, bf16[8,104,256]{2,1,0:T(8,128)(2,1)S(1)} %all_to_all.30.met_ref), custom_call_target="tpu_custom_call" | custom-call | tf_op jit(solution)/shard_map/pallas_call | solution.py:195
  58.1 9.9 %all_to_all.31 = f32[2,160,4,128]{3,2,1,0:T(4,128)S(1)} all-to-all(f32[2,160,4,128]{3,2,1,0:T(4,128)S(1)} %bitcast.7), channel_id=1, replica_groups={{0,1},{2,3},{4,5},{6,7},{8,9},{10,11},{12,13},{14,15},{16,17},{18,19},{..., dimensions={0} | all-to-all | bytes 1310720 | tf_op jit(solution)/shard_map/all_to_all | solution.py:32
  68.0 0.2 reduce_sum.27
  68.3 17.5 %all_to_all.32 = f32[32,5,4,128]{3,2,1,0:T(4,128)S(1)} all-to-all(f32[32,5,4,128]{3,2,1,0:T(4,128)S(1)} %bitcast.9), channel_id=1, replica_groups={{0,2,4,6,8,10,12,14,16,18,20,22,24,26,28,30,32,34,36,38,40,42,44,46,48,..., dimensions={0} | all-to-all | bytes 655360 | tf_op jit(solution)/shard_map/all_to_all | solution.py:32
  85.7 0.1 reduce_sum.28
  85.8 13.1 %all_to_all.33 = f32[12,5,4,128]{3,2,1,0:T(4,128)S(1)} all-to-all(f32[12,5,4,128]{3,2,1,0:T(4,128)S(1)} %broadcast_in_dim.4), channel_id=1, replica_groups={{0,64,128,192,256,320,384,448,512,576,640,704},{8,72,136,200,264,328,39..., dimensions={0} | all-to-all | bytes 245760 | tf_op jit(solution)/shard_map/all_to_all | solution.py:32
  99.0 15.3 %all_to_all.34 = f32[32,5,4,128]{3,2,1,0:T(4,128)S(1)} all-to-all(f32[32,5,4,128]{3,2,1,0:T(4,128)S(1)} %broadcast_in_dim.5), channel_id=1, replica_groups={{0,2,4,6,8,10,12,14,16,18,20,22,24,26,28,30,32,34,36,38,40,42,44,46,48,..., dimensions={0} | all-to-all | bytes 655360 | tf_op jit(solution)/shard_map/all_to_all | solution.py:32
  114.3 6.5 %all_gather.7 = f32[320,4,128]{2,1,0:T(4,128)S(1)} all-gather(f32[160,4,128]{2,1,0:T(4,128)S(1)} %bitcast.10), channel_id=1, replica_groups={{0,1},{2,3},{4,5},{6,7},{8,9},{10,11},{12,13},{14,15},{16,17},{18,19},{..., dimensions={0}, use_global_device_ids=true | all-gather | bytes 983040 | tf_op jit(solution)/shard_map/all_gather | solution.py:49
  120.8 0.9 shard_map.89
  (3 shorter events, 0.1 us)
Async XLA Ops:
  2.7 14.1 %copy-start.2 = (bf16[8,1024]{1,0:T(8,128)(2,1)S(1)}, bf16[8,1024]{1,0:T(8,128)(2,1)}, u32[]{:S(2)}) copy-start(bf16[8,1024]{1,0:T(8,128)(2,1)} %param.11) | copy-start | bytes 49156
  2.7 34.7 %copy-start = (bf16[1024,128]{1,0:T(8,128)(2,1)S(1)}, bf16[1024,128]{1,0:T(8,128)(2,1)}, u32[]{:S(2)}) copy-start(bf16[1024,128]{1,0:T(8,128)(2,1)} %dim_weight_ref.3) | copy-start | bytes 786436
  2.7 34.7 %all-to-all-start = ((bf16[8,136,384]{2,1,0:T(8,128)(2,1)}), bf16[8,136,384]{2,1,0:T(8,128)(2,1)S(1)}, u32[]{:S(2)}, u32[]{:S(2)}) async-start(bf16[8,136,384]{2,1,0:T(8,128)(2,1)} %shard_map.86), calls=%async_computation | async-start | bytes 1671168 | tf_op jit(solution)/shard_map/all_to_all | solution.py:32
  16.8 20.6 %copy-start.1 = (bf16[256,128]{1,0:T(8,128)(2,1)S(1)}, bf16[256,128]{1,0:T(8,128)(2,1)}, u32[]{:S(2)}) copy-start(bf16[256,128]{1,0:T(8,128)(2,1)} %fact_weight_ref.1) | copy-start | bytes 196612

commit v7 on v6

--- a/solution.py
+++ b/solution.py
@@ -38,16 +38,17 @@
     return spread(jnp.broadcast_to(array[None], (copies, *array.shape)), axis, groups)
 
 
-def total_over_devices(terms, one_y, chip, plane):
-    rows, width = terms.shape
+def total_over_devices(kept, given, one_y, chip, plane):
+    rows, width = kept.shape
     both = ("fact", "key")
     members = len(plane[0])
-    part = spread(terms.reshape(2, -1, 4, width), "key", chip).sum(axis=0)
+    swap = [(a, b) for pair in chip for a, b in (pair, pair[::-1])]
+    part = kept + lax.ppermute(given, "key", swap)
     part = spread(part.reshape(members, -1, 4, width), both, plane).sum(axis=0)
     part = collect(part, "fact", len(one_y[0]), one_y).sum(axis=0)
     part = collect(part, both, members, plane).reshape(-1, 4, width)
     part = lax.all_gather(part, "key", axis=0, tiled=True, axis_index_groups=chip)
-    return part.reshape(rows, width)
+    return part.reshape(2 * rows, width)
 
 
 def pack_slots(
@@ -135,7 +136,7 @@
         out_ref[m, pl.ds(ring_keys, extra_rows), :] = digits.astype(bf16)
 
 
-def both_terms(packed_ref, weight_ref, rows_ref, met_ref, out_ref):
+def both_terms(packed_ref, weight_ref, rows_ref, met_ref, kept_ref, given_ref):
     members, _, two_widths = met_ref.shape
     out_width = two_widths // 2
     ring_keys = rows_ref.shape[0]
@@ -161,8 +162,6 @@
         live = jnp.concatenate([codes[:, b : b + 1] for b in pair], axis=0) >= 0
         residual = jnp.where(live, value + found, f32(0.0)).astype(bf16)
         fact_term += lax.dot_general(features, residual, contract, preferred_element_type=f32)
-    out_ref[pl.ds(0, width), :] = fact_term
-
     me = lax.rem(lax.axis_index("fact"), ring_size)
     sums = jnp.zeros((ring_keys, out_width), f32)
     digits = jnp.zeros((extra_rows, two_widths), f32)
@@ -178,7 +177,17 @@
     dim_term = lax.dot_general(
         rows_ref[...], jnp.concatenate([high, low], axis=1), contract, preferred_element_type=f32
     )
-    out_ref[pl.ds(width, rows_ref.shape[1]), :] = dim_term[:, :out_width] + dim_term[:, out_width:]
+    dim_term = dim_term[:, :out_width] + dim_term[:, out_width:]
+    half = kept_ref.shape[0]
+
+    def store(upper_ref, lower_ref):
+        upper_ref[pl.ds(0, width), :] = fact_term
+        upper_ref[pl.ds(width, half - width), :] = dim_term[: half - width]
+        lower_ref[...] = dim_term[half - width :]
+
+    core = lax.rem(lax.axis_index("key"), 2)
+    pl.when(core == 0)(lambda: store(kept_ref, given_ref))
+    pl.when(core == 1)(lambda: store(given_ref, kept_ref))
 
 
 def finish(row_scale, totals_ref, fact_weight_ref, dim_weight_ref, fact_ref, dim_ref):
@@ -191,12 +200,13 @@
     ] * row_scale + ridge_weight * dim_weight_ref[...].astype(f32)
 
 
-def kernel_call(body, out_shape, dtype, *operands):
+def kernel_call(body, shapes, dtype, *operands):
+    vmem = pl.BlockSpec(memory_space=pltpu.VMEM)
     return pl.pallas_call(
         body,
-        out_shape=jax.ShapeDtypeStruct(out_shape, dtype),
-        in_specs=[pl.BlockSpec(memory_space=pltpu.VMEM)] * len(operands),
-        out_specs=pl.BlockSpec(memory_space=pltpu.VMEM),
+        out_shape=tuple(jax.ShapeDtypeStruct(shape, dtype) for shape in shapes),
+        in_specs=[vmem] * len(operands),
+        out_specs=(vmem,) * len(shapes),
         compiler_params=pltpu.CompilerParams(vmem_limit_bytes=32 << 20),
     )(*operands)
 
@@ -234,9 +244,9 @@
     packed = spread(packed, "key")
     rows = lax.all_gather(dim_features, "fact", axis=0, tiled=True, axis_index_groups=one_y)
 
-    met = kernel_call(
+    (met,) = kernel_call(
         sum_by_key,
-        (ring_size, ring_keys + extra_rows, 2 * out_width),
+        ((ring_size, ring_keys + extra_rows, 2 * out_width),),
         bf16,
         packed,
         fact_weight,
@@ -244,11 +254,9 @@
         dim_weight,
     )
     met = spread(met, "fact", one_z)
-    terms = kernel_call(
-        both_terms, (fact_width + dim_width, out_width), f32, packed, fact_weight, rows, met
-    )
-
-    totals = total_over_devices(terms, one_y, chip, plane)
+    half = ((fact_width + dim_width) // 2, out_width)
+    kept, given = kernel_call(both_terms, (half, half), f32, packed, fact_weight, rows, met)
+    totals = total_over_devices(kept, given, one_y, chip, plane)
     total_rows = slot_count * fact_devices * key_devices
     row_scale = float(total_rows) ** (-0.5)
     vmem = pl.BlockSpec(memory_space=pltpu.VMEM)

time: 122 us -> 121 us (level)
  blocking collectives: 101 us -> 90.8 us
  starting transfers between devices: 14.1 us -> 22 us
  waiting for transfers between devices: 0.01 us -> 1.24 us
    all_to_all x5 -> x4, blocking collectives: 73.5 us -> 63.7 us  [spread(): lax.all_to_all(array, axis, split_axis=0, concat_axis=0, tiled=True, axis...]
    ppermute x0 -> x1, starting transfers between devices: none -> 7.88 us  [total_over_devices(): part = kept + lax.ppermute(given, 'key', swap)]
    ppermute x0 -> x1, waiting for transfers between devices: none -> 1.23 us  [total_over_devices(): part = kept + lax.ppermute(given, 'key', swap)]
  transfers between devices with their start and end apart: 1 -> 2, of which waited for: 0 -> 1; matrix products, arithmetic and copies ran while one was open for 0% -> 0% of each run, Pallas kernels for 0% -> 0%
where the time goes in v7:
time: 121 us
  blocking collectives  90.8 us (75%)
  starting transfers between devices  22 us (18%)
  Pallas kernels  5.82 us (5%)
  waiting for transfers between devices  1.24 us (1%)
    all_to_all x4, blocking collectives, spread(): lax.all_to_all(array, axis, split_axis=0, concat_axis=0, tiled=True, axis...  63.7 us
    all_gather x1, blocking collectives, on_device(): lax.all_gather(dim_features, 'fact', axis=0, tiled=True, axis_index_group...  20.6 us
    all_to_all x1, starting transfers between devices, spread(): lax.all_to_all(array, axis, split_axis=0, concat_axis=0, tiled=True, axis...  14.1 us
    ppermute x1, starting transfers between devices, total_over_devices(): part = kept + lax.ppermute(given, 'key', swap)  7.88 us
    all_gather x1, blocking collectives, total_over_devices(): lax.all_gather(part, 'key', axis=0, tiled=True, axis_index_groups=chip)  6.49 us
    pallas_call x2, Pallas kernels, kernel_call(): pl.pallas_call(body, out_shape=tuple((jax.ShapeDtypeStruct(shape, dtype)...  2.88 us
  transfers between devices with their start and end apart: 2, of which 1 were waited for; matrix products, arithmetic and copies ran while one was open for 0% of the time, Pallas kernels for 0%

profile of v7, /device:TPU:1, one launch (start us, length us, event | category | flops | bytes accessed | tf_op | source)
XLA Modules:
  0.0 120.7 jit_solution(10560438968394095837)
XLA Ops:
  0.6 2.1 %shard_map.86 = bf16[8,136,384]{2,1,0:T(8,128)(2,1)} custom-call(s32[8,128]{1,0:T(8,128)} %bitcast.11, s32[1,8]{1,0:T(1,128)} %fill_hbm.1, bf16[8,128,256]{2,1,0:T(8,128)(2,1)} %bitcast.9, bf16[8,128,128]{2,1,0:T(8,128)(2,1)} %bitcast.10), custom_call_target="tpu_custom_call" | custom-call | tf_op jit(solution)/shard_map/pallas_call | solution.py:226
  2.7 0.0 copy-start.2
  2.7 0.0 copy-start
  2.7 14.1 %all-to-all-start = ((bf16[8,136,384]{2,1,0:T(8,128)(2,1)}), bf16[8,136,384]{2,1,0:T(8,128)(2,1)S(1)}, u32[]{:S(2)}, u32[]{:S(2)}) async-start(bf16[8,136,384]{2,1,0:T(8,128)(2,1)} %shard_map.86), calls=%async_computation | async-start | bytes 1671168 | tf_op jit(solution)/shard_map/all_to_all | solution.py:32
  16.8 0.0 copy-done.2
  16.8 0.0 copy-start.1
  16.8 20.6 %all_gather.6.rows_ref = bf16[96,1024]{1,0:T(8,128)(2,1)S(1)} all-gather(bf16[8,1024]{1,0:T(8,128)(2,1)S(1)} %copy-done.2), channel_id=1, replica_groups={{0,64,128,192,256,320,384,448,512,576,640,704},{8,72,136,200,264,328,39..., dimensions={0}, use_global_device_ids=true | all-gather | bytes 212992 | tf_op jit(solution)/shard_map/all_gather | solution.py:245
  37.5 0.0 all-to-all-done.packed_ref
  37.5 0.0 copy-done
  37.5 0.0 copy-done.1
  37.5 1.2 %shard_map.87 = bf16[8,104,256]{2,1,0:T(8,128)(2,1)S(1)} custom-call(bf16[8,136,384]{2,1,0:T(8,128)(2,1)S(1)} %all-to-all-done.packed_ref, bf16[256,128]{1,0:T(8,128)(2,1)S(1)} %copy-done.1, bf16[96,1024]{1,0:T(8,128)(2,1)S(1)} %all_gather.6.rows_ref, bf16[1024,128]{1,0:T(8,128)(2,1)S(1)} %copy-done), custom_call_target="tpu_custom_call" | custom-call | tf_op jit(solution)/shard_map/pallas_call | solution.py:205
  38.7 17.8 %all_to_all.25.met_ref = bf16[8,104,256]{2,1,0:T(8,128)(2,1)S(1)} all-to-all(bf16[8,104,256]{2,1,0:T(8,128)(2,1)S(1)} %shard_map.87), channel_id=1, replica_groups={{0,8,16,24,32,40,48,56},{64,72,80,88,96,104,112,120},{128,136,144,152,1..., dimensions={0} | all-to-all | bytes 851968 | tf_op jit(solution)/shard_map/all_to_all | solution.py:32
  56.5 1.6 %shard_map.88 = (f32[640,128]{1,0:T(8,128)S(1)}, f32[640,128]{1,0:T(8,128)S(1)}) custom-call(bf16[8,136,384]{2,1,0:T(8,128)(2,1)S(1)} %all-to-all-done.packed_ref, bf16[256,128]{1,0:T(8,128)(2,1)S(1)} %copy-done.1, bf16[96,1024]{1,0:T(8,128)(2,1)S(1)} %all_gather.6.rows_ref, bf16[8,104,256]{2,1,0:T(8,128)(2,1)S(1)} %all_to_all.25.met_ref), custom_call_target="tpu_custom_call" | custom-call | tf_op jit(solution)/shard_map/pallas_call | solution.py:205
  58.2 7.9 %collective-permute-start = (f32[640,128]{1,0:T(8,128)S(1)}, f32[640,128]{1,0:T(8,128)S(1)}, u32[]{:S(2)}, u32[]{:S(2)}) collective-permute-start(f32[640,128]{1,0:T(8,128)S(1)} %get-tuple-element.5), channel_id=1, source_target_pairs={{0,1},{1,0},{2,3},{3,2},{4,5},{5,4},{6,7},{7,6},{8,9},{9,8},{10,11... | collective-permute-start | bytes 983048 | tf_op jit(solution)/shard_map/ppermute | solution.py:46
  66.1 1.2 %collective-permute-done = f32[640,128]{1,0:T(8,128)S(1)} collective-permute-done((f32[640,128]{1,0:T(8,128)S(1)}, f32[640,128]{1,0:T(8,128)S(1)}, u32[]{:S(2)}, u32[]{:S(2)}) %collective-permute-start) | collective-permute-done | bytes 327712 | tf_op jit(solution)/shard_map/ppermute | solution.py:46
  67.3 17.5 %all_to_all.26 = f32[32,5,4,128]{3,2,1,0:T(4,128)S(1)} all-to-all(f32[32,5,4,128]{3,2,1,0:T(4,128)S(1)} %bitcast.7), channel_id=1, replica_groups={{0,2,4,6,8,10,12,14,16,18,20,22,24,26,28,30,32,34,36,38,40,42,44,46,48,..., dimensions={0} | all-to-all | bytes 655360 | tf_op jit(solution)/shard_map/all_to_all | solution.py:32
  84.8 0.1 reduce_sum.18
  84.9 13.1 %all_to_all.27 = f32[12,5,4,128]{3,2,1,0:T(4,128)S(1)} all-to-all(f32[12,5,4,128]{3,2,1,0:T(4,128)S(1)} %broadcast_in_dim.4), channel_id=1, replica_groups={{0,64,128,192,256,320,384,448,512,576,640,704},{8,72,136,200,264,328,39..., dimensions={0} | all-to-all | bytes 245760 | tf_op jit(solution)/shard_map/all_to_all | solution.py:32
  98.0 15.3 %all_to_all.28 = f32[32,5,4,128]{3,2,1,0:T(4,128)S(1)} all-to-all(f32[32,5,4,128]{3,2,1,0:T(4,128)S(1)} %broadcast_in_dim.5), channel_id=1, replica_groups={{0,2,4,6,8,10,12,14,16,18,20,22,24,26,28,30,32,34,36,38,40,42,44,46,48,..., dimensions={0} | all-to-all | bytes 655360 | tf_op jit(solution)/shard_map/all_to_all | solution.py:32
  113.4 6.5 %all_gather.7 = f32[320,4,128]{2,1,0:T(4,128)S(1)} all-gather(f32[160,4,128]{2,1,0:T(4,128)S(1)} %bitcast.8), channel_id=1, replica_groups={{0,1},{2,3},{4,5},{6,7},{8,9},{10,11},{12,13},{14,15},{16,17},{18,19},{..., dimensions={0}, use_global_device_ids=true | all-gather | bytes 983040 | tf_op jit(solution)/shard_map/all_gather | solution.py:50
  119.8 0.9 shard_map.89
  (4 shorter events, 0.1 us)
Async XLA Ops:
  2.7 14.1 %copy-start.2 = (bf16[8,1024]{1,0:T(8,128)(2,1)S(1)}, bf16[8,1024]{1,0:T(8,128)(2,1)}, u32[]{:S(2)}) copy-start(bf16[8,1024]{1,0:T(8,128)(2,1)} %param.11) | copy-start | bytes 49156
  2.7 34.7 %copy-start = (bf16[1024,128]{1,0:T(8,128)(2,1)S(1)}, bf16[1024,128]{1,0:T(8,128)(2,1)}, u32[]{:S(2)}) copy-start(bf16[1024,128]{1,0:T(8,128)(2,1)} %dim_weight_ref.3) | copy-start | bytes 786436
  2.7 34.7 %all-to-all-start = ((bf16[8,136,384]{2,1,0:T(8,128)(2,1)}), bf16[8,136,384]{2,1,0:T(8,128)(2,1)S(1)}, u32[]{:S(2)}, u32[]{:S(2)}) async-start(bf16[8,136,384]{2,1,0:T(8,128)(2,1)} %shard_map.86), calls=%async_computation | async-start | bytes 1671168 | tf_op jit(solution)/shard_map/all_to_all | solution.py:32
  16.8 20.6 %copy-start.1 = (bf16[256,128]{1,0:T(8,128)(2,1)S(1)}, bf16[256,128]{1,0:T(8,128)(2,1)}, u32[]{:S(2)}) copy-start(bf16[256,128]{1,0:T(8,128)(2,1)} %fact_weight_ref.1) | copy-start | bytes 196612
  58.2 9.1 %collective-permute-start = (f32[640,128]{1,0:T(8,128)S(1)}, f32[640,128]{1,0:T(8,128)S(1)}, u32[]{:S(2)}, u32[]{:S(2)}) collective-permute-start(f32[640,128]{1,0:T(8,128)S(1)} %get-tuple-element.5), channel_id=1, source_target_pairs={{0,1},{1,0},{2,3},{3,2},{4,5},{5,4},{6,7},{7,6},{8,9},{9,8},{10,11... | collective-permute-start | bytes 983048 | tf_op jit(solution)/shard_map/ppermute | solution.py:46

commit v8 on v7

--- a/solution.py
+++ b/solution.py
@@ -52,21 +52,34 @@
 
 
 def pack_slots(
-    own_keys, ring_keys, keys_hbm, fill_hbm, features_hbm, targets_hbm, out_ref, keys_ref, fill_ref, done
+    own_keys, ring_keys, keys_hbm, fill_hbm, features_hbm, targets_hbm, out_hbm, keys_ref, fill_ref, slots_ref, done
 ):
     buckets, bucket_rows, width = features_hbm.shape
     out_width = targets_hbm.shape[2]
     slots = pl.ds(0, bucket_rows)
-    copies = [
-        pltpu.make_async_copy(keys_hbm, keys_ref, done.at[0]),
-        pltpu.make_async_copy(fill_hbm, fill_ref, done.at[1]),
-        pltpu.make_async_copy(features_hbm, out_ref.at[:, slots, pl.ds(0, width)], done.at[2]),
-        pltpu.make_async_copy(targets_hbm, out_ref.at[:, slots, pl.ds(width, out_width)], done.at[3]),
-    ]
-    for copy in copies:
-        copy.start()
-    copies[0].wait()
-    copies[1].wait()
+    groups = range(buckets // 2)
+
+    def copies(g):
+        two = pl.ds(2 * g, 2)
+        return (
+            pltpu.make_async_copy(
+                features_hbm.at[two], slots_ref.at[two, slots, pl.ds(0, width)], done.at[g, 0]
+            ),
+            pltpu.make_async_copy(
+                targets_hbm.at[two], slots_ref.at[two, slots, pl.ds(width, out_width)], done.at[g, 1]
+            ),
+            pltpu.make_async_copy(slots_ref.at[two], out_hbm.at[two], done.at[g, 2]),
+        )
+
+    keys_in = pltpu.make_async_copy(keys_hbm, keys_ref, done.at[len(groups), 0])
+    fill_in = pltpu.make_async_copy(fill_hbm, fill_ref, done.at[len(groups), 1])
+    keys_in.start()
+    fill_in.start()
+    for g in groups:
+        for copy in copies(g)[:2]:
+            copy.start()
+    keys_in.wait()
+    fill_in.wait()
     keys = keys_ref[...]
     owner = keys // (own_keys * buckets)
     places = (owner % ring_size) * ring_keys + (owner // ring_size) * own_keys + keys % own_keys
@@ -77,9 +90,14 @@
         low = codes - high * digit
         digits = jnp.concatenate([high, low, jnp.zeros_like(high)], axis=1).astype(f32)
         digits = jnp.broadcast_to(digits, (extra_rows, width + out_width))
-        out_ref[b, pl.ds(bucket_rows, extra_rows), :] = digits.astype(bf16)
-    for copy in copies[2:]:
-        copy.wait()
+        slots_ref[b, pl.ds(bucket_rows, extra_rows), :] = digits.astype(bf16)
+    for g in groups:
+        features_in, targets_in, out = copies(g)
+        features_in.wait()
+        targets_in.wait()
+        out.start()
+    for g in groups:
+        copies(g)[2].wait()
 
 
 def codes_of(packed_ref, b):
@@ -229,11 +247,12 @@
             (key_devices, bucket_rows + extra_rows, fact_width + out_width), bf16
         ),
         in_specs=[pl.BlockSpec(memory_space=pl.ANY)] * 4,
-        out_specs=pl.BlockSpec(memory_space=pltpu.VMEM),
+        out_specs=pl.BlockSpec(memory_space=pl.ANY),
         scratch_shapes=[
             pltpu.VMEM((key_devices, bucket_rows), i32),
             pltpu.SMEM((1, key_devices), i32),
-            pltpu.SemaphoreType.DMA((4,)),
+            pltpu.VMEM((key_devices, bucket_rows + extra_rows, fact_width + out_width), bf16),
+            pltpu.SemaphoreType.DMA((key_devices // 2 + 1, 3)),
         ],
     )(
         fact_keys.reshape(key_devices, bucket_rows),

time: 121 us -> 121 us (level)
  no operation moved by 1% of the time
where the time goes in v8:
time: 121 us
  blocking collectives  90.8 us (75%)
  starting transfers between devices  22 us (18%)
  Pallas kernels  5.77 us (5%)
  waiting for transfers between devices  1.24 us (1%)
    all_to_all x4, blocking collectives, spread(): lax.all_to_all(array, axis, split_axis=0, concat_axis=0, tiled=True, axis...  63.7 us
    all_gather x1, blocking collectives, on_device(): lax.all_gather(dim_features, 'fact', axis=0, tiled=True, axis_index_group...  20.6 us
    all_to_all x1, starting transfers between devices, spread(): lax.all_to_all(array, axis, split_axis=0, concat_axis=0, tiled=True, axis...  14.1 us
    ppermute x1, starting transfers between devices, total_over_devices(): part = kept + lax.ppermute(given, 'key', swap)  7.87 us
    all_gather x1, blocking collectives, total_over_devices(): lax.all_gather(part, 'key', axis=0, tiled=True, axis_index_groups=chip)  6.49 us
    pallas_call x2, Pallas kernels, kernel_call(): pl.pallas_call(body, out_shape=tuple((jax.ShapeDtypeStruct(shape, dtype)...  2.88 us
  transfers between devices with their start and end apart: 2, of which 1 were waited for; matrix products, arithmetic and copies ran while one was open for 0% of the time, Pallas kernels for 0%

profile of v8, /device:TPU:1, one launch (start us, length us, event | category | flops | bytes accessed | tf_op | source)
XLA Modules:
  0.0 120.7 jit_solution(9343219757387361084)
XLA Ops:
  0.6 2.0 %shard_map.86 = bf16[8,136,384]{2,1,0:T(8,128)(2,1)} custom-call(s32[8,128]{1,0:T(8,128)} %bitcast.11, s32[1,8]{1,0:T(1,128)} %fill_hbm.1, bf16[8,128,256]{2,1,0:T(8,128)(2,1)} %bitcast.9, bf16[8,128,128]{2,1,0:T(8,128)(2,1)} %bitcast.10), custom_call_target="tpu_custom_call" | custom-call | tf_op jit(solution)/shard_map/pallas_call | solution.py:244
  2.7 0.0 copy-start.2
  2.7 0.0 copy-start
  2.7 14.1 %all-to-all-start = ((bf16[8,136,384]{2,1,0:T(8,128)(2,1)}), bf16[8,136,384]{2,1,0:T(8,128)(2,1)S(1)}, u32[]{:S(2)}, u32[]{:S(2)}) async-start(bf16[8,136,384]{2,1,0:T(8,128)(2,1)} %shard_map.86), calls=%async_computation | async-start | bytes 1671168 | tf_op jit(solution)/shard_map/all_to_all | solution.py:32
  16.8 0.0 copy-done.2
  16.8 0.0 copy-start.1
  16.8 20.6 %all_gather.6.rows_ref = bf16[96,1024]{1,0:T(8,128)(2,1)S(1)} all-gather(bf16[8,1024]{1,0:T(8,128)(2,1)S(1)} %copy-done.2), channel_id=1, replica_groups={{0,64,128,192,256,320,384,448,512,576,640,704},{8,72,136,200,264,328,39..., dimensions={0}, use_global_device_ids=true | all-gather | bytes 212992 | tf_op jit(solution)/shard_map/all_gather | solution.py:264
  37.4 0.0 all-to-all-done.packed_ref
  37.4 0.0 copy-done
  37.4 0.0 copy-done.1
  37.4 1.2 %shard_map.87 = bf16[8,104,256]{2,1,0:T(8,128)(2,1)S(1)} custom-call(bf16[8,136,384]{2,1,0:T(8,128)(2,1)S(1)} %all-to-all-done.packed_ref, bf16[256,128]{1,0:T(8,128)(2,1)S(1)} %copy-done.1, bf16[96,1024]{1,0:T(8,128)(2,1)S(1)} %all_gather.6.rows_ref, bf16[1024,128]{1,0:T(8,128)(2,1)S(1)} %copy-done), custom_call_target="tpu_custom_call" | custom-call | tf_op jit(solution)/shard_map/pallas_call | solution.py:223
  38.7 17.8 %all_to_all.25.met_ref = bf16[8,104,256]{2,1,0:T(8,128)(2,1)S(1)} all-to-all(bf16[8,104,256]{2,1,0:T(8,128)(2,1)S(1)} %shard_map.87), channel_id=1, replica_groups={{0,8,16,24,32,40,48,56},{64,72,80,88,96,104,112,120},{128,136,144,152,1..., dimensions={0} | all-to-all | bytes 851968 | tf_op jit(solution)/shard_map/all_to_all | solution.py:32
  56.5 1.6 %shard_map.88 = (f32[640,128]{1,0:T(8,128)S(1)}, f32[640,128]{1,0:T(8,128)S(1)}) custom-call(bf16[8,136,384]{2,1,0:T(8,128)(2,1)S(1)} %all-to-all-done.packed_ref, bf16[256,128]{1,0:T(8,128)(2,1)S(1)} %copy-done.1, bf16[96,1024]{1,0:T(8,128)(2,1)S(1)} %all_gather.6.rows_ref, bf16[8,104,256]{2,1,0:T(8,128)(2,1)S(1)} %all_to_all.25.met_ref), custom_call_target="tpu_custom_call" | custom-call | tf_op jit(solution)/shard_map/pallas_call | solution.py:223
  58.1 7.9 %collective-permute-start = (f32[640,128]{1,0:T(8,128)S(1)}, f32[640,128]{1,0:T(8,128)S(1)}, u32[]{:S(2)}, u32[]{:S(2)}) collective-permute-start(f32[640,128]{1,0:T(8,128)S(1)} %get-tuple-element.5), channel_id=1, source_target_pairs={{0,1},{1,0},{2,3},{3,2},{4,5},{5,4},{6,7},{7,6},{8,9},{9,8},{10,11... | collective-permute-start | bytes 983048 | tf_op jit(solution)/shard_map/ppermute | solution.py:46
  66.0 1.2 %collective-permute-done = f32[640,128]{1,0:T(8,128)S(1)} collective-permute-done((f32[640,128]{1,0:T(8,128)S(1)}, f32[640,128]{1,0:T(8,128)S(1)}, u32[]{:S(2)}, u32[]{:S(2)}) %collective-permute-start) | collective-permute-done | bytes 327712 | tf_op jit(solution)/shard_map/ppermute | solution.py:46
  67.3 17.5 %all_to_all.26 = f32[32,5,4,128]{3,2,1,0:T(4,128)S(1)} all-to-all(f32[32,5,4,128]{3,2,1,0:T(4,128)S(1)} %bitcast.7), channel_id=1, replica_groups={{0,2,4,6,8,10,12,14,16,18,20,22,24,26,28,30,32,34,36,38,40,42,44,46,48,..., dimensions={0} | all-to-all | bytes 655360 | tf_op jit(solution)/shard_map/all_to_all | solution.py:32
  84.8 0.1 reduce_sum.18
  84.8 13.1 %all_to_all.27 = f32[12,5,4,128]{3,2,1,0:T(4,128)S(1)} all-to-all(f32[12,5,4,128]{3,2,1,0:T(4,128)S(1)} %broadcast_in_dim.4), channel_id=1, replica_groups={{0,64,128,192,256,320,384,448,512,576,640,704},{8,72,136,200,264,328,39..., dimensions={0} | all-to-all | bytes 245760 | tf_op jit(solution)/shard_map/all_to_all | solution.py:32
  98.0 15.3 %all_to_all.28 = f32[32,5,4,128]{3,2,1,0:T(4,128)S(1)} all-to-all(f32[32,5,4,128]{3,2,1,0:T(4,128)S(1)} %broadcast_in_dim.5), channel_id=1, replica_groups={{0,2,4,6,8,10,12,14,16,18,20,22,24,26,28,30,32,34,36,38,40,42,44,46,48,..., dimensions={0} | all-to-all | bytes 655360 | tf_op jit(solution)/shard_map/all_to_all | solution.py:32
  113.3 6.5 %all_gather.7 = f32[320,4,128]{2,1,0:T(4,128)S(1)} all-gather(f32[160,4,128]{2,1,0:T(4,128)S(1)} %bitcast.8), channel_id=1, replica_groups={{0,1},{2,3},{4,5},{6,7},{8,9},{10,11},{12,13},{14,15},{16,17},{18,19},{..., dimensions={0}, use_global_device_ids=true | all-gather | bytes 983040 | tf_op jit(solution)/shard_map/all_gather | solution.py:50
  119.8 0.9 shard_map.89
  (4 shorter events, 0.1 us)
Async XLA Ops:
  2.7 14.1 %copy-start.2 = (bf16[8,1024]{1,0:T(8,128)(2,1)S(1)}, bf16[8,1024]{1,0:T(8,128)(2,1)}, u32[]{:S(2)}) copy-start(bf16[8,1024]{1,0:T(8,128)(2,1)} %param.11) | copy-start | bytes 49156
  2.7 34.7 %copy-start = (bf16[1024,128]{1,0:T(8,128)(2,1)S(1)}, bf16[1024,128]{1,0:T(8,128)(2,1)}, u32[]{:S(2)}) copy-start(bf16[1024,128]{1,0:T(8,128)(2,1)} %dim_weight_ref.3) | copy-start | bytes 786436
  2.7 34.7 %all-to-all-start = ((bf16[8,136,384]{2,1,0:T(8,128)(2,1)}), bf16[8,136,384]{2,1,0:T(8,128)(2,1)S(1)}, u32[]{:S(2)}, u32[]{:S(2)}) async-start(bf16[8,136,384]{2,1,0:T(8,128)(2,1)} %shard_map.86), calls=%async_computation | async-start | bytes 1671168 | tf_op jit(solution)/shard_map/all_to_all | solution.py:32
  16.8 20.6 %copy-start.1 = (bf16[256,128]{1,0:T(8,128)(2,1)S(1)}, bf16[256,128]{1,0:T(8,128)(2,1)}, u32[]{:S(2)}) copy-start(bf16[256,128]{1,0:T(8,128)(2,1)} %fact_weight_ref.1) | copy-start | bytes 196612
  58.1 9.1 %collective-permute-start = (f32[640,128]{1,0:T(8,128)S(1)}, f32[640,128]{1,0:T(8,128)S(1)}, u32[]{:S(2)}, u32[]{:S(2)}) collective-permute-start(f32[640,128]{1,0:T(8,128)S(1)} %get-tuple-element.5), channel_id=1, source_target_pairs={{0,1},{1,0},{2,3},{3,2},{4,5},{5,4},{6,7},{7,6},{8,9},{9,8},{10,11... | collective-permute-start | bytes 983048 | tf_op jit(solution)/shard_map/ppermute | solution.py:46

commit v9 on v8

--- a/solution.py
+++ b/solution.py
@@ -19,13 +19,15 @@
     chips, cores = range(key_devices // 2), range(2)
     one_z = [[z * ring_size + y for y in range(ring_size)] for z in levels]
     one_y = [[z * ring_size + y for z in levels] for y in range(ring_size)]
+    near = [line[i : i + 3] for line in one_y for i in range(0, len(line), 3)]
+    far = [line[i::3] for line in one_y for i in range(3)]
     chip = [[2 * x + core for core in cores] for x in chips]
     plane = [
         [(z * ring_size + y) * key_devices + 2 * x + core for y in range(ring_size) for x in chips]
         for z in levels
         for core in cores
     ]
-    return one_z, one_y, chip, plane
+    return one_z, one_y, near, far, chip, plane
 
 
 def spread(array, axis, groups=None):
@@ -75,9 +77,10 @@
     fill_in = pltpu.make_async_copy(fill_hbm, fill_ref, done.at[len(groups), 1])
     keys_in.start()
     fill_in.start()
-    for g in groups:
-        for copy in copies(g)[:2]:
-            copy.start()
+    plan = [copies(g) for g in groups]
+    for features_in, targets_in, _ in plan:
+        features_in.start()
+        targets_in.start()
     keys_in.wait()
     fill_in.wait()
     keys = keys_ref[...]
@@ -91,13 +94,12 @@
         digits = jnp.concatenate([high, low, jnp.zeros_like(high)], axis=1).astype(f32)
         digits = jnp.broadcast_to(digits, (extra_rows, width + out_width))
         slots_ref[b, pl.ds(bucket_rows, extra_rows), :] = digits.astype(bf16)
-    for g in groups:
-        features_in, targets_in, out = copies(g)
+    for features_in, targets_in, out in plan:
         features_in.wait()
         targets_in.wait()
         out.start()
-    for g in groups:
-        copies(g)[2].wait()
+    for _, _, out in plan:
+        out.wait()
 
 
 def codes_of(packed_ref, b):
@@ -126,75 +128,80 @@
     )
 
 
-def sum_by_key(packed_ref, weight_ref, rows_ref, dim_weight_ref, out_ref):
-    members, _, two_widths = out_ref.shape
-    out_width = two_widths // 2
-    ring_keys = rows_ref.shape[0]
-    two_rows = 2 * (packed_ref.shape[1] - extra_rows)
-    places = lax.broadcasted_iota(i32, (members * ring_keys, two_rows), 0)
-    ones = jnp.ones((two_rows, out_width), bf16)
-    sums = jnp.zeros((members * ring_keys, two_widths), f32)
+def split(value):
+    high = value.astype(bf16)
+    return high, (value - high.astype(f32)).astype(bf16)
+
+
+contract = (((0,), (0,)), ((), ()))
+
+
+def own_term(packed_ref, weight_ref, out_ref):
+    out_width = weight_ref.shape[1]
+    codes = [codes_of(packed_ref, b) for b in range(packed_ref.shape[0])]
+    codes = jnp.transpose(jnp.concatenate(codes, axis=0).astype(f32))
+    total = jnp.zeros((weight_ref.shape[0], 2 * out_width), f32)
+    for pair in pairs_of(packed_ref):
+        features, value = partial_of(packed_ref, weight_ref, pair)
+        live = jnp.concatenate([codes[:, b : b + 1] for b in pair], axis=0) >= 0.0
+        value = jnp.concatenate(split(jnp.where(live, value, f32(0.0))), axis=1)
+        total += lax.dot_general(features, value, contract, preferred_element_type=f32)
+    out_ref[...] = total[:, :out_width] + total[:, out_width:]
+
+
+def sum_by_key(packed_ref, rows_ref, own_ref, out_ref, rows_out_ref, own_out_ref):
+    members, _, width = out_ref.shape
+    ring_keys = out_ref.shape[1] - extra_rows
+    bucket_rows = packed_ref.shape[1] - extra_rows
+    slots = pl.ds(0, bucket_rows)
+    places = lax.broadcasted_iota(i32, (members * ring_keys, 2 * bucket_rows), 0)
+    ones = jnp.ones((2 * bucket_rows, 128), bf16)
+    sums = jnp.zeros((members * ring_keys, width + 128), f32)
     for pair in pairs_of(packed_ref):
         codes = jnp.concatenate([codes_of(packed_ref, b) for b in pair], axis=1)
         one_hot = jnp.where(places == codes, f32(1.0), f32(0.0)).astype(bf16)
-        _, value = partial_of(packed_ref, weight_ref, pair)
-        value = jnp.concatenate([value.astype(bf16), ones], axis=1)
+        value = jnp.concatenate([packed_ref[b, slots, :] for b in pair], axis=0)
+        value = jnp.concatenate([value, ones], axis=1)
         sums += jnp.dot(one_hot, value, preferred_element_type=f32)
-    values = jnp.dot(rows_ref[...], dim_weight_ref[...], preferred_element_type=f32).astype(bf16)
-    diagonal = diagonal_of(ring_keys, out_width)
-    own = pl.ds(0, ring_keys)
+    diagonal = diagonal_of(ring_keys, 128)
     for m in range(members):
         part = sums[m * ring_keys : (m + 1) * ring_keys]
-        out_ref[m, own, pl.ds(0, out_width)] = part[:, :out_width].astype(bf16)
-        out_ref[m, own, pl.ds(out_width, out_width)] = values
-        counts = jnp.where(diagonal, part[:, out_width:], f32(0.0)).sum(axis=0, keepdims=True)
+        out_ref[m, pl.ds(0, ring_keys), :] = part[:, :width].astype(bf16)
+        counts = jnp.where(diagonal, part[:, width:], f32(0.0)).sum(axis=0, keepdims=True)
         high = jnp.floor(counts * (1.0 / digit))
-        digits = jnp.concatenate([high, counts - high * digit], axis=1)
-        digits = jnp.broadcast_to(digits, (extra_rows, two_widths))
-        out_ref[m, pl.ds(ring_keys, extra_rows), :] = digits.astype(bf16)
-
-
-def both_terms(packed_ref, weight_ref, rows_ref, met_ref, kept_ref, given_ref):
-    members, _, two_widths = met_ref.shape
-    out_width = two_widths // 2
-    ring_keys = rows_ref.shape[0]
-    buckets = packed_ref.shape[0]
-    bucket_rows = packed_ref.shape[1] - extra_rows
-    width = weight_ref.shape[0]
-    contract = (((0,), (0,)), ((), ()))
-
-    own = pl.ds(0, ring_keys)
-    values = jnp.concatenate(
-        [met_ref[m, own, pl.ds(out_width, out_width)] for m in range(members)], axis=0
-    )
-    codes = jnp.concatenate([codes_of(packed_ref, b) for b in range(buckets)], axis=0)
-    codes = jnp.transpose(codes.astype(f32)).astype(i32)
-    places = lax.broadcasted_iota(i32, (bucket_rows, members * ring_keys), 1)
-    fact_term = jnp.zeros((width, out_width), f32)
-    for pair in pairs_of(packed_ref):
-        one_hot = [
-            jnp.where(places == codes[:, b : b + 1], f32(1.0), f32(0.0)).astype(bf16) for b in pair
-        ]
-        features, value = partial_of(packed_ref, weight_ref, pair)
-        found = jnp.dot(jnp.concatenate(one_hot, axis=0), values, preferred_element_type=f32)
-        live = jnp.concatenate([codes[:, b : b + 1] for b in pair], axis=0) >= 0
-        residual = jnp.where(live, value + found, f32(0.0)).astype(bf16)
-        fact_term += lax.dot_general(features, residual, contract, preferred_element_type=f32)
-    me = lax.rem(lax.axis_index("fact"), ring_size)
-    sums = jnp.zeros((ring_keys, out_width), f32)
-    digits = jnp.zeros((extra_rows, two_widths), f32)
+        rest = jnp.zeros((1, width - 256), f32)
+        digits = jnp.concatenate([high, counts - high * digit, rest], axis=1)
+        out_ref[m, pl.ds(ring_keys, extra_rows), :] = jnp.broadcast_to(
+            digits, (extra_rows, width)
+        ).astype(bf16)
+    rows_out_ref[...] = rows_ref[...]
+    own_out_ref[...] = own_ref[...]
+
+
+def both_terms(own_ref, weight_ref, rows_ref, dim_weight_ref, met_ref, kept_ref, given_ref):
+    members = met_ref.shape[0]
+    ring_keys, dim_width = rows_ref.shape
+    width, out_width = weight_ref.shape
+    keys = pl.ds(0, ring_keys)
+    rows = rows_ref[...]
+    values = jnp.dot(rows, dim_weight_ref[...], preferred_element_type=f32).astype(bf16)
+    met = jnp.zeros((ring_keys, width + out_width), f32)
+    digits = jnp.zeros((extra_rows, width + out_width), f32)
     for m in range(members):
-        sums += met_ref[m, own, pl.ds(0, out_width)].astype(f32)
+        met += met_ref[m, keys, :].astype(f32)
         digits += met_ref[m, pl.ds(ring_keys, extra_rows), :].astype(f32)
-    counts = digits[:1, :out_width] * digit + digits[:1, out_width:]
-    diagonal = diagonal_of(ring_keys, out_width)
+    counts = digits[:1, :128] * digit + digits[:1, 128:256]
+    diagonal = diagonal_of(ring_keys, 128)
     counts = jnp.sum(jnp.where(diagonal, counts, f32(0.0)), axis=1, keepdims=True)
-    sums += counts * met_ref[me, own, pl.ds(out_width, out_width)].astype(f32)
-    high = sums.astype(bf16)
-    low = (sums - high.astype(f32)).astype(bf16)
-    dim_term = lax.dot_general(
-        rows_ref[...], jnp.concatenate([high, low], axis=1), contract, preferred_element_type=f32
-    )
+    high, low = split(met[:, :width])
+    sums = jnp.dot(high, weight_ref[...], preferred_element_type=f32)
+    sums += jnp.dot(low, weight_ref[...], preferred_element_type=f32)
+    sums += counts * values.astype(f32) - met[:, width:]
+    fact_term = own_ref[...]
+    fact_term += lax.dot_general(high, values, contract, preferred_element_type=f32)
+    fact_term += lax.dot_general(low, values, contract, preferred_element_type=f32)
+    sums = jnp.concatenate(split(sums), axis=1)
+    dim_term = lax.dot_general(rows, sums, contract, preferred_element_type=f32)
     dim_term = dim_term[:, :out_width] + dim_term[:, out_width:]
     half = kept_ref.shape[0]
 
@@ -218,13 +225,13 @@
     ] * row_scale + ridge_weight * dim_weight_ref[...].astype(f32)
 
 
-def kernel_call(body, shapes, dtype, *operands):
+def kernel_call(body, outs, *operands):
     vmem = pl.BlockSpec(memory_space=pltpu.VMEM)
     return pl.pallas_call(
         body,
-        out_shape=tuple(jax.ShapeDtypeStruct(shape, dtype) for shape in shapes),
+        out_shape=tuple(jax.ShapeDtypeStruct(shape, dtype) for shape, dtype in outs),
         in_specs=[vmem] * len(operands),
-        out_specs=(vmem,) * len(shapes),
+        out_specs=(vmem,) * len(outs),
         compiler_params=pltpu.CompilerParams(vmem_limit_bytes=32 << 20),
     )(*operands)
 
@@ -234,7 +241,7 @@
 ):
     key_devices = lax.axis_size("key")
     fact_devices = lax.axis_size("fact")
-    one_z, one_y, chip, plane = groups_of(fact_devices, key_devices)
+    one_z, one_y, near, far, chip, plane = groups_of(fact_devices, key_devices)
     slot_count = fact_keys.shape[0]
     bucket_rows = slot_count // key_devices
     own_keys, dim_width = dim_features.shape
@@ -260,21 +267,17 @@
         fact_features.reshape(key_devices, bucket_rows, fact_width),
         targets.reshape(key_devices, bucket_rows, out_width),
     )
-    packed = spread(packed, "key")
-    rows = lax.all_gather(dim_features, "fact", axis=0, tiled=True, axis_index_groups=one_y)
-
-    (met,) = kernel_call(
-        sum_by_key,
-        ((ring_size, ring_keys + extra_rows, 2 * out_width),),
-        bf16,
-        packed,
-        fact_weight,
-        rows,
-        dim_weight,
-    )
+    slots = spread(packed, "key")
+    rows = lax.all_gather(dim_features, "fact", axis=0, tiled=True, axis_index_groups=near)
+    (own,) = kernel_call(own_term, (((fact_width, out_width), f32),), packed, fact_weight)
+
+    block = (ring_size, ring_keys + extra_rows, fact_width + out_width)
+    outs = ((block, bf16), (rows.shape, bf16), (own.shape, f32))
+    met, rows, own = kernel_call(sum_by_key, outs, slots, rows, own)
     met = spread(met, "fact", one_z)
-    half = ((fact_width + dim_width) // 2, out_width)
-    kept, given = kernel_call(both_terms, (half, half), f32, packed, fact_weight, rows, met)
+    rows = lax.all_gather(rows, "fact", axis=0, tiled=True, axis_index_groups=far)
+    half = (((fact_width + dim_width) // 2, out_width), f32)
+    kept, given = kernel_call(both_terms, (half, half), own, fact_weight, rows, dim_weight, met)
     totals = total_over_devices(kept, given, one_y, chip, plane)
     total_rows = slot_count * fact_devices * key_devices
     row_scale = float(total_rows) ** (-0.5)

time: 121 us -> 122 us (level)
  waiting for transfers between devices: 1.24 us -> 9.5 us
  blocking collectives: 90.8 us -> 84.4 us
  starting transfers between devices: 22 us -> 20.4 us
    all_gather x0 -> x1, blocking collectives: none -> 18 us  [on_device(): lax.all_gather(rows, 'fact', axis=0, tiled=True, axis_index_groups=far)]
    all_gather x1, blocking collectives: 20.6 us -> 5.98 us  [on_device(): lax.all_gather(dim_features, 'fact', axis=0, tiled=True, axis_index_group...]
    all_to_all x4 -> x3, blocking collectives: 63.7 us -> 53.9 us  [spread(): lax.all_to_all(array, axis, split_axis=0, concat_axis=0, tiled=True, axis...]
    all_to_all x1 -> x2, waiting for transfers between devices: 0.01 us -> 8.27 us  [spread(): lax.all_to_all(array, axis, split_axis=0, concat_axis=0, tiled=True, axis...]
    ppermute x1, starting transfers between devices: 7.87 us -> 2.61 us  [total_over_devices(): part = kept + lax.ppermute(given, 'key', swap)]
    all_to_all x1 -> x2, starting transfers between devices: 14.1 us -> 17.8 us  [spread(): lax.all_to_all(array, axis, split_axis=0, concat_axis=0, tiled=True, axis...]
    pallas_call x2 -> x3, Pallas kernels: 2.88 us -> 3.26 us  [kernel_call(): pl.pallas_call(body, out_shape=tuple((jax.ShapeDtypeStruct(shape, dtype)...]
  transfers between devices with their start and end apart: 2 -> 3, of which waited for: 1 -> 3; matrix products, arithmetic and copies ran while one was open for 0% -> 0% of each run, Pallas kernels for 0% -> 1%
where the time goes in v9:
time: 122 us; the launch traced here: 121 us
  blocking collectives  84.4 us (69%)
  starting transfers between devices  20.4 us (17%)
  waiting for transfers between devices  9.5 us (8%)
  Pallas kernels  6.16 us (5%)
    all_to_all x3, blocking collectives, spread(): lax.all_to_all(array, axis, split_axis=0, concat_axis=0, tiled=True, axis...  53.9 us
    all_gather x1, blocking collectives, on_device(): lax.all_gather(rows, 'fact', axis=0, tiled=True, axis_index_groups=far)  18 us
    all_to_all x2, starting transfers between devices, spread(): lax.all_to_all(array, axis, split_axis=0, concat_axis=0, tiled=True, axis...  17.8 us
    all_to_all x2, waiting for transfers between devices, spread(): lax.all_to_all(array, axis, split_axis=0, concat_axis=0, tiled=True, axis...  8.27 us
    all_gather x1, blocking collectives, total_over_devices(): lax.all_gather(part, 'key', axis=0, tiled=True, axis_index_groups=chip)  6.49 us
    all_gather x1, blocking collectives, on_device(): lax.all_gather(dim_features, 'fact', axis=0, tiled=True, axis_index_group...  5.98 us
    pallas_call x3, Pallas kernels, kernel_call(): pl.pallas_call(body, out_shape=tuple((jax.ShapeDtypeStruct(shape, dtype)...  3.26 us
    ppermute x1, starting transfers between devices, total_over_devices(): part = kept + lax.ppermute(given, 'key', swap)  2.61 us
  transfers between devices with their start and end apart: 3, of which 3 were waited for; matrix products, arithmetic and copies ran while one was open for 0% of the time, Pallas kernels for 1%

profile of v9, /device:TPU:1, one launch (start us, length us, event | category | flops | bytes accessed | tf_op | source)
XLA Modules:
  0.0 121.5 jit_solution(9381738906824461073)
XLA Ops:
  0.6 2.0 %shard_map.86.packed_ref = bf16[8,136,384]{2,1,0:T(8,128)(2,1)} custom-call(s32[8,128]{1,0:T(8,128)} %bitcast.11, s32[1,8]{1,0:T(1,128)} %fill_hbm.1, bf16[8,128,256]{2,1,0:T(8,128)(2,1)} %bitcast.9, bf16[8,128,128]{2,1,0:T(8,128)(2,1)} %bitcast.10), custom_call_target="tpu_custom_call" | custom-call | tf_op jit(solution)/shard_map/pallas_call | solution.py:251
  2.7 0.0 copy-start
  2.7 0.0 copy-start.2
  2.7 14.1 %all-to-all-start = ((bf16[8,136,384]{2,1,0:T(8,128)(2,1)}), bf16[8,136,384]{2,1,0:T(8,128)(2,1)S(1)}, u32[]{:S(2)}, u32[]{:S(2)}) async-start(bf16[8,136,384]{2,1,0:T(8,128)(2,1)} %shard_map.86.packed_ref), calls=%async_computation | async-start | bytes 1671168 | tf_op jit(solution)/shard_map/all_to_all | solution.py:34
  16.8 0.0 copy-done
  16.8 0.0 copy-start.3
  16.8 0.8 shard_map.87.own_ref
  17.6 0.0 copy-done.3
  17.7 6.0 %all_gather.9.rows_ref = bf16[24,1024]{1,0:T(8,128)(2,1)S(1)} all-gather(bf16[8,1024]{1,0:T(8,128)(2,1)S(1)} %copy-done.3), channel_id=1, replica_groups={{0,64,128},{192,256,320},{384,448,512},{576,640,704},{8,72,136},{200,26..., dimensions={0}, use_global_device_ids=true | all-gather | bytes 65536 | tf_op jit(solution)/shard_map/all_gather | solution.py:271
  23.6 6.0 %all-to-all-done.packed_ref = bf16[8,136,384]{2,1,0:T(8,128)(2,1)S(1)} async-done(((bf16[8,136,384]{2,1,0:T(8,128)(2,1)}), bf16[8,136,384]{2,1,0:T(8,128)(2,1)S(1)}, u32[]{:S(2)}, u32[]{:S(2)}) %all-to-all-start) | async-done | bytes 835616 | tf_op jit(solution)/shard_map/all_to_all | solution.py:34
  29.6 1.8 %shard_map.88 = (bf16[8,104,384]{2,1,0:T(8,128)(2,1)}, bf16[24,1024]{1,0:T(8,128)(2,1)S(1)}, f32[256,128]{1,0:T(8,128)S(1)}) custom-call(bf16[8,136,384]{2,1,0:T(8,128)(2,1)S(1)} %all-to-all-done.packed_ref, bf16[24,1024]{1,0:T(8,128)(2,1)S(1)} %all_gather.9.rows_ref, f32[256,128]{1,0:T(8,128)S(1)} %shard_map.87.own_ref), custom_call_target="tpu_custom_call" | custom-call | tf_op jit(solution)/shard_map/pallas_call | solution.py:230
  31.5 3.7 %all-to-all-start.1 = ((bf16[8,104,384]{2,1,0:T(8,128)(2,1)}), bf16[8,104,384]{2,1,0:T(8,128)(2,1)S(1)}, u32[]{:S(2)}, u32[]{:S(2)}) async-start(bf16[8,104,384]{2,1,0:T(8,128)(2,1)} %get-tuple-element.9), calls=%async_computation.1 | async-start | bytes 1277952 | tf_op jit(solution)/shard_map/all_to_all | solution.py:34
  35.1 18.0 %all_gather.10.rows_ref = bf16[96,1024]{1,0:T(8,128)(2,1)S(1)} all-gather(bf16[24,1024]{1,0:T(8,128)(2,1)S(1)} %get-tuple-element.8), channel_id=1, replica_groups={{0,192,384,576},{64,256,448,640},{128,320,512,704},{8,200,392,584},{72,..., dimensions={0}, use_global_device_ids=true | all-gather | bytes 245760 | tf_op jit(solution)/shard_map/all_gather | solution.py:278
  53.2 2.3 %all-to-all-done.1.met_ref = bf16[8,104,384]{2,1,0:T(8,128)(2,1)S(1)} async-done(((bf16[8,104,384]{2,1,0:T(8,128)(2,1)}), bf16[8,104,384]{2,1,0:T(8,128)(2,1)S(1)}, u32[]{:S(2)}, u32[]{:S(2)}) %all-to-all-start.1) | async-done | bytes 639008 | tf_op jit(solution)/shard_map/all_to_all | solution.py:34
  55.5 0.0 copy-done.1
  55.5 0.6 shard_map.89
  56.1 2.6 %collective-permute-start = (f32[640,128]{1,0:T(8,128)S(1)}, f32[640,128]{1,0:T(8,128)S(1)}, u32[]{:S(2)}, u32[]{:S(2)}) collective-permute-start(f32[640,128]{1,0:T(8,128)S(1)} %get-tuple-element.11), channel_id=1, source_target_pairs={{0,1},{1,0},{2,3},{3,2},{4,5},{5,4},{6,7},{7,6},{8,9},{9,8},{10,11... | collective-permute-start | bytes 983048 | tf_op jit(solution)/shard_map/ppermute | solution.py:48
  58.7 1.2 %collective-permute-done = f32[640,128]{1,0:T(8,128)S(1)} collective-permute-done((f32[640,128]{1,0:T(8,128)S(1)}, f32[640,128]{1,0:T(8,128)S(1)}, u32[]{:S(2)}, u32[]{:S(2)}) %collective-permute-start) | collective-permute-done | bytes 327712 | tf_op jit(solution)/shard_map/ppermute | solution.py:48
  60.0 21.2 %all_to_all.25 = f32[32,5,4,128]{3,2,1,0:T(4,128)S(1)} all-to-all(f32[32,5,4,128]{3,2,1,0:T(4,128)S(1)} %bitcast.7), channel_id=1, replica_groups={{0,2,4,6,8,10,12,14,16,18,20,22,24,26,28,30,32,34,36,38,40,42,44,46,48,..., dimensions={0} | all-to-all | bytes 655360 | tf_op jit(solution)/shard_map/all_to_all | solution.py:34
  81.2 0.1 reduce_sum.18
  81.3 17.4 %all_to_all.26 = f32[12,5,4,128]{3,2,1,0:T(4,128)S(1)} all-to-all(f32[12,5,4,128]{3,2,1,0:T(4,128)S(1)} %broadcast_in_dim.4), channel_id=1, replica_groups={{0,64,128,192,256,320,384,448,512,576,640,704},{8,72,136,200,264,328,39..., dimensions={0} | all-to-all | bytes 245760 | tf_op jit(solution)/shard_map/all_to_all | solution.py:34
  98.8 15.3 %all_to_all.27 = f32[32,5,4,128]{3,2,1,0:T(4,128)S(1)} all-to-all(f32[32,5,4,128]{3,2,1,0:T(4,128)S(1)} %broadcast_in_dim.5), channel_id=1, replica_groups={{0,2,4,6,8,10,12,14,16,18,20,22,24,26,28,30,32,34,36,38,40,42,44,46,48,..., dimensions={0} | all-to-all | bytes 655360 | tf_op jit(solution)/shard_map/all_to_all | solution.py:34
  114.1 6.5 %all_gather.11 = f32[320,4,128]{2,1,0:T(4,128)S(1)} all-gather(f32[160,4,128]{2,1,0:T(4,128)S(1)} %bitcast.8), channel_id=1, replica_groups={{0,1},{2,3},{4,5},{6,7},{8,9},{10,11},{12,13},{14,15},{16,17},{18,19},{..., dimensions={0}, use_global_device_ids=true | all-gather | bytes 983040 | tf_op jit(solution)/shard_map/all_gather | solution.py:52
  120.6 0.9 shard_map.90
  (6 shorter events, 0.1 us)
Async XLA Ops:
  2.7 14.1 %copy-start = (bf16[8,136,384]{2,1,0:T(8,128)(2,1)S(1)}, bf16[8,136,384]{2,1,0:T(8,128)(2,1)}, u32[]{:S(2)}) copy-start(bf16[8,136,384]{2,1,0:T(8,128)(2,1)} %shard_map.86.packed_ref) | copy-start | bytes 2506756
  2.7 14.1 %copy-start.2 = (bf16[256,128]{1,0:T(8,128)(2,1)S(1)}, bf16[256,128]{1,0:T(8,128)(2,1)}, u32[]{:S(2)}) copy-start(bf16[256,128]{1,0:T(8,128)(2,1)} %fact_weight_ref.1) | copy-start | bytes 196612
  2.7 26.9 %all-to-all-start = ((bf16[8,136,384]{2,1,0:T(8,128)(2,1)}), bf16[8,136,384]{2,1,0:T(8,128)(2,1)S(1)}, u32[]{:S(2)}, u32[]{:S(2)}) async-start(bf16[8,136,384]{2,1,0:T(8,128)(2,1)} %shard_map.86.packed_ref), calls=%async_computation | async-start | bytes 1671168 | tf_op jit(solution)/shard_map/all_to_all | solution.py:34
  16.8 0.8 copy-start.3
  31.5 24.0 %copy-start.1 = (bf16[1024,128]{1,0:T(8,128)(2,1)S(1)}, bf16[1024,128]{1,0:T(8,128)(2,1)}, u32[]{:S(2)}) copy-start(bf16[1024,128]{1,0:T(8,128)(2,1)} %dim_weight_ref.3) | copy-start | bytes 786436
  31.5 24.0 %all-to-all-start.1 = ((bf16[8,104,384]{2,1,0:T(8,128)(2,1)}), bf16[8,104,384]{2,1,0:T(8,128)(2,1)S(1)}, u32[]{:S(2)}, u32[]{:S(2)}) async-start(bf16[8,104,384]{2,1,0:T(8,128)(2,1)} %get-tuple-element.9), calls=%async_computation.1 | async-start | bytes 1277952 | tf_op jit(solution)/shard_map/all_to_all | solution.py:34
  56.1 3.9 %collective-permute-start = (f32[640,128]{1,0:T(8,128)S(1)}, f32[640,128]{1,0:T(8,128)S(1)}, u32[]{:S(2)}, u32[]{:S(2)}) collective-permute-start(f32[640,128]{1,0:T(8,128)S(1)} %get-tuple-element.11), channel_id=1, source_target_pairs={{0,1},{1,0},{2,3},{3,2},{4,5},{5,4},{6,7},{7,6},{8,9},{9,8},{10,11... | collective-permute-start | bytes 983048 | tf_op jit(solution)/shard_map/ppermute | solution.py:48

commit v10 on v8

--- a/solution.py
+++ b/solution.py
@@ -75,9 +75,10 @@
     fill_in = pltpu.make_async_copy(fill_hbm, fill_ref, done.at[len(groups), 1])
     keys_in.start()
     fill_in.start()
-    for g in groups:
-        for copy in copies(g)[:2]:
-            copy.start()
+    plan = [copies(g) for g in groups]
+    for features_in, targets_in, _ in plan:
+        features_in.start()
+        targets_in.start()
     keys_in.wait()
     fill_in.wait()
     keys = keys_ref[...]
@@ -91,13 +92,12 @@
         digits = jnp.concatenate([high, low, jnp.zeros_like(high)], axis=1).astype(f32)
         digits = jnp.broadcast_to(digits, (extra_rows, width + out_width))
         slots_ref[b, pl.ds(bucket_rows, extra_rows), :] = digits.astype(bf16)
-    for g in groups:
-        features_in, targets_in, out = copies(g)
+    for features_in, targets_in, out in plan:
         features_in.wait()
         targets_in.wait()
         out.start()
-    for g in groups:
-        copies(g)[2].wait()
+    for _, _, out in plan:
+        out.wait()
 
 
 def codes_of(packed_ref, b):
@@ -154,32 +154,51 @@
         out_ref[m, pl.ds(ring_keys, extra_rows), :] = digits.astype(bf16)
 
 
-def both_terms(packed_ref, weight_ref, rows_ref, met_ref, kept_ref, given_ref):
+def split(value):
+    high = value.astype(bf16)
+    return high, (value - high.astype(f32)).astype(bf16)
+
+
+contract = (((0,), (0,)), ((), ()))
+
+
+def own_term(packed_ref, weight_ref, term_ref, one_hot_ref):
+    buckets = packed_ref.shape[0]
+    bucket_rows = packed_ref.shape[1] - extra_rows
+    out_width = weight_ref.shape[1]
+    codes = jnp.concatenate([codes_of(packed_ref, b) for b in range(buckets)], axis=0)
+    codes = jnp.transpose(codes.astype(f32)).astype(i32)
+    places = lax.broadcasted_iota(i32, (bucket_rows, one_hot_ref.shape[1]), 1)
+    total = jnp.zeros((weight_ref.shape[0], 2 * out_width), f32)
+    for pair in pairs_of(packed_ref):
+        for b in pair:
+            one_hot = jnp.where(places == codes[:, b : b + 1], f32(1.0), f32(0.0))
+            one_hot_ref[pl.ds(b * bucket_rows, bucket_rows), :] = one_hot.astype(bf16)
+        features, value = partial_of(packed_ref, weight_ref, pair)
+        live = jnp.concatenate([codes[:, b : b + 1] for b in pair], axis=0) >= 0
+        value = jnp.concatenate(split(jnp.where(live, value, f32(0.0))), axis=1)
+        total += lax.dot_general(features, value, contract, preferred_element_type=f32)
+    term_ref[...] = total[:, :out_width] + total[:, out_width:]
+
+
+def both_terms(packed_ref, own_ref, one_hot_ref, rows_ref, met_ref, kept_ref, given_ref):
     members, _, two_widths = met_ref.shape
     out_width = two_widths // 2
     ring_keys = rows_ref.shape[0]
-    buckets = packed_ref.shape[0]
-    bucket_rows = packed_ref.shape[1] - extra_rows
-    width = weight_ref.shape[0]
-    contract = (((0,), (0,)), ((), ()))
+    slots = pl.ds(0, packed_ref.shape[1] - extra_rows)
+    width = own_ref.shape[0]
 
     own = pl.ds(0, ring_keys)
     values = jnp.concatenate(
         [met_ref[m, own, pl.ds(out_width, out_width)] for m in range(members)], axis=0
     )
-    codes = jnp.concatenate([codes_of(packed_ref, b) for b in range(buckets)], axis=0)
-    codes = jnp.transpose(codes.astype(f32)).astype(i32)
-    places = lax.broadcasted_iota(i32, (bucket_rows, members * ring_keys), 1)
-    fact_term = jnp.zeros((width, out_width), f32)
-    for pair in pairs_of(packed_ref):
-        one_hot = [
-            jnp.where(places == codes[:, b : b + 1], f32(1.0), f32(0.0)).astype(bf16) for b in pair
-        ]
-        features, value = partial_of(packed_ref, weight_ref, pair)
-        found = jnp.dot(jnp.concatenate(one_hot, axis=0), values, preferred_element_type=f32)
-        live = jnp.concatenate([codes[:, b : b + 1] for b in pair], axis=0) >= 0
-        residual = jnp.where(live, value + found, f32(0.0)).astype(bf16)
-        fact_term += lax.dot_general(features, residual, contract, preferred_element_type=f32)
+    found = jnp.dot(one_hot_ref[...], values, preferred_element_type=f32).astype(bf16)
+    features = jnp.concatenate(
+        [packed_ref[b, slots, pl.ds(0, width)] for b in range(packed_ref.shape[0])], axis=0
+    )
+    fact_term = lax.dot_general(features, found, contract, preferred_element_type=f32)
+    fact_term += own_ref[...]
+
     me = lax.rem(lax.axis_index("fact"), ring_size)
     sums = jnp.zeros((ring_keys, out_width), f32)
     digits = jnp.zeros((extra_rows, two_widths), f32)
@@ -190,11 +209,8 @@
     diagonal = diagonal_of(ring_keys, out_width)
     counts = jnp.sum(jnp.where(diagonal, counts, f32(0.0)), axis=1, keepdims=True)
     sums += counts * met_ref[me, own, pl.ds(out_width, out_width)].astype(f32)
-    high = sums.astype(bf16)
-    low = (sums - high.astype(f32)).astype(bf16)
-    dim_term = lax.dot_general(
-        rows_ref[...], jnp.concatenate([high, low], axis=1), contract, preferred_element_type=f32
-    )
+    sums = jnp.concatenate(split(sums), axis=1)
+    dim_term = lax.dot_general(rows_ref[...], sums, contract, preferred_element_type=f32)
     dim_term = dim_term[:, :out_width] + dim_term[:, out_width:]
     half = kept_ref.shape[0]
 
@@ -218,13 +234,13 @@
     ] * row_scale + ridge_weight * dim_weight_ref[...].astype(f32)
 
 
-def kernel_call(body, shapes, dtype, *operands):
+def kernel_call(body, outs, *operands):
     vmem = pl.BlockSpec(memory_space=pltpu.VMEM)
     return pl.pallas_call(
         body,
-        out_shape=tuple(jax.ShapeDtypeStruct(shape, dtype) for shape in shapes),
+        out_shape=tuple(jax.ShapeDtypeStruct(shape, dtype) for shape, dtype in outs),
         in_specs=[vmem] * len(operands),
-        out_specs=(vmem,) * len(shapes),
+        out_specs=(vmem,) * len(outs),
         compiler_params=pltpu.CompilerParams(vmem_limit_bytes=32 << 20),
     )(*operands)
 
@@ -263,18 +279,13 @@
     packed = spread(packed, "key")
     rows = lax.all_gather(dim_features, "fact", axis=0, tiled=True, axis_index_groups=one_y)
 
-    (met,) = kernel_call(
-        sum_by_key,
-        ((ring_size, ring_keys + extra_rows, 2 * out_width),),
-        bf16,
-        packed,
-        fact_weight,
-        rows,
-        dim_weight,
-    )
+    block = (ring_size, ring_keys + extra_rows, 2 * out_width)
+    (met,) = kernel_call(sum_by_key, ((block, bf16),), packed, fact_weight, rows, dim_weight)
     met = spread(met, "fact", one_z)
-    half = ((fact_width + dim_width) // 2, out_width)
-    kept, given = kernel_call(both_terms, (half, half), f32, packed, fact_weight, rows, met)
+    outs = (((fact_width, out_width), f32), ((slot_count, ring_size * ring_keys), bf16))
+    own, one_hot = kernel_call(own_term, outs, packed, fact_weight)
+    half = (((fact_width + dim_width) // 2, out_width), f32)
+    kept, given = kernel_call(both_terms, (half, half), packed, own, one_hot, rows, met)
     totals = total_over_devices(kept, given, one_y, chip, plane)
     total_rows = slot_count * fact_devices * key_devices
     row_scale = float(total_rows) ** (-0.5)

time: 121 us -> 122 us (level)
  blocking collectives: 90.8 us -> 72.7 us
  waiting for transfers between devices: 1.24 us -> 11.6 us
  starting transfers between devices: 22 us -> 28.7 us
  Pallas kernels: 5.77 us -> 7.14 us
    all_to_all x4 -> x3, blocking collectives: 63.7 us -> 45.8 us  [spread(): lax.all_to_all(array, axis, split_axis=0, concat_axis=0, tiled=True, axis...]
    all_to_all x1 -> x2, waiting for transfers between devices: 0.01 us -> 10.4 us  [spread(): lax.all_to_all(array, axis, split_axis=0, concat_axis=0, tiled=True, axis...]
    all_to_all x1 -> x2, starting transfers between devices: 14.1 us -> 20.8 us  [spread(): lax.all_to_all(array, axis, split_axis=0, concat_axis=0, tiled=True, axis...]
    pallas_call x2 -> x3, Pallas kernels: 2.88 us -> 4.21 us  [kernel_call(): pl.pallas_call(body, out_shape=tuple((jax.ShapeDtypeStruct(shape, dtype)...]
  transfers between devices with their start and end apart: 2 -> 3, of which waited for: 1 -> 2; matrix products, arithmetic and copies ran while one was open for 0% -> 0% of each run, Pallas kernels for 0% -> 1%
where the time goes in v10:
time: 122 us; the launch traced here: 121 us
  blocking collectives  72.7 us (60%)
  starting transfers between devices  28.7 us (24%)
  waiting for transfers between devices  11.6 us (10%)
  Pallas kernels  7.14 us (6%)
    all_to_all x3, blocking collectives, spread(): lax.all_to_all(array, axis, split_axis=0, concat_axis=0, tiled=True, axis...  45.8 us
    all_to_all x2, starting transfers between devices, spread(): lax.all_to_all(array, axis, split_axis=0, concat_axis=0, tiled=True, axis...  20.8 us
    all_gather x1, blocking collectives, on_device(): lax.all_gather(dim_features, 'fact', axis=0, tiled=True, axis_index_group...  20.4 us
    all_to_all x2, waiting for transfers between devices, spread(): lax.all_to_all(array, axis, split_axis=0, concat_axis=0, tiled=True, axis...  10.4 us
    ppermute x1, starting transfers between devices, total_over_devices(): part = kept + lax.ppermute(given, 'key', swap)  7.9 us
    all_gather x1, blocking collectives, total_over_devices(): lax.all_gather(part, 'key', axis=0, tiled=True, axis_index_groups=chip)  6.49 us
    pallas_call x3, Pallas kernels, kernel_call(): pl.pallas_call(body, out_shape=tuple((jax.ShapeDtypeStruct(shape, dtype)...  4.21 us
  transfers between devices with their start and end apart: 3, of which 2 were waited for; matrix products, arithmetic and copies ran while one was open for 0% of the time, Pallas kernels for 1%

profile of v10, /device:TPU:1, one launch (start us, length us, event | category | flops | bytes accessed | tf_op | source)
XLA Modules:
  0.0 121.1 jit_solution(12592092545669926573)
XLA Ops:
  0.6 0.0 copy-start.2
  0.6 0.0 copy-start
  0.7 0.0 copy-start.1
  0.7 2.1 %shard_map.86 = bf16[8,136,384]{2,1,0:T(8,128)(2,1)} custom-call(s32[8,128]{1,0:T(8,128)} %bitcast.11, s32[1,8]{1,0:T(1,128)} %fill_hbm.1, bf16[8,128,256]{2,1,0:T(8,128)(2,1)} %bitcast.9, bf16[8,128,128]{2,1,0:T(8,128)(2,1)} %bitcast.10), custom_call_target="tpu_custom_call" | custom-call | tf_op jit(solution)/shard_map/pallas_call | solution.py:260
  2.7 14.0 %all-to-all-start = ((bf16[8,136,384]{2,1,0:T(8,128)(2,1)}), bf16[8,136,384]{2,1,0:T(8,128)(2,1)S(1)}, u32[]{:S(2)}, u32[]{:S(2)}) async-start(bf16[8,136,384]{2,1,0:T(8,128)(2,1)} %shard_map.86), calls=%async_computation | async-start | bytes 1671168 | tf_op jit(solution)/shard_map/all_to_all | solution.py:32
  16.7 0.0 copy-done.2
  16.7 20.4 %all_gather.6.rows_ref = bf16[96,1024]{1,0:T(8,128)(2,1)S(1)} all-gather(bf16[8,1024]{1,0:T(8,128)(2,1)S(1)} %copy-done.2), channel_id=1, replica_groups={{0,64,128,192,256,320,384,448,512,576,640,704},{8,72,136,200,264,328,39..., dimensions={0}, use_global_device_ids=true | all-gather | bytes 212992 | tf_op jit(solution)/shard_map/all_gather | solution.py:280
  37.1 0.0 all-to-all-done.packed_ref
  37.1 0.0 copy-done
  37.1 0.0 copy-done.1
  37.1 2.0 %shard_map.88 = bf16[8,104,256]{2,1,0:T(8,128)(2,1)} custom-call(bf16[8,136,384]{2,1,0:T(8,128)(2,1)S(1)} %all-to-all-done.packed_ref, bf16[256,128]{1,0:T(8,128)(2,1)S(1)} %copy-done.1, bf16[96,1024]{1,0:T(8,128)(2,1)S(1)} %all_gather.6.rows_ref, bf16[1024,128]{1,0:T(8,128)(2,1)S(1)} %copy-done), custom_call_target="tpu_custom_call" | custom-call | tf_op jit(solution)/shard_map/pallas_call | solution.py:239
  39.1 6.8 %all-to-all-start.1 = ((bf16[8,104,256]{2,1,0:T(8,128)(2,1)}), bf16[8,104,256]{2,1,0:T(8,128)(2,1)S(1)}, u32[]{:S(2)}, u32[]{:S(2)}) async-start(bf16[8,104,256]{2,1,0:T(8,128)(2,1)} %shard_map.88), calls=%async_computation.1 | async-start | bytes 851968 | tf_op jit(solution)/shard_map/all_to_all | solution.py:32
  45.9 0.9 shard_map.87
  46.8 10.4 %all-to-all-done.1.met_ref = bf16[8,104,256]{2,1,0:T(8,128)(2,1)S(1)} async-done(((bf16[8,104,256]{2,1,0:T(8,128)(2,1)}), bf16[8,104,256]{2,1,0:T(8,128)(2,1)S(1)}, u32[]{:S(2)}, u32[]{:S(2)}) %all-to-all-start.1) | async-done | bytes 426016 | tf_op jit(solution)/shard_map/all_to_all | solution.py:32
  57.2 1.3 %shard_map.89 = (f32[640,128]{1,0:T(8,128)S(1)}, f32[640,128]{1,0:T(8,128)S(1)}) custom-call(bf16[8,136,384]{2,1,0:T(8,128)(2,1)S(1)} %all-to-all-done.packed_ref, f32[256,128]{1,0:T(8,128)S(1)} %get-tuple-element.6.own_ref, bf16[1024,768]{1,0:T(8,128)(2,1)S(1)} %get-tuple-element.7.one_hot_ref, bf16[96,1024]{1,0:T(8,128)(2,1)S(1)} %all_gather.6.rows_ref, ...), custom_call_target="tpu_custom_call" | custom-call | tf_op jit(solution)/shard_map/pallas_call | solution.py:239
  58.5 7.9 %collective-permute-start = (f32[640,128]{1,0:T(8,128)S(1)}, f32[640,128]{1,0:T(8,128)S(1)}, u32[]{:S(2)}, u32[]{:S(2)}) collective-permute-start(f32[640,128]{1,0:T(8,128)S(1)} %get-tuple-element.9), channel_id=1, source_target_pairs={{0,1},{1,0},{2,3},{3,2},{4,5},{5,4},{6,7},{7,6},{8,9},{9,8},{10,11... | collective-permute-start | bytes 983048 | tf_op jit(solution)/shard_map/ppermute | solution.py:46
  66.4 1.2 %collective-permute-done = f32[640,128]{1,0:T(8,128)S(1)} collective-permute-done((f32[640,128]{1,0:T(8,128)S(1)}, f32[640,128]{1,0:T(8,128)S(1)}, u32[]{:S(2)}, u32[]{:S(2)}) %collective-permute-start) | collective-permute-done | bytes 327712 | tf_op jit(solution)/shard_map/ppermute | solution.py:46
  67.7 17.5 %all_to_all.25 = f32[32,5,4,128]{3,2,1,0:T(4,128)S(1)} all-to-all(f32[32,5,4,128]{3,2,1,0:T(4,128)S(1)} %bitcast.7), channel_id=1, replica_groups={{0,2,4,6,8,10,12,14,16,18,20,22,24,26,28,30,32,34,36,38,40,42,44,46,48,..., dimensions={0} | all-to-all | bytes 655360 | tf_op jit(solution)/shard_map/all_to_all | solution.py:32
  85.2 0.1 reduce_sum.18
  85.3 13.1 %all_to_all.26 = f32[12,5,4,128]{3,2,1,0:T(4,128)S(1)} all-to-all(f32[12,5,4,128]{3,2,1,0:T(4,128)S(1)} %broadcast_in_dim.4), channel_id=1, replica_groups={{0,64,128,192,256,320,384,448,512,576,640,704},{8,72,136,200,264,328,39..., dimensions={0} | all-to-all | bytes 245760 | tf_op jit(solution)/shard_map/all_to_all | solution.py:32
  98.4 15.3 %all_to_all.27 = f32[32,5,4,128]{3,2,1,0:T(4,128)S(1)} all-to-all(f32[32,5,4,128]{3,2,1,0:T(4,128)S(1)} %broadcast_in_dim.5), channel_id=1, replica_groups={{0,2,4,6,8,10,12,14,16,18,20,22,24,26,28,30,32,34,36,38,40,42,44,46,48,..., dimensions={0} | all-to-all | bytes 655360 | tf_op jit(solution)/shard_map/all_to_all | solution.py:32
  113.7 6.5 %all_gather.7 = f32[320,4,128]{2,1,0:T(4,128)S(1)} all-gather(f32[160,4,128]{2,1,0:T(4,128)S(1)} %bitcast.8), channel_id=1, replica_groups={{0,1},{2,3},{4,5},{6,7},{8,9},{10,11},{12,13},{14,15},{16,17},{18,19},{..., dimensions={0}, use_global_device_ids=true | all-gather | bytes 983040 | tf_op jit(solution)/shard_map/all_gather | solution.py:50
  120.2 0.9 shard_map.90
  (4 shorter events, 0.1 us)
Async XLA Ops:
  0.6 16.1 %copy-start.2 = (bf16[8,1024]{1,0:T(8,128)(2,1)S(1)}, bf16[8,1024]{1,0:T(8,128)(2,1)}, u32[]{:S(2)}) copy-start(bf16[8,1024]{1,0:T(8,128)(2,1)} %param.11) | copy-start | bytes 49156
  0.6 36.4 %copy-start = (bf16[1024,128]{1,0:T(8,128)(2,1)S(1)}, bf16[1024,128]{1,0:T(8,128)(2,1)}, u32[]{:S(2)}) copy-start(bf16[1024,128]{1,0:T(8,128)(2,1)} %dim_weight_ref.3) | copy-start | bytes 786436
  0.7 36.4 %copy-start.1 = (bf16[256,128]{1,0:T(8,128)(2,1)S(1)}, bf16[256,128]{1,0:T(8,128)(2,1)}, u32[]{:S(2)}) copy-start(bf16[256,128]{1,0:T(8,128)(2,1)} %fact_weight_ref.1) | copy-start | bytes 196612
  2.7 34.4 %all-to-all-start = ((bf16[8,136,384]{2,1,0:T(8,128)(2,1)}), bf16[8,136,384]{2,1,0:T(8,128)(2,1)S(1)}, u32[]{:S(2)}, u32[]{:S(2)}) async-start(bf16[8,136,384]{2,1,0:T(8,128)(2,1)} %shard_map.86), calls=%async_computation | async-start | bytes 1671168 | tf_op jit(solution)/shard_map/all_to_all | solution.py:32
  39.1 18.1 %all-to-all-start.1 = ((bf16[8,104,256]{2,1,0:T(8,128)(2,1)}), bf16[8,104,256]{2,1,0:T(8,128)(2,1)S(1)}, u32[]{:S(2)}, u32[]{:S(2)}) async-start(bf16[8,104,256]{2,1,0:T(8,128)(2,1)} %shard_map.88), calls=%async_computation.1 | async-start | bytes 851968 | tf_op jit(solution)/shard_map/all_to_all | solution.py:32
  58.5 9.1 %collective-permute-start = (f32[640,128]{1,0:T(8,128)S(1)}, f32[640,128]{1,0:T(8,128)S(1)}, u32[]{:S(2)}, u32[]{:S(2)}) collective-permute-start(f32[640,128]{1,0:T(8,128)S(1)} %get-tuple-element.9), channel_id=1, source_target_pairs={{0,1},{1,0},{2,3},{3,2},{4,5},{5,4},{6,7},{7,6},{8,9},{9,8},{10,11... | collective-permute-start | bytes 983048 | tf_op jit(solution)/shard_map/ppermute | solution.py:46

commit v11 on v8

--- a/solution.py
+++ b/solution.py
@@ -21,7 +21,7 @@
     one_y = [[z * ring_size + y for z in levels] for y in range(ring_size)]
     chip = [[2 * x + core for core in cores] for x in chips]
     plane = [
-        [(z * ring_size + y) * key_devices + 2 * x + core for y in range(ring_size) for x in chips]
+        [(z * ring_size + y) * key_devices + 2 * x + core for x in chips for y in range(ring_size)]
         for z in levels
         for core in cores
     ]
@@ -75,9 +75,10 @@
     fill_in = pltpu.make_async_copy(fill_hbm, fill_ref, done.at[len(groups), 1])
     keys_in.start()
     fill_in.start()
-    for g in groups:
-        for copy in copies(g)[:2]:
-            copy.start()
+    plan = [copies(g) for g in groups]
+    for features_in, targets_in, _ in plan:
+        features_in.start()
+        targets_in.start()
     keys_in.wait()
     fill_in.wait()
     keys = keys_ref[...]
@@ -91,13 +92,12 @@
         digits = jnp.concatenate([high, low, jnp.zeros_like(high)], axis=1).astype(f32)
         digits = jnp.broadcast_to(digits, (extra_rows, width + out_width))
         slots_ref[b, pl.ds(bucket_rows, extra_rows), :] = digits.astype(bf16)
-    for g in groups:
-        features_in, targets_in, out = copies(g)
+    for features_in, targets_in, out in plan:
         features_in.wait()
         targets_in.wait()
         out.start()
-    for g in groups:
-        copies(g)[2].wait()
+    for _, _, out in plan:
+        out.wait()
 
 
 def codes_of(packed_ref, b):

time: 121 us -> 122 us (level)
  no operation moved by 1% of the time
where the time goes in v11:
time: 122 us; the launch traced here: 121 us
  blocking collectives  91.6 us (75%)
  starting transfers between devices  22 us (18%)
  Pallas kernels  5.77 us (5%)
  waiting for transfers between devices  1.24 us (1%)
    all_to_all x4, blocking collectives, spread(): lax.all_to_all(array, axis, split_axis=0, concat_axis=0, tiled=True, axis...  63.7 us
    all_gather x1, blocking collectives, on_device(): lax.all_gather(dim_features, 'fact', axis=0, tiled=True, axis_index_group...  20.6 us
    all_to_all x1, starting transfers between devices, spread(): lax.all_to_all(array, axis, split_axis=0, concat_axis=0, tiled=True, axis...  14.1 us
    ppermute x1, starting transfers between devices, total_over_devices(): part = kept + lax.ppermute(given, 'key', swap)  7.87 us
    all_gather x1, blocking collectives, total_over_devices(): lax.all_gather(part, 'key', axis=0, tiled=True, axis_index_groups=chip)  7.26 us
    pallas_call x2, Pallas kernels, kernel_call(): pl.pallas_call(body, out_shape=tuple((jax.ShapeDtypeStruct(shape, dtype)...  2.88 us
  transfers between devices with their start and end apart: 2, of which 1 were waited for; matrix products, arithmetic and copies ran while one was open for 0% of the time, Pallas kernels for 0%

profile of v11, /device:TPU:1, one launch (start us, length us, event | category | flops | bytes accessed | tf_op | source)
XLA Modules:
  0.0 121.5 jit_solution(4364677802225623439)
XLA Ops:
  0.6 2.0 %shard_map.86 = bf16[8,136,384]{2,1,0:T(8,128)(2,1)} custom-call(s32[8,128]{1,0:T(8,128)} %bitcast.11, s32[1,8]{1,0:T(1,128)} %fill_hbm.1, bf16[8,128,256]{2,1,0:T(8,128)(2,1)} %bitcast.9, bf16[8,128,128]{2,1,0:T(8,128)(2,1)} %bitcast.10), custom_call_target="tpu_custom_call" | custom-call | tf_op jit(solution)/shard_map/pallas_call | solution.py:244
  2.7 0.0 copy-start.2
  2.7 0.0 copy-start
  2.7 14.1 %all-to-all-start = ((bf16[8,136,384]{2,1,0:T(8,128)(2,1)}), bf16[8,136,384]{2,1,0:T(8,128)(2,1)S(1)}, u32[]{:S(2)}, u32[]{:S(2)}) async-start(bf16[8,136,384]{2,1,0:T(8,128)(2,1)} %shard_map.86), calls=%async_computation | async-start | bytes 1671168 | tf_op jit(solution)/shard_map/all_to_all | solution.py:32
  16.8 0.0 copy-done.2
  16.8 0.0 copy-start.1
  16.8 20.6 %all_gather.6.rows_ref = bf16[96,1024]{1,0:T(8,128)(2,1)S(1)} all-gather(bf16[8,1024]{1,0:T(8,128)(2,1)S(1)} %copy-done.2), channel_id=1, replica_groups={{0,64,128,192,256,320,384,448,512,576,640,704},{8,72,136,200,264,328,39..., dimensions={0}, use_global_device_ids=true | all-gather | bytes 212992 | tf_op jit(solution)/shard_map/all_gather | solution.py:264
  37.4 0.0 all-to-all-done.packed_ref
  37.4 0.0 copy-done
  37.4 0.0 copy-done.1
  37.4 1.2 %shard_map.87 = bf16[8,104,256]{2,1,0:T(8,128)(2,1)S(1)} custom-call(bf16[8,136,384]{2,1,0:T(8,128)(2,1)S(1)} %all-to-all-done.packed_ref, bf16[256,128]{1,0:T(8,128)(2,1)S(1)} %copy-done.1, bf16[96,1024]{1,0:T(8,128)(2,1)S(1)} %all_gather.6.rows_ref, bf16[1024,128]{1,0:T(8,128)(2,1)S(1)} %copy-done), custom_call_target="tpu_custom_call" | custom-call | tf_op jit(solution)/shard_map/pallas_call | solution.py:223
  38.7 17.8 %all_to_all.25.met_ref = bf16[8,104,256]{2,1,0:T(8,128)(2,1)S(1)} all-to-all(bf16[8,104,256]{2,1,0:T(8,128)(2,1)S(1)} %shard_map.87), channel_id=1, replica_groups={{0,8,16,24,32,40,48,56},{64,72,80,88,96,104,112,120},{128,136,144,152,1..., dimensions={0} | all-to-all | bytes 851968 | tf_op jit(solution)/shard_map/all_to_all | solution.py:32
  56.5 1.6 %shard_map.88 = (f32[640,128]{1,0:T(8,128)S(1)}, f32[640,128]{1,0:T(8,128)S(1)}) custom-call(bf16[8,136,384]{2,1,0:T(8,128)(2,1)S(1)} %all-to-all-done.packed_ref, bf16[256,128]{1,0:T(8,128)(2,1)S(1)} %copy-done.1, bf16[96,1024]{1,0:T(8,128)(2,1)S(1)} %all_gather.6.rows_ref, bf16[8,104,256]{2,1,0:T(8,128)(2,1)S(1)} %all_to_all.25.met_ref), custom_call_target="tpu_custom_call" | custom-call | tf_op jit(solution)/shard_map/pallas_call | solution.py:223
  58.1 7.9 %collective-permute-start = (f32[640,128]{1,0:T(8,128)S(1)}, f32[640,128]{1,0:T(8,128)S(1)}, u32[]{:S(2)}, u32[]{:S(2)}) collective-permute-start(f32[640,128]{1,0:T(8,128)S(1)} %get-tuple-element.5), channel_id=1, source_target_pairs={{0,1},{1,0},{2,3},{3,2},{4,5},{5,4},{6,7},{7,6},{8,9},{9,8},{10,11... | collective-permute-start | bytes 983048 | tf_op jit(solution)/shard_map/ppermute | solution.py:46
  66.0 1.2 %collective-permute-done = f32[640,128]{1,0:T(8,128)S(1)} collective-permute-done((f32[640,128]{1,0:T(8,128)S(1)}, f32[640,128]{1,0:T(8,128)S(1)}, u32[]{:S(2)}, u32[]{:S(2)}) %collective-permute-start) | collective-permute-done | bytes 327712 | tf_op jit(solution)/shard_map/ppermute | solution.py:46
  67.3 15.2 %all_to_all.26 = f32[32,5,4,128]{3,2,1,0:T(4,128)S(1)} all-to-all(f32[32,5,4,128]{3,2,1,0:T(4,128)S(1)} %bitcast.7), channel_id=1, replica_groups={{0,8,16,24,32,40,48,56,2,10,18,26,34,42,50,58,4,12,20,28,36,44,52,60,6,..., dimensions={0} | all-to-all | bytes 655360 | tf_op jit(solution)/shard_map/all_to_all | solution.py:32
  82.5 0.1 reduce_sum.18
  82.6 13.2 %all_to_all.27 = f32[12,5,4,128]{3,2,1,0:T(4,128)S(1)} all-to-all(f32[12,5,4,128]{3,2,1,0:T(4,128)S(1)} %broadcast_in_dim.4), channel_id=1, replica_groups={{0,64,128,192,256,320,384,448,512,576,640,704},{8,72,136,200,264,328,39..., dimensions={0} | all-to-all | bytes 245760 | tf_op jit(solution)/shard_map/all_to_all | solution.py:32
  95.8 17.5 %all_to_all.28 = f32[32,5,4,128]{3,2,1,0:T(4,128)S(1)} all-to-all(f32[32,5,4,128]{3,2,1,0:T(4,128)S(1)} %broadcast_in_dim.5), channel_id=1, replica_groups={{0,8,16,24,32,40,48,56,2,10,18,26,34,42,50,58,4,12,20,28,36,44,52,60,6,..., dimensions={0} | all-to-all | bytes 655360 | tf_op jit(solution)/shard_map/all_to_all | solution.py:32
  113.3 7.3 %all_gather.7 = f32[320,4,128]{2,1,0:T(4,128)S(1)} all-gather(f32[160,4,128]{2,1,0:T(4,128)S(1)} %bitcast.8), channel_id=1, replica_groups={{0,1},{2,3},{4,5},{6,7},{8,9},{10,11},{12,13},{14,15},{16,17},{18,19},{..., dimensions={0}, use_global_device_ids=true | all-gather | bytes 983040 | tf_op jit(solution)/shard_map/all_gather | solution.py:50
  120.6 0.9 shard_map.89
  (4 shorter events, 0.1 us)
Async XLA Ops:
  2.7 14.1 %copy-start.2 = (bf16[8,1024]{1,0:T(8,128)(2,1)S(1)}, bf16[8,1024]{1,0:T(8,128)(2,1)}, u32[]{:S(2)}) copy-start(bf16[8,1024]{1,0:T(8,128)(2,1)} %param.11) | copy-start | bytes 49156
  2.7 34.7 %copy-start = (bf16[1024,128]{1,0:T(8,128)(2,1)S(1)}, bf16[1024,128]{1,0:T(8,128)(2,1)}, u32[]{:S(2)}) copy-start(bf16[1024,128]{1,0:T(8,128)(2,1)} %dim_weight_ref.3) | copy-start | bytes 786436
  2.7 34.7 %all-to-all-start = ((bf16[8,136,384]{2,1,0:T(8,128)(2,1)}), bf16[8,136,384]{2,1,0:T(8,128)(2,1)S(1)}, u32[]{:S(2)}, u32[]{:S(2)}) async-start(bf16[8,136,384]{2,1,0:T(8,128)(2,1)} %shard_map.86), calls=%async_computation | async-start | bytes 1671168 | tf_op jit(solution)/shard_map/all_to_all | solution.py:32
  16.8 20.6 %copy-start.1 = (bf16[256,128]{1,0:T(8,128)(2,1)S(1)}, bf16[256,128]{1,0:T(8,128)(2,1)}, u32[]{:S(2)}) copy-start(bf16[256,128]{1,0:T(8,128)(2,1)} %fact_weight_ref.1) | copy-start | bytes 196612
  58.1 9.1 %collective-permute-start = (f32[640,128]{1,0:T(8,128)S(1)}, f32[640,128]{1,0:T(8,128)S(1)}, u32[]{:S(2)}, u32[]{:S(2)}) collective-permute-start(f32[640,128]{1,0:T(8,128)S(1)} %get-tuple-element.5), channel_id=1, source_target_pairs={{0,1},{1,0},{2,3},{3,2},{4,5},{5,4},{6,7},{7,6},{8,9},{9,8},{10,11... | collective-permute-start | bytes 983048 | tf_op jit(solution)/shard_map/ppermute | solution.py:46

commit v12 on v11

--- a/solution.py
+++ b/solution.py
@@ -46,7 +46,10 @@
     part = kept + lax.ppermute(given, "key", swap)
     part = spread(part.reshape(members, -1, 4, width), both, plane).sum(axis=0)
     part = collect(part, "fact", len(one_y[0]), one_y).sum(axis=0)
-    part = collect(part, both, members, plane).reshape(-1, 4, width)
+    rings = members // ring_size
+    back = [[line[x * ring_size + y] for y in range(ring_size) for x in range(rings)] for line in plane]
+    part = collect(part, both, members, back).reshape(ring_size, rings, *part.shape)
+    part = part.swapaxes(0, 1).reshape(-1, 4, width)
     part = lax.all_gather(part, "key", axis=0, tiled=True, axis_index_groups=chip)
     return part.reshape(2 * rows, width)
 

time: 122 us -> 122 us (level)
  no operation moved by 1% of the time
where the time goes in v12:
time: 122 us
  blocking collectives  91.4 us (75%)
  starting transfers between devices  22 us (18%)
  Pallas kernels  5.77 us (5%)
  waiting for transfers between devices  1.24 us (1%)
    all_to_all x4, blocking collectives, spread(): lax.all_to_all(array, axis, split_axis=0, concat_axis=0, tiled=True, axis...  64.4 us
    all_gather x1, blocking collectives, on_device(): lax.all_gather(dim_features, 'fact', axis=0, tiled=True, axis_index_group...  20.6 us
    all_to_all x1, starting transfers between devices, spread(): lax.all_to_all(array, axis, split_axis=0, concat_axis=0, tiled=True, axis...  14.1 us
    ppermute x1, starting transfers between devices, total_over_devices(): part = kept + lax.ppermute(given, 'key', swap)  7.87 us
    all_gather x1, blocking collectives, total_over_devices(): lax.all_gather(part, 'key', axis=0, tiled=True, axis_index_groups=chip)  6.47 us
    pallas_call x2, Pallas kernels, kernel_call(): pl.pallas_call(body, out_shape=tuple((jax.ShapeDtypeStruct(shape, dtype)...  2.88 us
  transfers between devices with their start and end apart: 2, of which 1 were waited for; matrix products, arithmetic and copies ran while one was open for 0% of the time, Pallas kernels for 0%

profile of v12, /device:TPU:1, one launch (start us, length us, event | category | flops | bytes accessed | tf_op | source)
XLA Modules:
  0.0 121.6 jit_solution(12259554024188218581)
XLA Ops:
  0.6 2.0 %shard_map.86 = bf16[8,136,384]{2,1,0:T(8,128)(2,1)} custom-call(s32[8,128]{1,0:T(8,128)} %bitcast.15, s32[1,8]{1,0:T(1,128)} %fill_hbm.1, bf16[8,128,256]{2,1,0:T(8,128)(2,1)} %bitcast.13, bf16[8,128,128]{2,1,0:T(8,128)(2,1)} %bitcast.14), custom_call_target="tpu_custom_call" | custom-call | tf_op jit(solution)/shard_map/pallas_call | solution.py:247
  2.7 0.0 copy-start.2
  2.7 0.0 copy-start
  2.7 14.1 %all-to-all-start = ((bf16[8,136,384]{2,1,0:T(8,128)(2,1)}), bf16[8,136,384]{2,1,0:T(8,128)(2,1)S(1)}, u32[]{:S(2)}, u32[]{:S(2)}) async-start(bf16[8,136,384]{2,1,0:T(8,128)(2,1)} %shard_map.86), calls=%async_computation | async-start | bytes 1671168 | tf_op jit(solution)/shard_map/all_to_all | solution.py:32
  16.8 0.0 copy-done.2
  16.8 0.0 copy-start.1
  16.8 20.6 %all_gather.6.rows_ref = bf16[96,1024]{1,0:T(8,128)(2,1)S(1)} all-gather(bf16[8,1024]{1,0:T(8,128)(2,1)S(1)} %copy-done.2), channel_id=1, replica_groups={{0,64,128,192,256,320,384,448,512,576,640,704},{8,72,136,200,264,328,39..., dimensions={0}, use_global_device_ids=true | all-gather | bytes 212992 | tf_op jit(solution)/shard_map/all_gather | solution.py:267
  37.4 0.0 all-to-all-done.packed_ref
  37.4 0.0 copy-done
  37.4 0.0 copy-done.1
  37.4 1.2 %shard_map.87 = bf16[8,104,256]{2,1,0:T(8,128)(2,1)S(1)} custom-call(bf16[8,136,384]{2,1,0:T(8,128)(2,1)S(1)} %all-to-all-done.packed_ref, bf16[256,128]{1,0:T(8,128)(2,1)S(1)} %copy-done.1, bf16[96,1024]{1,0:T(8,128)(2,1)S(1)} %all_gather.6.rows_ref, bf16[1024,128]{1,0:T(8,128)(2,1)S(1)} %copy-done), custom_call_target="tpu_custom_call" | custom-call | tf_op jit(solution)/shard_map/pallas_call | solution.py:226
  38.7 17.8 %all_to_all.25.met_ref = bf16[8,104,256]{2,1,0:T(8,128)(2,1)S(1)} all-to-all(bf16[8,104,256]{2,1,0:T(8,128)(2,1)S(1)} %shard_map.87), channel_id=1, replica_groups={{0,8,16,24,32,40,48,56},{64,72,80,88,96,104,112,120},{128,136,144,152,1..., dimensions={0} | all-to-all | bytes 851968 | tf_op jit(solution)/shard_map/all_to_all | solution.py:32
  56.5 1.6 %shard_map.88 = (f32[640,128]{1,0:T(8,128)S(1)}, f32[640,128]{1,0:T(8,128)S(1)}) custom-call(bf16[8,136,384]{2,1,0:T(8,128)(2,1)S(1)} %all-to-all-done.packed_ref, bf16[256,128]{1,0:T(8,128)(2,1)S(1)} %copy-done.1, bf16[96,1024]{1,0:T(8,128)(2,1)S(1)} %all_gather.6.rows_ref, bf16[8,104,256]{2,1,0:T(8,128)(2,1)S(1)} %all_to_all.25.met_ref), custom_call_target="tpu_custom_call" | custom-call | tf_op jit(solution)/shard_map/pallas_call | solution.py:226
  58.1 7.9 %collective-permute-start = (f32[640,128]{1,0:T(8,128)S(1)}, f32[640,128]{1,0:T(8,128)S(1)}, u32[]{:S(2)}, u32[]{:S(2)}) collective-permute-start(f32[640,128]{1,0:T(8,128)S(1)} %get-tuple-element.5), channel_id=1, source_target_pairs={{0,1},{1,0},{2,3},{3,2},{4,5},{5,4},{6,7},{7,6},{8,9},{9,8},{10,11... | collective-permute-start | bytes 983048 | tf_op jit(solution)/shard_map/ppermute | solution.py:46
  66.0 1.2 %collective-permute-done = f32[640,128]{1,0:T(8,128)S(1)} collective-permute-done((f32[640,128]{1,0:T(8,128)S(1)}, f32[640,128]{1,0:T(8,128)S(1)}, u32[]{:S(2)}, u32[]{:S(2)}) %collective-permute-start) | collective-permute-done | bytes 327712 | tf_op jit(solution)/shard_map/ppermute | solution.py:46
  67.3 15.2 %all_to_all.26 = f32[32,5,4,128]{3,2,1,0:T(4,128)S(1)} all-to-all(f32[32,5,4,128]{3,2,1,0:T(4,128)S(1)} %bitcast.11), channel_id=1, replica_groups={{0,8,16,24,32,40,48,56,2,10,18,26,34,42,50,58,4,12,20,28,36,44,52,60,6,..., dimensions={0} | all-to-all | bytes 655360 | tf_op jit(solution)/shard_map/all_to_all | solution.py:32
  82.5 0.1 reduce_sum.18
  82.6 13.2 %all_to_all.27 = f32[12,5,4,128]{3,2,1,0:T(4,128)S(1)} all-to-all(f32[12,5,4,128]{3,2,1,0:T(4,128)S(1)} %broadcast_in_dim.4), channel_id=1, replica_groups={{0,64,128,192,256,320,384,448,512,576,640,704},{8,72,136,200,264,328,39..., dimensions={0} | all-to-all | bytes 245760 | tf_op jit(solution)/shard_map/all_to_all | solution.py:32
  95.8 18.2 %all_to_all.28 = f32[32,5,4,128]{3,2,1,0:T(4,128)S(1)} all-to-all(f32[32,5,4,128]{3,2,1,0:T(4,128)S(1)} %broadcast_in_dim.5), channel_id=1, replica_groups={{0,2,4,6,8,10,12,14,16,18,20,22,24,26,28,30,32,34,36,38,40,42,44,46,48,..., dimensions={0} | all-to-all | bytes 655360 | tf_op jit(solution)/shard_map/all_to_all | solution.py:32
  114.0 0.2 copy.13
  114.3 6.5 %all_gather.7 = f32[320,4,128]{2,1,0:T(4,128)S(1)} all-gather(f32[160,4,128]{2,1,0:T(4,128)S(1)} %bitcast.12), channel_id=1, replica_groups={{0,1},{2,3},{4,5},{6,7},{8,9},{10,11},{12,13},{14,15},{16,17},{18,19},{..., dimensions={0}, use_global_device_ids=true | all-gather | bytes 983040 | tf_op jit(solution)/shard_map/all_gather | solution.py:53
  120.7 0.9 shard_map.89
  (5 shorter events, 0.2 us)
Async XLA Ops:
  2.7 14.1 %copy-start.2 = (bf16[8,1024]{1,0:T(8,128)(2,1)S(1)}, bf16[8,1024]{1,0:T(8,128)(2,1)}, u32[]{:S(2)}) copy-start(bf16[8,1024]{1,0:T(8,128)(2,1)} %param.11) | copy-start | bytes 49156
  2.7 34.7 %copy-start = (bf16[1024,128]{1,0:T(8,128)(2,1)S(1)}, bf16[1024,128]{1,0:T(8,128)(2,1)}, u32[]{:S(2)}) copy-start(bf16[1024,128]{1,0:T(8,128)(2,1)} %dim_weight_ref.3) | copy-start | bytes 786436
  2.7 34.7 %all-to-all-start = ((bf16[8,136,384]{2,1,0:T(8,128)(2,1)}), bf16[8,136,384]{2,1,0:T(8,128)(2,1)S(1)}, u32[]{:S(2)}, u32[]{:S(2)}) async-start(bf16[8,136,384]{2,1,0:T(8,128)(2,1)} %shard_map.86), calls=%async_computation | async-start | bytes 1671168 | tf_op jit(solution)/shard_map/all_to_all | solution.py:32
  16.8 20.6 %copy-start.1 = (bf16[256,128]{1,0:T(8,128)(2,1)S(1)}, bf16[256,128]{1,0:T(8,128)(2,1)}, u32[]{:S(2)}) copy-start(bf16[256,128]{1,0:T(8,128)(2,1)} %fact_weight_ref.1) | copy-start | bytes 196612
  58.1 9.1 %collective-permute-start = (f32[640,128]{1,0:T(8,128)S(1)}, f32[640,128]{1,0:T(8,128)S(1)}, u32[]{:S(2)}, u32[]{:S(2)}) collective-permute-start(f32[640,128]{1,0:T(8,128)S(1)} %get-tuple-element.5), channel_id=1, source_target_pairs={{0,1},{1,0},{2,3},{3,2},{4,5},{5,4},{6,7},{7,6},{8,9},{9,8},{10,11... | collective-permute-start | bytes 983048 | tf_op jit(solution)/shard_map/ppermute | solution.py:46

commit v13 on v11

--- a/solution.py
+++ b/solution.py
@@ -11,7 +11,7 @@
 ring_size = 8
 digit = 64
 extra_rows = 8
-f32, bf16, i32 = jnp.float32, jnp.bfloat16, jnp.int32
+f32, bf16, i32, i16 = jnp.float32, jnp.bfloat16, jnp.int32, jnp.int16
 
 
 def groups_of(fact_devices, key_devices):
@@ -21,7 +21,7 @@
     one_y = [[z * ring_size + y for z in levels] for y in range(ring_size)]
     chip = [[2 * x + core for core in cores] for x in chips]
     plane = [
-        [(z * ring_size + y) * key_devices + 2 * x + core for x in chips for y in range(ring_size)]
+        [(z * ring_size + y) * key_devices + 2 * x + core for y in range(ring_size) for x in chips]
         for z in levels
         for core in cores
     ]
@@ -131,12 +131,15 @@
     out_width = two_widths // 2
     ring_keys = rows_ref.shape[0]
     two_rows = 2 * (packed_ref.shape[1] - extra_rows)
-    places = lax.broadcasted_iota(i32, (members * ring_keys, two_rows), 0)
+    places = lax.broadcasted_iota(i32, (members * ring_keys, two_rows), 0).astype(i16)
+    places = places.reshape(-1, 16, two_rows)
     ones = jnp.ones((two_rows, out_width), bf16)
     sums = jnp.zeros((members * ring_keys, two_widths), f32)
     for pair in pairs_of(packed_ref):
         codes = jnp.concatenate([codes_of(packed_ref, b) for b in pair], axis=1)
-        one_hot = jnp.where(places == codes, f32(1.0), f32(0.0)).astype(bf16)
+        codes = jnp.broadcast_to(codes, (16, two_rows)).astype(i16)
+        one_hot = jnp.where(places == codes[None], bf16(1.0), bf16(0.0))
+        one_hot = one_hot.reshape(members * ring_keys, two_rows)
         _, value = partial_of(packed_ref, weight_ref, pair)
         value = jnp.concatenate([value.astype(bf16), ones], axis=1)
         sums += jnp.dot(one_hot, value, preferred_element_type=f32)
@@ -169,12 +172,14 @@
     )
     codes = jnp.concatenate([codes_of(packed_ref, b) for b in range(buckets)], axis=0)
     codes = jnp.transpose(codes.astype(f32)).astype(i32)
-    places = lax.broadcasted_iota(i32, (bucket_rows, members * ring_keys), 1)
+    places = lax.broadcasted_iota(i32, (bucket_rows, members * ring_keys), 1).astype(i16)
     fact_term = jnp.zeros((width, out_width), f32)
     for pair in pairs_of(packed_ref):
-        one_hot = [
-            jnp.where(places == codes[:, b : b + 1], f32(1.0), f32(0.0)).astype(bf16) for b in pair
-        ]
+        one_hot = []
+        for b in pair:
+            code = jnp.broadcast_to(codes[:, b : b + 1], (bucket_rows, 128)).astype(i16)
+            code = jnp.concatenate([code] * (members * ring_keys // 128), axis=1)
+            one_hot.append(jnp.where(places == code, bf16(1.0), bf16(0.0)))
         features, value = partial_of(packed_ref, weight_ref, pair)
         found = jnp.dot(jnp.concatenate(one_hot, axis=0), values, preferred_element_type=f32)
         live = jnp.concatenate([codes[:, b : b + 1] for b in pair], axis=0) >= 0

time: 122 us -> 121 us (level)
  no operation moved by 1% of the time
where the time goes in v13:
time: 121 us
  blocking collectives  90.8 us (75%)
  starting transfers between devices  22 us (18%)
  Pallas kernels  5.77 us (5%)
  waiting for transfers between devices  1.24 us (1%)
    all_to_all x4, blocking collectives, spread(): lax.all_to_all(array, axis, split_axis=0, concat_axis=0, tiled=True, axis...  63.7 us
    all_gather x1, blocking collectives, on_device(): lax.all_gather(dim_features, 'fact', axis=0, tiled=True, axis_index_group...  20.6 us
    all_to_all x1, starting transfers between devices, spread(): lax.all_to_all(array, axis, split_axis=0, concat_axis=0, tiled=True, axis...  14.1 us
    ppermute x1, starting transfers between devices, total_over_devices(): part = kept + lax.ppermute(given, 'key', swap)  7.88 us
    all_gather x1, blocking collectives, total_over_devices(): lax.all_gather(part, 'key', axis=0, tiled=True, axis_index_groups=chip)  6.49 us
    pallas_call x2, Pallas kernels, kernel_call(): pl.pallas_call(body, out_shape=tuple((jax.ShapeDtypeStruct(shape, dtype)...  2.87 us
  transfers between devices with their start and end apart: 2, of which 1 were waited for; matrix products, arithmetic and copies ran while one was open for 0% of the time, Pallas kernels for 0%

profile of v13, /device:TPU:1, one launch (start us, length us, event | category | flops | bytes accessed | tf_op | source)
XLA Modules:
  0.0 120.7 jit_solution(10032716885407484443)
XLA Ops:
  0.6 2.0 %shard_map.86 = bf16[8,136,384]{2,1,0:T(8,128)(2,1)} custom-call(s32[8,128]{1,0:T(8,128)} %bitcast.11, s32[1,8]{1,0:T(1,128)} %fill_hbm.1, bf16[8,128,256]{2,1,0:T(8,128)(2,1)} %bitcast.9, bf16[8,128,128]{2,1,0:T(8,128)(2,1)} %bitcast.10), custom_call_target="tpu_custom_call" | custom-call | tf_op jit(solution)/shard_map/pallas_call | solution.py:249
  2.7 0.0 copy-start.2
  2.7 0.0 copy-start
  2.7 14.1 %all-to-all-start = ((bf16[8,136,384]{2,1,0:T(8,128)(2,1)}), bf16[8,136,384]{2,1,0:T(8,128)(2,1)S(1)}, u32[]{:S(2)}, u32[]{:S(2)}) async-start(bf16[8,136,384]{2,1,0:T(8,128)(2,1)} %shard_map.86), calls=%async_computation | async-start | bytes 1671168 | tf_op jit(solution)/shard_map/all_to_all | solution.py:32
  16.8 0.0 copy-done.2
  16.8 0.0 copy-start.1
  16.8 20.6 %all_gather.6.rows_ref = bf16[96,1024]{1,0:T(8,128)(2,1)S(1)} all-gather(bf16[8,1024]{1,0:T(8,128)(2,1)S(1)} %copy-done.2), channel_id=1, replica_groups={{0,64,128,192,256,320,384,448,512,576,640,704},{8,72,136,200,264,328,39..., dimensions={0}, use_global_device_ids=true | all-gather | bytes 212992 | tf_op jit(solution)/shard_map/all_gather | solution.py:269
  37.4 0.0 all-to-all-done.packed_ref
  37.4 0.0 copy-done
  37.4 0.0 copy-done.1
  37.4 1.2 %shard_map.87 = bf16[8,104,256]{2,1,0:T(8,128)(2,1)S(1)} custom-call(bf16[8,136,384]{2,1,0:T(8,128)(2,1)S(1)} %all-to-all-done.packed_ref, bf16[256,128]{1,0:T(8,128)(2,1)S(1)} %copy-done.1, bf16[96,1024]{1,0:T(8,128)(2,1)S(1)} %all_gather.6.rows_ref, bf16[1024,128]{1,0:T(8,128)(2,1)S(1)} %copy-done), custom_call_target="tpu_custom_call" | custom-call | tf_op jit(solution)/shard_map/pallas_call | solution.py:228
  38.7 17.8 %all_to_all.25.met_ref = bf16[8,104,256]{2,1,0:T(8,128)(2,1)S(1)} all-to-all(bf16[8,104,256]{2,1,0:T(8,128)(2,1)S(1)} %shard_map.87), channel_id=1, replica_groups={{0,8,16,24,32,40,48,56},{64,72,80,88,96,104,112,120},{128,136,144,152,1..., dimensions={0} | all-to-all | bytes 851968 | tf_op jit(solution)/shard_map/all_to_all | solution.py:32
  56.5 1.6 %shard_map.88 = (f32[640,128]{1,0:T(8,128)S(1)}, f32[640,128]{1,0:T(8,128)S(1)}) custom-call(bf16[8,136,384]{2,1,0:T(8,128)(2,1)S(1)} %all-to-all-done.packed_ref, bf16[256,128]{1,0:T(8,128)(2,1)S(1)} %copy-done.1, bf16[96,1024]{1,0:T(8,128)(2,1)S(1)} %all_gather.6.rows_ref, bf16[8,104,256]{2,1,0:T(8,128)(2,1)S(1)} %all_to_all.25.met_ref), custom_call_target="tpu_custom_call" | custom-call | tf_op jit(solution)/shard_map/pallas_call | solution.py:228
  58.1 7.9 %collective-permute-start = (f32[640,128]{1,0:T(8,128)S(1)}, f32[640,128]{1,0:T(8,128)S(1)}, u32[]{:S(2)}, u32[]{:S(2)}) collective-permute-start(f32[640,128]{1,0:T(8,128)S(1)} %get-tuple-element.5), channel_id=1, source_target_pairs={{0,1},{1,0},{2,3},{3,2},{4,5},{5,4},{6,7},{7,6},{8,9},{9,8},{10,11... | collective-permute-start | bytes 983048 | tf_op jit(solution)/shard_map/ppermute | solution.py:46
  66.0 1.2 %collective-permute-done = f32[640,128]{1,0:T(8,128)S(1)} collective-permute-done((f32[640,128]{1,0:T(8,128)S(1)}, f32[640,128]{1,0:T(8,128)S(1)}, u32[]{:S(2)}, u32[]{:S(2)}) %collective-permute-start) | collective-permute-done | bytes 327712 | tf_op jit(solution)/shard_map/ppermute | solution.py:46
  67.3 17.5 %all_to_all.26 = f32[32,5,4,128]{3,2,1,0:T(4,128)S(1)} all-to-all(f32[32,5,4,128]{3,2,1,0:T(4,128)S(1)} %bitcast.7), channel_id=1, replica_groups={{0,2,4,6,8,10,12,14,16,18,20,22,24,26,28,30,32,34,36,38,40,42,44,46,48,..., dimensions={0} | all-to-all | bytes 655360 | tf_op jit(solution)/shard_map/all_to_all | solution.py:32
  84.8 0.1 reduce_sum.18
  84.8 13.1 %all_to_all.27 = f32[12,5,4,128]{3,2,1,0:T(4,128)S(1)} all-to-all(f32[12,5,4,128]{3,2,1,0:T(4,128)S(1)} %broadcast_in_dim.4), channel_id=1, replica_groups={{0,64,128,192,256,320,384,448,512,576,640,704},{8,72,136,200,264,328,39..., dimensions={0} | all-to-all | bytes 245760 | tf_op jit(solution)/shard_map/all_to_all | solution.py:32
  98.0 15.3 %all_to_all.28 = f32[32,5,4,128]{3,2,1,0:T(4,128)S(1)} all-to-all(f32[32,5,4,128]{3,2,1,0:T(4,128)S(1)} %broadcast_in_dim.5), channel_id=1, replica_groups={{0,2,4,6,8,10,12,14,16,18,20,22,24,26,28,30,32,34,36,38,40,42,44,46,48,..., dimensions={0} | all-to-all | bytes 655360 | tf_op jit(solution)/shard_map/all_to_all | solution.py:32
  113.3 6.5 %all_gather.7 = f32[320,4,128]{2,1,0:T(4,128)S(1)} all-gather(f32[160,4,128]{2,1,0:T(4,128)S(1)} %bitcast.8), channel_id=1, replica_groups={{0,1},{2,3},{4,5},{6,7},{8,9},{10,11},{12,13},{14,15},{16,17},{18,19},{..., dimensions={0}, use_global_device_ids=true | all-gather | bytes 983040 | tf_op jit(solution)/shard_map/all_gather | solution.py:50
  119.8 0.9 shard_map.89
  (4 shorter events, 0.1 us)
Async XLA Ops:
  2.7 14.1 %copy-start.2 = (bf16[8,1024]{1,0:T(8,128)(2,1)S(1)}, bf16[8,1024]{1,0:T(8,128)(2,1)}, u32[]{:S(2)}) copy-start(bf16[8,1024]{1,0:T(8,128)(2,1)} %param.11) | copy-start | bytes 49156
  2.7 34.7 %copy-start = (bf16[1024,128]{1,0:T(8,128)(2,1)S(1)}, bf16[1024,128]{1,0:T(8,128)(2,1)}, u32[]{:S(2)}) copy-start(bf16[1024,128]{1,0:T(8,128)(2,1)} %dim_weight_ref.3) | copy-start | bytes 786436
  2.7 34.7 %all-to-all-start = ((bf16[8,136,384]{2,1,0:T(8,128)(2,1)}), bf16[8,136,384]{2,1,0:T(8,128)(2,1)S(1)}, u32[]{:S(2)}, u32[]{:S(2)}) async-start(bf16[8,136,384]{2,1,0:T(8,128)(2,1)} %shard_map.86), calls=%async_computation | async-start | bytes 1671168 | tf_op jit(solution)/shard_map/all_to_all | solution.py:32
  16.8 20.6 %copy-start.1 = (bf16[256,128]{1,0:T(8,128)(2,1)S(1)}, bf16[256,128]{1,0:T(8,128)(2,1)}, u32[]{:S(2)}) copy-start(bf16[256,128]{1,0:T(8,128)(2,1)} %fact_weight_ref.1) | copy-start | bytes 196612
  58.1 9.1 %collective-permute-start = (f32[640,128]{1,0:T(8,128)S(1)}, f32[640,128]{1,0:T(8,128)S(1)}, u32[]{:S(2)}, u32[]{:S(2)}) collective-permute-start(f32[640,128]{1,0:T(8,128)S(1)} %get-tuple-element.5), channel_id=1, source_target_pairs={{0,1},{1,0},{2,3},{3,2},{4,5},{5,4},{6,7},{7,6},{8,9},{9,8},{10,11... | collective-permute-start | bytes 983048 | tf_op jit(solution)/shard_map/ppermute | solution.py:46

commit v14 on v9

--- a/solution.py
+++ b/solution.py
@@ -19,8 +19,8 @@
     chips, cores = range(key_devices // 2), range(2)
     one_z = [[z * ring_size + y for y in range(ring_size)] for z in levels]
     one_y = [[z * ring_size + y for z in levels] for y in range(ring_size)]
-    near = [line[i : i + 3] for line in one_y for i in range(0, len(line), 3)]
-    far = [line[i::3] for line in one_y for i in range(3)]
+    near = [line[i : i + 4] for line in one_y for i in range(0, len(line), 4)]
+    far = [line[i::4] for line in one_y for i in range(4)]
     chip = [[2 * x + core for core in cores] for x in chips]
     plane = [
         [(z * ring_size + y) * key_devices + 2 * x + core for y in range(ring_size) for x in chips]
@@ -149,7 +149,7 @@
     out_ref[...] = total[:, :out_width] + total[:, out_width:]
 
 
-def sum_by_key(packed_ref, rows_ref, own_ref, out_ref, rows_out_ref, own_out_ref):
+def sum_by_key(packed_ref, rows_ref, out_ref, rows_out_ref):
     members, _, width = out_ref.shape
     ring_keys = out_ref.shape[1] - extra_rows
     bucket_rows = packed_ref.shape[1] - extra_rows
@@ -175,7 +175,6 @@
             digits, (extra_rows, width)
         ).astype(bf16)
     rows_out_ref[...] = rows_ref[...]
-    own_out_ref[...] = own_ref[...]
 
 
 def both_terms(own_ref, weight_ref, rows_ref, dim_weight_ref, met_ref, kept_ref, given_ref):
@@ -272,8 +271,7 @@
     (own,) = kernel_call(own_term, (((fact_width, out_width), f32),), packed, fact_weight)
 
     block = (ring_size, ring_keys + extra_rows, fact_width + out_width)
-    outs = ((block, bf16), (rows.shape, bf16), (own.shape, f32))
-    met, rows, own = kernel_call(sum_by_key, outs, slots, rows, own)
+    met, rows = kernel_call(sum_by_key, ((block, bf16), (rows.shape, bf16)), slots, rows)
     met = spread(met, "fact", one_z)
     rows = lax.all_gather(rows, "fact", axis=0, tiled=True, axis_index_groups=far)
     half = (((fact_width + dim_width) // 2, out_width), f32)

time: 122 us -> 123 us (level)
  blocking collectives: 84.4 us -> 89.8 us
  waiting for transfers between devices: 9.5 us -> 5.17 us
    all_gather x1, blocking collectives: 5.98 us -> 10.8 us  [on_device(): lax.all_gather(dim_features, 'fact', axis=0, tiled=True, axis_index_group...]
    all_to_all x2, waiting for transfers between devices: 8.27 us -> 3.93 us  [spread(): lax.all_to_all(array, axis, split_axis=0, concat_axis=0, tiled=True, axis...]
where the time goes in v14:
time: 123 us; the launch traced here: 122 us
  blocking collectives  89.8 us (73%)
  starting transfers between devices  20.2 us (16%)
  Pallas kernels  6.18 us (5%)
  waiting for transfers between devices  5.17 us (4%)
    all_to_all x3, blocking collectives, spread(): lax.all_to_all(array, axis, split_axis=0, concat_axis=0, tiled=True, axis...  54.9 us
    all_to_all x2, starting transfers between devices, spread(): lax.all_to_all(array, axis, split_axis=0, concat_axis=0, tiled=True, axis...  17.6 us
    all_gather x1, blocking collectives, on_device(): lax.all_gather(rows, 'fact', axis=0, tiled=True, axis_index_groups=far)  17.5 us
    all_gather x1, blocking collectives, on_device(): lax.all_gather(dim_features, 'fact', axis=0, tiled=True, axis_index_group...  10.8 us
    all_gather x1, blocking collectives, total_over_devices(): lax.all_gather(part, 'key', axis=0, tiled=True, axis_index_groups=chip)  6.49 us
    all_to_all x2, waiting for transfers between devices, spread(): lax.all_to_all(array, axis, split_axis=0, concat_axis=0, tiled=True, axis...  3.93 us
    pallas_call x3, Pallas kernels, kernel_call(): pl.pallas_call(body, out_shape=tuple((jax.ShapeDtypeStruct(shape, dtype)...  3.28 us
    ppermute x1, starting transfers between devices, total_over_devices(): part = kept + lax.ppermute(given, 'key', swap)  2.54 us
  transfers between devices with their start and end apart: 3, of which 3 were waited for; matrix products, arithmetic and copies ran while one was open for 0% of the time, Pallas kernels for 1%

profile of v14, /device:TPU:1, one launch (start us, length us, event | category | flops | bytes accessed | tf_op | source)
XLA Modules:
  0.0 122.2 jit_solution(7709838192808405201)
XLA Ops:
  0.6 2.0 %shard_map.86.packed_ref = bf16[8,136,384]{2,1,0:T(8,128)(2,1)} custom-call(s32[8,128]{1,0:T(8,128)} %bitcast.11, s32[1,8]{1,0:T(1,128)} %fill_hbm.1, bf16[8,128,256]{2,1,0:T(8,128)(2,1)} %bitcast.9, bf16[8,128,128]{2,1,0:T(8,128)(2,1)} %bitcast.10), custom_call_target="tpu_custom_call" | custom-call | tf_op jit(solution)/shard_map/pallas_call | solution.py:250
  2.7 0.0 copy-start.3
  2.7 14.0 %all-to-all-start = ((bf16[8,136,384]{2,1,0:T(8,128)(2,1)}), bf16[8,136,384]{2,1,0:T(8,128)(2,1)S(1)}, u32[]{:S(2)}, u32[]{:S(2)}) async-start(bf16[8,136,384]{2,1,0:T(8,128)(2,1)} %shard_map.86.packed_ref), calls=%async_computation | async-start | bytes 1671168 | tf_op jit(solution)/shard_map/all_to_all | solution.py:34
  16.7 0.0 copy-done.3
  16.7 10.8 %all_gather.9.rows_ref = bf16[32,1024]{1,0:T(8,128)(2,1)S(1)} all-gather(bf16[8,1024]{1,0:T(8,128)(2,1)S(1)} %copy-done.3), channel_id=1, replica_groups={{0,64,128,192},{256,320,384,448},{512,576,640,704},{8,72,136,200},{264,..., dimensions={0}, use_global_device_ids=true | all-gather | bytes 81920 | tf_op jit(solution)/shard_map/all_gather | solution.py:270
  27.5 2.0 %all-to-all-done.packed_ref = bf16[8,136,384]{2,1,0:T(8,128)(2,1)S(1)} async-done(((bf16[8,136,384]{2,1,0:T(8,128)(2,1)}), bf16[8,136,384]{2,1,0:T(8,128)(2,1)S(1)}, u32[]{:S(2)}, u32[]{:S(2)}) %all-to-all-start) | async-done | bytes 835616 | tf_op jit(solution)/shard_map/all_to_all | solution.py:34
  29.5 1.9 %shard_map.88 = (bf16[8,104,384]{2,1,0:T(8,128)(2,1)}, bf16[32,1024]{1,0:T(8,128)(2,1)S(1)}) custom-call(bf16[8,136,384]{2,1,0:T(8,128)(2,1)S(1)} %all-to-all-done.packed_ref, bf16[32,1024]{1,0:T(8,128)(2,1)S(1)} %all_gather.9.rows_ref), custom_call_target="tpu_custom_call" | custom-call | tf_op jit(solution)/shard_map/pallas_call | solution.py:229
  31.3 3.7 %all-to-all-start.1 = ((bf16[8,104,384]{2,1,0:T(8,128)(2,1)}), bf16[8,104,384]{2,1,0:T(8,128)(2,1)S(1)}, u32[]{:S(2)}, u32[]{:S(2)}) async-start(bf16[8,104,384]{2,1,0:T(8,128)(2,1)} %get-tuple-element.7), calls=%async_computation.1 | async-start | bytes 1277952 | tf_op jit(solution)/shard_map/all_to_all | solution.py:34
  35.0 0.0 copy-done
  35.0 0.0 copy-done.2
  35.0 0.8 shard_map.87.own_ref
  35.9 0.0 copy-start.1
  35.9 17.5 %all_gather.10.rows_ref = bf16[96,1024]{1,0:T(8,128)(2,1)S(1)} all-gather(bf16[32,1024]{1,0:T(8,128)(2,1)S(1)} %get-tuple-element.6), channel_id=1, replica_groups={{0,256,512},{64,320,576},{128,384,640},{192,448,704},{8,264,520},{72,32..., dimensions={0}, use_global_device_ids=true | all-gather | bytes 262144 | tf_op jit(solution)/shard_map/all_gather | solution.py:276
  53.4 1.9 %all-to-all-done.1.met_ref = bf16[8,104,384]{2,1,0:T(8,128)(2,1)S(1)} async-done(((bf16[8,104,384]{2,1,0:T(8,128)(2,1)}), bf16[8,104,384]{2,1,0:T(8,128)(2,1)S(1)}, u32[]{:S(2)}, u32[]{:S(2)}) %all-to-all-start.1) | async-done | bytes 639008 | tf_op jit(solution)/shard_map/all_to_all | solution.py:34
  55.4 0.0 copy-done.1
  55.4 0.6 shard_map.89
  56.0 2.5 %collective-permute-start = (f32[640,128]{1,0:T(8,128)S(1)}, f32[640,128]{1,0:T(8,128)S(1)}, u32[]{:S(2)}, u32[]{:S(2)}) collective-permute-start(f32[640,128]{1,0:T(8,128)S(1)} %get-tuple-element.9), channel_id=1, source_target_pairs={{0,1},{1,0},{2,3},{3,2},{4,5},{5,4},{6,7},{7,6},{8,9},{9,8},{10,11... | collective-permute-start | bytes 983048 | tf_op jit(solution)/shard_map/ppermute | solution.py:48
  58.5 1.2 %collective-permute-done = f32[640,128]{1,0:T(8,128)S(1)} collective-permute-done((f32[640,128]{1,0:T(8,128)S(1)}, f32[640,128]{1,0:T(8,128)S(1)}, u32[]{:S(2)}, u32[]{:S(2)}) %collective-permute-start) | collective-permute-done | bytes 327712 | tf_op jit(solution)/shard_map/ppermute | solution.py:48
  59.8 22.9 %all_to_all.25 = f32[32,5,4,128]{3,2,1,0:T(4,128)S(1)} all-to-all(f32[32,5,4,128]{3,2,1,0:T(4,128)S(1)} %bitcast.7), channel_id=1, replica_groups={{0,2,4,6,8,10,12,14,16,18,20,22,24,26,28,30,32,34,36,38,40,42,44,46,48,..., dimensions={0} | all-to-all | bytes 655360 | tf_op jit(solution)/shard_map/all_to_all | solution.py:34
  82.7 0.1 reduce_sum.18
  82.8 16.7 %all_to_all.26 = f32[12,5,4,128]{3,2,1,0:T(4,128)S(1)} all-to-all(f32[12,5,4,128]{3,2,1,0:T(4,128)S(1)} %broadcast_in_dim.4), channel_id=1, replica_groups={{0,64,128,192,256,320,384,448,512,576,640,704},{8,72,136,200,264,328,39..., dimensions={0} | all-to-all | bytes 245760 | tf_op jit(solution)/shard_map/all_to_all | solution.py:34
  99.6 15.3 %all_to_all.27 = f32[32,5,4,128]{3,2,1,0:T(4,128)S(1)} all-to-all(f32[32,5,4,128]{3,2,1,0:T(4,128)S(1)} %broadcast_in_dim.5), channel_id=1, replica_groups={{0,2,4,6,8,10,12,14,16,18,20,22,24,26,28,30,32,34,36,38,40,42,44,46,48,..., dimensions={0} | all-to-all | bytes 655360 | tf_op jit(solution)/shard_map/all_to_all | solution.py:34
  114.9 6.5 %all_gather.11 = f32[320,4,128]{2,1,0:T(4,128)S(1)} all-gather(f32[160,4,128]{2,1,0:T(4,128)S(1)} %bitcast.8), channel_id=1, replica_groups={{0,1},{2,3},{4,5},{6,7},{8,9},{10,11},{12,13},{14,15},{16,17},{18,19},{..., dimensions={0}, use_global_device_ids=true | all-gather | bytes 983040 | tf_op jit(solution)/shard_map/all_gather | solution.py:52
  121.4 0.9 shard_map.90
  (6 shorter events, 0.1 us)
Async XLA Ops:
  2.7 14.0 %copy-start.3 = (bf16[8,1024]{1,0:T(8,128)(2,1)S(1)}, bf16[8,1024]{1,0:T(8,128)(2,1)}, u32[]{:S(2)}) copy-start(bf16[8,1024]{1,0:T(8,128)(2,1)} %param.11) | copy-start | bytes 49156
  2.7 26.8 %all-to-all-start = ((bf16[8,136,384]{2,1,0:T(8,128)(2,1)}), bf16[8,136,384]{2,1,0:T(8,128)(2,1)S(1)}, u32[]{:S(2)}, u32[]{:S(2)}) async-start(bf16[8,136,384]{2,1,0:T(8,128)(2,1)} %shard_map.86.packed_ref), calls=%async_computation | async-start | bytes 1671168 | tf_op jit(solution)/shard_map/all_to_all | solution.py:34
  31.3 3.7 %copy-start = (bf16[8,136,384]{2,1,0:T(8,128)(2,1)S(1)}, bf16[8,136,384]{2,1,0:T(8,128)(2,1)}, u32[]{:S(2)}) copy-start(bf16[8,136,384]{2,1,0:T(8,128)(2,1)} %shard_map.86.packed_ref) | copy-start | bytes 2506756
  31.3 3.7 %copy-start.2 = (bf16[256,128]{1,0:T(8,128)(2,1)S(1)}, bf16[256,128]{1,0:T(8,128)(2,1)}, u32[]{:S(2)}) copy-start(bf16[256,128]{1,0:T(8,128)(2,1)} %fact_weight_ref.1) | copy-start | bytes 196612
  31.3 24.0 %all-to-all-start.1 = ((bf16[8,104,384]{2,1,0:T(8,128)(2,1)}), bf16[8,104,384]{2,1,0:T(8,128)(2,1)S(1)}, u32[]{:S(2)}, u32[]{:S(2)}) async-start(bf16[8,104,384]{2,1,0:T(8,128)(2,1)} %get-tuple-element.7), calls=%async_computation.1 | async-start | bytes 1277952 | tf_op jit(solution)/shard_map/all_to_all | solution.py:34
  35.9 19.5 %copy-start.1 = (bf16[1024,128]{1,0:T(8,128)(2,1)S(1)}, bf16[1024,128]{1,0:T(8,128)(2,1)}, u32[]{:S(2)}) copy-start(bf16[1024,128]{1,0:T(8,128)(2,1)} %dim_weight_ref.3) | copy-start | bytes 786436
  56.0 3.8 %collective-permute-start = (f32[640,128]{1,0:T(8,128)S(1)}, f32[640,128]{1,0:T(8,128)S(1)}, u32[]{:S(2)}, u32[]{:S(2)}) collective-permute-start(f32[640,128]{1,0:T(8,128)S(1)} %get-tuple-element.9), channel_id=1, source_target_pairs={{0,1},{1,0},{2,3},{3,2},{4,5},{5,4},{6,7},{7,6},{8,9},{9,8},{10,11... | collective-permute-start | bytes 983048 | tf_op jit(solution)/shard_map/ppermute | solution.py:48

commit v15 on v8

--- a/solution.py
+++ b/solution.py
@@ -10,7 +10,7 @@
 ridge_weight = 4.0
 ring_size = 8
 digit = 64
-extra_rows = 8
+extra_rows = 16
 f32, bf16, i32 = jnp.float32, jnp.bfloat16, jnp.int32
 
 

time: 121 us -> 121 us (level)
  no operation moved by 1% of the time
where the time goes in v15:
time: 121 us
  blocking collectives  91 us (75%)
  starting transfers between devices  22.1 us (18%)
  Pallas kernels  5.77 us (5%)
  waiting for transfers between devices  1.24 us (1%)
    all_to_all x4, blocking collectives, spread(): lax.all_to_all(array, axis, split_axis=0, concat_axis=0, tiled=True, axis...  63.9 us
    all_gather x1, blocking collectives, on_device(): lax.all_gather(dim_features, 'fact', axis=0, tiled=True, axis_index_group...  20.6 us
    all_to_all x1, starting transfers between devices, spread(): lax.all_to_all(array, axis, split_axis=0, concat_axis=0, tiled=True, axis...  14.1 us
    ppermute x1, starting transfers between devices, total_over_devices(): part = kept + lax.ppermute(given, 'key', swap)  8.04 us
    all_gather x1, blocking collectives, total_over_devices(): lax.all_gather(part, 'key', axis=0, tiled=True, axis_index_groups=chip)  6.49 us
    pallas_call x2, Pallas kernels, kernel_call(): pl.pallas_call(body, out_shape=tuple((jax.ShapeDtypeStruct(shape, dtype)...  2.87 us
  transfers between devices with their start and end apart: 2, of which 1 were waited for; matrix products, arithmetic and copies ran while one was open for 0% of the time, Pallas kernels for 0%

profile of v15, /device:TPU:1, one launch (start us, length us, event | category | flops | bytes accessed | tf_op | source)
XLA Modules:
  0.0 121.0 jit_solution(8399420879102995124)
XLA Ops:
  0.6 2.0 %shard_map.86 = bf16[8,144,384]{2,1,0:T(8,128)(2,1)} custom-call(s32[8,128]{1,0:T(8,128)} %bitcast.11, s32[1,8]{1,0:T(1,128)} %fill_hbm.1, bf16[8,128,256]{2,1,0:T(8,128)(2,1)} %bitcast.9, bf16[8,128,128]{2,1,0:T(8,128)(2,1)} %bitcast.10), custom_call_target="tpu_custom_call" | custom-call | tf_op jit(solution)/shard_map/pallas_call | solution.py:244
  2.7 0.0 copy-start.2
  2.7 0.0 copy-start
  2.7 14.1 %all-to-all-start = ((bf16[8,144,384]{2,1,0:T(8,128)(2,1)}), bf16[8,144,384]{2,1,0:T(8,128)(2,1)S(1)}, u32[]{:S(2)}, u32[]{:S(2)}) async-start(bf16[8,144,384]{2,1,0:T(8,128)(2,1)} %shard_map.86), calls=%async_computation | async-start | bytes 1769472 | tf_op jit(solution)/shard_map/all_to_all | solution.py:32
  16.8 0.0 copy-done.2
  16.8 0.0 copy-start.1
  16.8 20.6 %all_gather.6.rows_ref = bf16[96,1024]{1,0:T(8,128)(2,1)S(1)} all-gather(bf16[8,1024]{1,0:T(8,128)(2,1)S(1)} %copy-done.2), channel_id=1, replica_groups={{0,64,128,192,256,320,384,448,512,576,640,704},{8,72,136,200,264,328,39..., dimensions={0}, use_global_device_ids=true | all-gather | bytes 212992 | tf_op jit(solution)/shard_map/all_gather | solution.py:264
  37.4 0.0 all-to-all-done.packed_ref
  37.4 0.0 copy-done
  37.4 0.0 copy-done.1
  37.4 1.2 %shard_map.87 = bf16[8,112,256]{2,1,0:T(8,128)(2,1)S(1)} custom-call(bf16[8,144,384]{2,1,0:T(8,128)(2,1)S(1)} %all-to-all-done.packed_ref, bf16[256,128]{1,0:T(8,128)(2,1)S(1)} %copy-done.1, bf16[96,1024]{1,0:T(8,128)(2,1)S(1)} %all_gather.6.rows_ref, bf16[1024,128]{1,0:T(8,128)(2,1)S(1)} %copy-done), custom_call_target="tpu_custom_call" | custom-call | tf_op jit(solution)/shard_map/pallas_call | solution.py:223
  38.6 18.1 %all_to_all.25.met_ref = bf16[8,112,256]{2,1,0:T(8,128)(2,1)S(1)} all-to-all(bf16[8,112,256]{2,1,0:T(8,128)(2,1)S(1)} %shard_map.87), channel_id=1, replica_groups={{0,8,16,24,32,40,48,56},{64,72,80,88,96,104,112,120},{128,136,144,152,1..., dimensions={0} | all-to-all | bytes 917504 | tf_op jit(solution)/shard_map/all_to_all | solution.py:32
  56.7 1.6 %shard_map.88 = (f32[640,128]{1,0:T(8,128)S(1)}, f32[640,128]{1,0:T(8,128)S(1)}) custom-call(bf16[8,144,384]{2,1,0:T(8,128)(2,1)S(1)} %all-to-all-done.packed_ref, bf16[256,128]{1,0:T(8,128)(2,1)S(1)} %copy-done.1, bf16[96,1024]{1,0:T(8,128)(2,1)S(1)} %all_gather.6.rows_ref, bf16[8,112,256]{2,1,0:T(8,128)(2,1)S(1)} %all_to_all.25.met_ref), custom_call_target="tpu_custom_call" | custom-call | tf_op jit(solution)/shard_map/pallas_call | solution.py:223
  58.3 8.0 %collective-permute-start = (f32[640,128]{1,0:T(8,128)S(1)}, f32[640,128]{1,0:T(8,128)S(1)}, u32[]{:S(2)}, u32[]{:S(2)}) collective-permute-start(f32[640,128]{1,0:T(8,128)S(1)} %get-tuple-element.5), channel_id=1, source_target_pairs={{0,1},{1,0},{2,3},{3,2},{4,5},{5,4},{6,7},{7,6},{8,9},{9,8},{10,11... | collective-permute-start | bytes 983048 | tf_op jit(solution)/shard_map/ppermute | solution.py:46
  66.4 1.2 %collective-permute-done = f32[640,128]{1,0:T(8,128)S(1)} collective-permute-done((f32[640,128]{1,0:T(8,128)S(1)}, f32[640,128]{1,0:T(8,128)S(1)}, u32[]{:S(2)}, u32[]{:S(2)}) %collective-permute-start) | collective-permute-done | bytes 327712 | tf_op jit(solution)/shard_map/ppermute | solution.py:46
  67.6 17.5 %all_to_all.26 = f32[32,5,4,128]{3,2,1,0:T(4,128)S(1)} all-to-all(f32[32,5,4,128]{3,2,1,0:T(4,128)S(1)} %bitcast.7), channel_id=1, replica_groups={{0,2,4,6,8,10,12,14,16,18,20,22,24,26,28,30,32,34,36,38,40,42,44,46,48,..., dimensions={0} | all-to-all | bytes 655360 | tf_op jit(solution)/shard_map/all_to_all | solution.py:32
  85.1 0.1 reduce_sum.18
  85.2 13.1 %all_to_all.27 = f32[12,5,4,128]{3,2,1,0:T(4,128)S(1)} all-to-all(f32[12,5,4,128]{3,2,1,0:T(4,128)S(1)} %broadcast_in_dim.4), channel_id=1, replica_groups={{0,64,128,192,256,320,384,448,512,576,640,704},{8,72,136,200,264,328,39..., dimensions={0} | all-to-all | bytes 245760 | tf_op jit(solution)/shard_map/all_to_all | solution.py:32
  98.4 15.3 %all_to_all.28 = f32[32,5,4,128]{3,2,1,0:T(4,128)S(1)} all-to-all(f32[32,5,4,128]{3,2,1,0:T(4,128)S(1)} %broadcast_in_dim.5), channel_id=1, replica_groups={{0,2,4,6,8,10,12,14,16,18,20,22,24,26,28,30,32,34,36,38,40,42,44,46,48,..., dimensions={0} | all-to-all | bytes 655360 | tf_op jit(solution)/shard_map/all_to_all | solution.py:32
  113.7 6.5 %all_gather.7 = f32[320,4,128]{2,1,0:T(4,128)S(1)} all-gather(f32[160,4,128]{2,1,0:T(4,128)S(1)} %bitcast.8), channel_id=1, replica_groups={{0,1},{2,3},{4,5},{6,7},{8,9},{10,11},{12,13},{14,15},{16,17},{18,19},{..., dimensions={0}, use_global_device_ids=true | all-gather | bytes 983040 | tf_op jit(solution)/shard_map/all_gather | solution.py:50
  120.2 0.9 shard_map.89
  (4 shorter events, 0.1 us)
Async XLA Ops:
  2.7 14.1 %copy-start.2 = (bf16[8,1024]{1,0:T(8,128)(2,1)S(1)}, bf16[8,1024]{1,0:T(8,128)(2,1)}, u32[]{:S(2)}) copy-start(bf16[8,1024]{1,0:T(8,128)(2,1)} %param.11) | copy-start | bytes 49156
  2.7 34.7 %copy-start = (bf16[1024,128]{1,0:T(8,128)(2,1)S(1)}, bf16[1024,128]{1,0:T(8,128)(2,1)}, u32[]{:S(2)}) copy-start(bf16[1024,128]{1,0:T(8,128)(2,1)} %dim_weight_ref.3) | copy-start | bytes 786436
  2.7 34.7 %all-to-all-start = ((bf16[8,144,384]{2,1,0:T(8,128)(2,1)}), bf16[8,144,384]{2,1,0:T(8,128)(2,1)S(1)}, u32[]{:S(2)}, u32[]{:S(2)}) async-start(bf16[8,144,384]{2,1,0:T(8,128)(2,1)} %shard_map.86), calls=%async_computation | async-start | bytes 1769472 | tf_op jit(solution)/shard_map/all_to_all | solution.py:32
  16.8 20.6 %copy-start.1 = (bf16[256,128]{1,0:T(8,128)(2,1)S(1)}, bf16[256,128]{1,0:T(8,128)(2,1)}, u32[]{:S(2)}) copy-start(bf16[256,128]{1,0:T(8,128)(2,1)} %fact_weight_ref.1) | copy-start | bytes 196612
  58.3 9.3 %collective-permute-start = (f32[640,128]{1,0:T(8,128)S(1)}, f32[640,128]{1,0:T(8,128)S(1)}, u32[]{:S(2)}, u32[]{:S(2)}) collective-permute-start(f32[640,128]{1,0:T(8,128)S(1)} %get-tuple-element.5), channel_id=1, source_target_pairs={{0,1},{1,0},{2,3},{3,2},{4,5},{5,4},{6,7},{7,6},{8,9},{9,8},{10,11... | collective-permute-start | bytes 983048 | tf_op jit(solution)/shard_map/ppermute | solution.py:46
